TPU v7x, 128 devices: a whole 4x4x4 slice. The times are simulated.
128 devices in a mesh: spec: 8 (over y, core), mass: 16 (over z, x).
Axes of the slice: x: 4, y: 4, z: 4, core: 2. Of those that a mesh axis runs over, the one named last changes fastest.
Arguments:
- spectra: bfloat16 [4096, 2048], P(('spec', 'mass')), may hold values from 0.001 to 10000, as said below
- routes: int32 [4096, 2], P(('spec', 'mass')), may hold values from 0 to 47, all different within a row; in each aligned block of 32 rows (0 to 31, 32 to 63, ...) at most 2 rows name the same one
- pep_bins: int32 [48, 32, 4096], P('mass', None, 'spec'), may hold values from 0 to 2047
- counts: int32 [48], replicated, may hold values from 2048 to 4096
Outputs:
- xcorr_best: float32 [4096, 2], P(('spec', 'mass'))
- xcorr_z: float32 [4096, 2], P(('spec', 'mass'))
Inputs may be any that keep to these rules, and one draw needn't show every extreme that they name: `routes`: among the rows of one device each window is named by at most 2 entries, and in some device by exactly 2. `spectra`: intensities are positive.
All inputs are finite; a program needn't handle non-finite values.
Results may differ from a plain program's by a relative error of at most 0.005.
Values may be sent and summed in bfloat16 or wider, within the bound.
No kernel may reach another device: no remote copies, remote signals or barrier semaphores. Data moves between devices by JAX's collectives and lax.ppermute only.
A program may use at most 64 MiB of HBM per device.

v0:
```python
import jax
import jax.numpy as jnp
from jax import lax
from jax.sharding import PartitionSpec as P

LAG = 75


EPS = 1e-06


def band_matrix(width, dtype):
    offset = jnp.abs(jnp.arange(width)[:, None] - jnp.arange(width)[None, :])
    return ((offset <= LAG) & (offset > 0)).astype(dtype)


def build_theory(bin_table, width):
    bin_ids = jnp.arange(width, dtype=jnp.int32)[:, None]
    theory = jnp.zeros((width, bin_table.shape[1]), jnp.bfloat16)
    for fragment in range(bin_table.shape[0]):
        theory = theory + (bin_ids == bin_table[fragment][None, :]).astype(jnp.bfloat16)
    return theory


def window_stats(rows_now, theory, valid, frags, capacity):
    scores = jnp.dot(rows_now, theory, preferred_element_type=jnp.float32) / frags
    highest = jnp.max(jnp.where(valid, scores, -1e30), axis=1).reshape(-1, capacity)
    summed = jnp.sum(jnp.where(valid, scores, 0.0), axis=1).reshape(-1, capacity)
    squared = jnp.sum(jnp.where(valid, scores * scores, 0.0), axis=1).reshape(-1, capacity)
    return (highest, summed, squared)


def per_device(spectra, routes, pep_bins, counts):
    spec_count = lax.axis_size("spec")
    mass_count = lax.axis_size("mass")
    width = spectra.shape[1]
    windows = counts.shape[0]
    steps = pep_bins.shape[0]
    frags = pep_bins.shape[1]
    pep_local = pep_bins.shape[2]
    spec_rows = routes.shape[0]
    picks = routes.shape[1]
    capacity = 3 * spec_rows * picks // (2 * windows)
    rooted = jnp.sqrt(spectra.astype(jnp.float32)).astype(jnp.bfloat16)
    background = jnp.dot(
        rooted, band_matrix(width, jnp.bfloat16), preferred_element_type=jnp.float32
    )
    prepared = (rooted.astype(jnp.float32) - background / (2.0 * LAG)).astype(jnp.bfloat16)
    flat_windows = routes.reshape(-1)
    onehot = (flat_windows[:, None] == jnp.arange(windows)[None, :]).astype(jnp.int32)
    earlier = jnp.cumsum(onehot, axis=0) - onehot
    slot_index = jnp.sum(earlier * onehot, axis=1)
    slot_flat = flat_windows * capacity + slot_index
    slot_table = (slot_flat[:, None] == jnp.arange(windows * capacity)[None, :]).astype(
        jnp.bfloat16
    )
    routing = jnp.sum(slot_table.reshape(spec_rows, picks, windows * capacity), axis=1)
    outgoing = lax.dot_general(
        routing, prepared, (((0,), (0,)), ((), ())), preferred_element_type=jnp.float32
    )
    outgoing = outgoing.astype(jnp.bfloat16).reshape(mass_count, steps, capacity, width)
    copies = jnp.broadcast_to(outgoing[None], (spec_count,) + outgoing.shape)
    copies = copies.reshape(spec_count * mass_count, steps, capacity, width)
    incoming = lax.all_to_all(copies, ("spec", "mass"), split_axis=0, concat_axis=0, tiled=True)
    pep_global = lax.axis_index("spec") * pep_local + jnp.arange(pep_local)
    high_list = []
    total_list = []
    square_list = []
    for window_step in range(steps):
        theory = build_theory(pep_bins[window_step], width)
        window_id = lax.axis_index("mass") * steps + window_step
        valid = (pep_global < counts[window_id])[None, :]
        rows_now = incoming[:, window_step].reshape(-1, width)
        highest_now, summed_now, squared_now = window_stats(
            rows_now, theory, valid, frags, capacity
        )
        high_list.append(highest_now)
        total_list.append(summed_now)
        square_list.append(squared_now)
    highest = jnp.stack(high_list, axis=1)
    summed = jnp.stack(total_list, axis=1)
    squared = jnp.stack(square_list, axis=1)
    returned = (
        lax.all_to_all(highest, ("spec", "mass"), split_axis=0, concat_axis=0, tiled=True),
        lax.all_to_all(summed, ("spec", "mass"), split_axis=0, concat_axis=0, tiled=True),
        lax.all_to_all(squared, ("spec", "mass"), split_axis=0, concat_axis=0, tiled=True),
    )
    shaped = [item.reshape(spec_count, mass_count, steps, capacity) for item in returned]
    high_win = jnp.max(shaped[0], axis=0).reshape(windows, capacity)
    total_win = jnp.sum(shaped[1], axis=0).reshape(windows, capacity)
    square_win = jnp.sum(shaped[2], axis=0).reshape(windows, capacity)
    peak = high_win[flat_windows, slot_index]
    live_count = counts[flat_windows].astype(jnp.float32)
    mean_score = total_win[flat_windows, slot_index] / live_count
    spread = square_win[flat_windows, slot_index] / live_count - mean_score * mean_score
    standard = (peak - mean_score) / jnp.sqrt(spread + EPS)
    return (peak.reshape(spec_rows, picks), standard.reshape(spec_rows, picks))


def solution(mesh):
    return jax.shard_map(
        per_device,
        mesh=mesh,
        in_specs=(
            P(("spec", "mass"), None),
            P(("spec", "mass"), None),
            P("mass", None, "spec"),
            P(),
        ),
        out_specs=(P(("spec", "mass"), None), P(("spec", "mass"), None)),
        check_vma=False,
    )
```

profile of v0, /device:TPU:1, one launch (start us, length us, event | category | flops | bytes accessed | tf_op | source)
XLA Modules:
  0.0 158.6 jit_solution(14123422853376896192)
XLA Ops:
  0.6 0.8 copy.58
  1.7 0.2 select_reduce_fusion.9
  2.0 0.7 multiply_add_fusion
  2.8 2.1 %convolution_convert_fusion = bf16[96,2048]{1,0:T(8,128)(2,1)S(1)} fusion(bf16[32,96]{1,0:T(8,128)(2,1)S(1)} %fusion.418, bf16[32,2048]{1,0:T(8,128)(2,1)} %param.4), kind=kOutput, calls=%fused_computation.203 | convolution fusion | flops 302710784 | bytes 530432 | tf_op jit(solution)/shard_map/dot_general | solution.py:58
  4.9 0.3 broadcast_in_dim.76
  5.2 3.9 %broadcast_in_dim.77 = bf16[8,16,3,2,2048]{4,3,2,1,0:T(2,128)(2,1)} broadcast(bf16[16,3,2,2048]{3,2,1,0:T(2,128)(2,1)S(1)} %broadcast_in_dim.76), dimensions={1,2,3,4} | broadcast | bytes 3538944 | tf_op jit(solution)/shard_map/broadcast_in_dim | solution.py:62
  9.1 11.5 %all-to-all-start = ((bf16[128,3,2,2048]{3,2,1,0:T(2,128)(2,1)}), bf16[128,3,2,2048]{3,2,1,0:T(2,128)(2,1)S(1)}, u32[]{:S(2)}, u32[]{:S(2)}) async-start(bf16[128,3,2,2048]{3,2,1,0:T(2,128)(2,1)} %bitcast.129), calls=%async_computation | async-start | bytes 6291456 | tf_op jit(solution)/shard_map/all_to_all | solution.py:64
  20.7 0.6 slice.589
  21.3 0.6 fusion.438
  21.9 1.2 fusion.421
  23.0 1.9 %fusion.419 = (pred[512]{0:T(512)(128)(4,1)}, pred[512]{0:T(512)(128)(4,1)}) fusion(s32[]{:T(128)} %bitcast.68, s32[]{:T(128)S(6)} %mul.31, s32[]{:T(128)} %bitcast.35), kind=kLoop, calls=%fused_computation.429 | loop fusion | flops 1536 | bytes 1036 | tf_op jit(solution)/shard_map/lt | solution.py:72
  24.9 0.5 fusion.431
  25.4 0.7 fusion.433
  26.1 0.7 fusion.434
  26.8 0.6 fusion.435
  27.4 0.6 fusion.436
  28.3 32.8 %all-to-all-done = bf16[128,3,2,2048]{3,2,1,0:T(2,128)(2,1)S(1)} async-done(((bf16[128,3,2,2048]{3,2,1,0:T(2,128)(2,1)}), bf16[128,3,2,2048]{3,2,1,0:T(2,128)(2,1)S(1)}, u32[]{:S(2)}, u32[]{:S(2)}) %all-to-all-start) | async-done | bytes 3145760 | tf_op jit(solution)/shard_map/all_to_all | solution.py:64
  61.1 3.7 %fusion.432 = (bf16[128,1,2,2048]{3,2,1,0:T(2,128)(2,1)}, bf16[128,1,2,2048]{3,2,1,0:T(2,128)(2,1)}, bf16[128,1,2,2048]{3,2,1,0:T(2,128)(2,1)}) fusion(bf16[128,3,2,2048]{3,2,1,0:T(2,128)(2,1)S(1)} %all-to-all-done), kind=kLoop, calls=%fused_computation.443 | loop fusion | bytes 6291456 | tf_op jit(solution)/shard_map/slice | solution.py:73
  64.8 1.5 reshape_squeeze.11
  66.7 14.6 %select_reduce_fusion.3 = (f32[256]{0:T(256)S(1)}, f32[256]{0:T(256)S(1)}, f32[256]{0:T(256)S(1)}) fusion(pred[512]{0:T(512)(128)(4,1)} %get-tuple-element.126, bf16[256,2048]{1,0:T(8,128)(2,1)S(1)} %reshape_squeeze.11, s32[512]{0:T(512)S(1)} %bitcast.165, s32[512]{0:T(512)} %bitcast.228, s32[512]{0:T(512)S(1)} %bitcast.198, s32[512]{0:T(512)S(1)} %bitcast.199, ...), kind=kOutput, calls=%fused_computation.406 | convolution fusion | flops 672136448 | bytes 1117696 | tf_op jit(solution)/shard_map/dot_general | solution.py:26
  81.3 0.1 stack_reshape.29
  81.5 0.4 reshape_squeeze.10
  82.1 14.7 %select_reduce_fusion.4 = (f32[256]{0:T(256)S(1)}, f32[256]{0:T(256)S(1)}, f32[256]{0:T(256)S(1)}) fusion(pred[512]{0:T(512)(128)(4,1)} %get-tuple-element.127, bf16[256,2048]{1,0:T(8,128)(2,1)S(1)} %reshape_squeeze.10, s32[512]{0:T(512)S(1)} %bitcast.166, s32[512]{0:T(512)S(1)} %bitcast.167, s32[512]{0:T(512)S(1)} %bitcast.168, s32[512]{0:T(512)S(1)} %bitcast.169, ...), kind=kOutput, calls=%fused_computation.407 | convolution fusion | flops 672136448 | bytes 1117696 | tf_op jit(solution)/shard_map/dot_general | solution.py:26
  96.8 0.1 stack_reshape.28
  96.9 0.4 reshape_squeeze.9
  97.4 14.1 %select_reduce_fusion.5 = (f32[256]{0:T(256)S(1)}, f32[256]{0:T(256)S(1)}, f32[256]{0:T(256)S(1)}) fusion(pred[512]{0:T(512)(128)(4,1)S(1)} %copy-done.44, bf16[256,2048]{1,0:T(8,128)(2,1)S(1)} %reshape_squeeze.9, s32[512]{0:T(512)S(1)} %bitcast.155, s32[512]{0:T(512)S(1)} %bitcast.156, s32[512]{0:T(512)S(1)} %bitcast.157, s32[512]{0:T(512)S(1)} %bitcast.158, ...), kind=kOutput, calls=%fused_computation.408 | convolution fusion | flops 672136448 | bytes 1117696 | tf_op jit(solution)/shard_map/dot_general | solution.py:26
  111.5 0.1 stack_reshape.27
  111.6 1.5 copy.60
  113.1 4.9 %all-to-all-start.1 = ((f32[128,3,2]{1,2,0:T(2,128)}), f32[128,3,2]{1,2,0:T(2,128)S(1)}, u32[]{:S(2)}, u32[]{:S(2)}) async-start(f32[128,3,2]{1,2,0:T(2,128)} %copy.60), calls=%async_computation.1 | async-start | bytes 262144 | tf_op jit(solution)/shard_map/all_to_all | solution.py:84
  118.0 0.1 stack_reshape.32
  118.2 0.1 stack_reshape.31
  118.3 0.1 stack_reshape.30
  118.5 1.5 copy.64
  120.0 0.1 stack_reshape.35
  120.1 0.1 stack_reshape.34
  120.3 0.1 stack_reshape.33
  120.4 7.8 %all-to-all-done.1 = f32[128,3,2]{1,2,0:T(2,128)S(1)} async-done(((f32[128,3,2]{1,2,0:T(2,128)}), f32[128,3,2]{1,2,0:T(2,128)S(1)}, u32[]{:S(2)}, u32[]{:S(2)}) %all-to-all-start.1) | async-done | bytes 3104 | tf_op jit(solution)/shard_map/all_to_all | solution.py:84
  128.2 4.0 %all-to-all-start.2 = ((f32[128,3,2]{1,2,0:T(2,128)}), f32[128,3,2]{1,2,0:T(2,128)S(1)}, u32[]{:S(2)}, u32[]{:S(2)}) async-start(f32[128,3,2]{1,2,0:T(2,128)} %copy.64), calls=%async_computation.2 | async-start | bytes 262144 | tf_op jit(solution)/shard_map/all_to_all | solution.py:85
  132.3 1.5 copy.67
  133.8 8.7 %all-to-all-done.2 = f32[128,3,2]{1,2,0:T(2,128)S(1)} async-done(((f32[128,3,2]{1,2,0:T(2,128)}), f32[128,3,2]{1,2,0:T(2,128)S(1)}, u32[]{:S(2)}, u32[]{:S(2)}) %all-to-all-start.2) | async-done | bytes 3104 | tf_op jit(solution)/shard_map/all_to_all | solution.py:85
  142.5 4.0 %all-to-all-start.3 = ((f32[128,3,2]{1,2,0:T(2,128)}), f32[128,3,2]{1,2,0:T(2,128)S(1)}, u32[]{:S(2)}, u32[]{:S(2)}) async-start(f32[128,3,2]{1,2,0:T(2,128)} %copy.67), calls=%async_computation.3 | async-start | bytes 262144 | tf_op jit(solution)/shard_map/all_to_all | solution.py:86
  146.5 0.8 gather_fusion.2
  147.5 0.9 gather_fusion
  148.4 0.6 copy.70
  149.3 0.9 gather_fusion.1
  150.1 6.5 %all-to-all-done.3 = f32[128,3,2]{1,2,0:T(2,128)S(1)} async-done(((f32[128,3,2]{1,2,0:T(2,128)}), f32[128,3,2]{1,2,0:T(2,128)S(1)}, u32[]{:S(2)}, u32[]{:S(2)}) %all-to-all-start.3) | async-done | bytes 3104 | tf_op jit(solution)/shard_map/all_to_all | solution.py:86
  156.9 0.9 gather_fusion.3
  158.0 0.6 copy.71
  (116 shorter events, 1.7 us)
Async XLA Ops:
  9.1 12.2 %copy-start = (s32[48]{0:T(128)S(1)}, s32[48]{0:T(128)}, u32[]{:S(2)}) copy-start(s32[48]{0:T(128)} %param.7) | copy-start | bytes 580
  9.1 52.0 %all-to-all-start = ((bf16[128,3,2,2048]{3,2,1,0:T(2,128)(2,1)}), bf16[128,3,2,2048]{3,2,1,0:T(2,128)(2,1)S(1)}, u32[]{:S(2)}, u32[]{:S(2)}) async-start(bf16[128,3,2,2048]{3,2,1,0:T(2,128)(2,1)} %bitcast.129), calls=%async_computation | async-start | bytes 6291456 | tf_op jit(solution)/shard_map/all_to_all | solution.py:64
  28.0 38.2 %copy-start.19 = (s32[1,1,512]{2,1,0:T(1,128)S(1)}, s32[1,1,512]{2,1,0:T(1,128)}, u32[]{:S(2)}) copy-start(s32[1,1,512]{2,1,0:T(1,128)} %get-tuple-element.25) | copy-start | bytes 6148
  28.0 38.3 %copy-start.20 = (s32[1,1,512]{2,1,0:T(1,128)S(1)}, s32[1,1,512]{2,1,0:T(1,128)}, u32[]{:S(2)}) copy-start(s32[1,1,512]{2,1,0:T(1,128)} %get-tuple-element.26) | copy-start | bytes 6148
  28.0 38.3 %copy-start.21 = (s32[1,1,512]{2,1,0:T(1,128)S(1)}, s32[1,1,512]{2,1,0:T(1,128)}, u32[]{:S(2)}) copy-start(s32[1,1,512]{2,1,0:T(1,128)} %get-tuple-element.27) | copy-start | bytes 6148
  28.0 38.3 %copy-start.22 = (s32[1,1,512]{2,1,0:T(1,128)S(1)}, s32[1,1,512]{2,1,0:T(1,128)}, u32[]{:S(2)}) copy-start(s32[1,1,512]{2,1,0:T(1,128)} %get-tuple-element.28) | copy-start | bytes 6148
  28.1 38.3 %copy-start.23 = (s32[1,1,512]{2,1,0:T(1,128)S(1)}, s32[1,1,512]{2,1,0:T(1,128)}, u32[]{:S(2)}) copy-start(s32[1,1,512]{2,1,0:T(1,128)} %get-tuple-element.29) | copy-start | bytes 6148
  28.1 38.3 %copy-start.24 = (s32[1,1,512]{2,1,0:T(1,128)S(1)}, s32[1,1,512]{2,1,0:T(1,128)}, u32[]{:S(2)}) copy-start(s32[1,1,512]{2,1,0:T(1,128)} %get-tuple-element.30) | copy-start | bytes 6148
  28.1 38.3 %copy-start.25 = (s32[1,1,512]{2,1,0:T(1,128)S(1)}, s32[1,1,512]{2,1,0:T(1,128)}, u32[]{:S(2)}) copy-start(s32[1,1,512]{2,1,0:T(1,128)} %get-tuple-element.31) | copy-start | bytes 6148
  28.1 38.3 %copy-start.26 = (s32[1,1,512]{2,1,0:T(1,128)S(1)}, s32[1,1,512]{2,1,0:T(1,128)}, u32[]{:S(2)}) copy-start(s32[1,1,512]{2,1,0:T(1,128)} %get-tuple-element.32) | copy-start | bytes 6148
  28.1 38.3 %copy-start.27 = (s32[1,1,512]{2,1,0:T(1,128)S(1)}, s32[1,1,512]{2,1,0:T(1,128)}, u32[]{:S(2)}) copy-start(s32[1,1,512]{2,1,0:T(1,128)} %get-tuple-element.33) | copy-start | bytes 6148
  28.1 38.3 %copy-start.28 = (s32[1,1,512]{2,1,0:T(1,128)S(1)}, s32[1,1,512]{2,1,0:T(1,128)}, u32[]{:S(2)}) copy-start(s32[1,1,512]{2,1,0:T(1,128)} %get-tuple-element.34) | copy-start | bytes 6148
  28.1 38.3 %copy-start.29 = (s32[1,1,512]{2,1,0:T(1,128)S(1)}, s32[1,1,512]{2,1,0:T(1,128)}, u32[]{:S(2)}) copy-start(s32[1,1,512]{2,1,0:T(1,128)} %get-tuple-element.35) | copy-start | bytes 6148
  28.1 38.3 %copy-start.30 = (s32[1,1,512]{2,1,0:T(1,128)S(1)}, s32[1,1,512]{2,1,0:T(1,128)}, u32[]{:S(2)}) copy-start(s32[1,1,512]{2,1,0:T(1,128)} %get-tuple-element.36) | copy-start | bytes 6148
  28.1 38.3 %copy-start.31 = (s32[1,1,512]{2,1,0:T(1,128)S(1)}, s32[1,1,512]{2,1,0:T(1,128)}, u32[]{:S(2)}) copy-start(s32[1,1,512]{2,1,0:T(1,128)} %get-tuple-element.37) | copy-start | bytes 6148
  28.1 38.3 %copy-start.32 = (s32[1,1,512]{2,1,0:T(1,128)S(1)}, s32[1,1,512]{2,1,0:T(1,128)}, u32[]{:S(2)}) copy-start(s32[1,1,512]{2,1,0:T(1,128)} %get-tuple-element.38) | copy-start | bytes 6148
  28.2 38.3 %copy-start.33 = (s32[1,1,512]{2,1,0:T(1,128)S(1)}, s32[1,1,512]{2,1,0:T(1,128)}, u32[]{:S(2)}) copy-start(s32[1,1,512]{2,1,0:T(1,128)} %get-tuple-element.39) | copy-start | bytes 6148
  28.2 38.3 %copy-start.34 = (s32[1,1,512]{2,1,0:T(1,128)S(1)}, s32[1,1,512]{2,1,0:T(1,128)}, u32[]{:S(2)}) copy-start(s32[1,1,512]{2,1,0:T(1,128)} %get-tuple-element.40) | copy-start | bytes 6148
  28.2 38.3 %copy-start.35 = (s32[1,1,512]{2,1,0:T(1,128)S(1)}, s32[1,1,512]{2,1,0:T(1,128)}, u32[]{:S(2)}) copy-start(s32[1,1,512]{2,1,0:T(1,128)} %get-tuple-element.41) | copy-start | bytes 6148
  28.2 38.3 %copy-start.36 = (s32[1,1,512]{2,1,0:T(1,128)S(1)}, s32[1,1,512]{2,1,0:T(1,128)}, u32[]{:S(2)}) copy-start(s32[1,1,512]{2,1,0:T(1,128)} %get-tuple-element.42) | copy-start | bytes 6148
  28.2 38.3 %copy-start.37 = (s32[1,1,512]{2,1,0:T(1,128)S(1)}, s32[1,1,512]{2,1,0:T(1,128)}, u32[]{:S(2)}) copy-start(s32[1,1,512]{2,1,0:T(1,128)} %get-tuple-element.44) | copy-start | bytes 6148
  28.2 38.3 %copy-start.38 = (s32[1,1,512]{2,1,0:T(1,128)S(1)}, s32[1,1,512]{2,1,0:T(1,128)}, u32[]{:S(2)}) copy-start(s32[1,1,512]{2,1,0:T(1,128)} %get-tuple-element.45) | copy-start | bytes 6148
  28.2 38.3 %copy-start.39 = (s32[1,1,512]{2,1,0:T(1,128)S(1)}, s32[1,1,512]{2,1,0:T(1,128)}, u32[]{:S(2)}) copy-start(s32[1,1,512]{2,1,0:T(1,128)} %get-tuple-element.46) | copy-start | bytes 6148
  28.2 38.3 %copy-start.40 = (s32[1,1,512]{2,1,0:T(1,128)S(1)}, s32[1,1,512]{2,1,0:T(1,128)}, u32[]{:S(2)}) copy-start(s32[1,1,512]{2,1,0:T(1,128)} %get-tuple-element.47) | copy-start | bytes 6148
  28.2 38.3 %copy-start.41 = (s32[1,1,512]{2,1,0:T(1,128)S(1)}, s32[1,1,512]{2,1,0:T(1,128)}, u32[]{:S(2)}) copy-start(s32[1,1,512]{2,1,0:T(1,128)} %get-tuple-element.48) | copy-start | bytes 6148
  28.2 38.3 %copy-start.42 = (s32[1,1,512]{2,1,0:T(1,128)S(1)}, s32[1,1,512]{2,1,0:T(1,128)}, u32[]{:S(2)}) copy-start(s32[1,1,512]{2,1,0:T(1,128)} %get-tuple-element.49) | copy-start | bytes 6148
  66.5 15.0 %copy-start.2 = (bf16[128,1,2,2048]{3,2,1,0:T(2,128)(2,1)S(1)}, bf16[128,1,2,2048]{3,2,1,0:T(2,128)(2,1)}, u32[]{:S(2)}) copy-start(bf16[128,1,2,2048]{3,2,1,0:T(2,128)(2,1)} %get-tuple-element.23) | copy-start | bytes 3145732
  66.5 15.4 %copy-start.4 = (s32[1,1,512]{2,1,0:T(1,128)S(1)}, s32[1,1,512]{2,1,0:T(1,128)}, u32[]{:S(2)}) copy-start(s32[1,1,512]{2,1,0:T(1,128)} %get-tuple-element.74) | copy-start | bytes 6148
  66.5 15.4 %copy-start.5 = (s32[1,1,512]{2,1,0:T(1,128)S(1)}, s32[1,1,512]{2,1,0:T(1,128)}, u32[]{:S(2)}) copy-start(s32[1,1,512]{2,1,0:T(1,128)} %get-tuple-element.75) | copy-start | bytes 6148
  66.5 15.4 %copy-start.6 = (s32[1,1,512]{2,1,0:T(1,128)S(1)}, s32[1,1,512]{2,1,0:T(1,128)}, u32[]{:S(2)}) copy-start(s32[1,1,512]{2,1,0:T(1,128)} %get-tuple-element.76) | copy-start | bytes 6148
  66.5 15.4 %copy-start.7 = (s32[1,1,512]{2,1,0:T(1,128)S(1)}, s32[1,1,512]{2,1,0:T(1,128)}, u32[]{:S(2)}) copy-start(s32[1,1,512]{2,1,0:T(1,128)} %get-tuple-element.77) | copy-start | bytes 6148
  66.6 15.4 %copy-start.8 = (s32[1,1,512]{2,1,0:T(1,128)S(1)}, s32[1,1,512]{2,1,0:T(1,128)}, u32[]{:S(2)}) copy-start(s32[1,1,512]{2,1,0:T(1,128)} %get-tuple-element.78) | copy-start | bytes 6148
  66.6 15.4 %copy-start.9 = (s32[1,1,512]{2,1,0:T(1,128)S(1)}, s32[1,1,512]{2,1,0:T(1,128)}, u32[]{:S(2)}) copy-start(s32[1,1,512]{2,1,0:T(1,128)} %get-tuple-element.79) | copy-start | bytes 6148
  66.6 15.4 %copy-start.10 = (s32[1,1,512]{2,1,0:T(1,128)S(1)}, s32[1,1,512]{2,1,0:T(1,128)}, u32[]{:S(2)}) copy-start(s32[1,1,512]{2,1,0:T(1,128)} %get-tuple-element.80) | copy-start | bytes 6148
  66.6 15.4 %copy-start.11 = (s32[1,1,512]{2,1,0:T(1,128)S(1)}, s32[1,1,512]{2,1,0:T(1,128)}, u32[]{:S(2)}) copy-start(s32[1,1,512]{2,1,0:T(1,128)} %get-tuple-element.82) | copy-start | bytes 6148
  66.6 15.4 %copy-start.12 = (s32[1,1,512]{2,1,0:T(1,128)S(1)}, s32[1,1,512]{2,1,0:T(1,128)}, u32[]{:S(2)}) copy-start(s32[1,1,512]{2,1,0:T(1,128)} %get-tuple-element.83) | copy-start | bytes 6148
  66.6 15.4 %copy-start.13 = (s32[1,1,512]{2,1,0:T(1,128)S(1)}, s32[1,1,512]{2,1,0:T(1,128)}, u32[]{:S(2)}) copy-start(s32[1,1,512]{2,1,0:T(1,128)} %get-tuple-element.84) | copy-start | bytes 6148
  66.6 15.4 %copy-start.14 = (s32[1,1,512]{2,1,0:T(1,128)S(1)}, s32[1,1,512]{2,1,0:T(1,128)}, u32[]{:S(2)}) copy-start(s32[1,1,512]{2,1,0:T(1,128)} %get-tuple-element.85) | copy-start | bytes 6148
  66.6 15.4 %copy-start.15 = (s32[1,1,512]{2,1,0:T(1,128)S(1)}, s32[1,1,512]{2,1,0:T(1,128)}, u32[]{:S(2)}) copy-start(s32[1,1,512]{2,1,0:T(1,128)} %get-tuple-element.86) | copy-start | bytes 6148
  66.6 15.4 %copy-start.16 = (s32[1,1,512]{2,1,0:T(1,128)S(1)}, s32[1,1,512]{2,1,0:T(1,128)}, u32[]{:S(2)}) copy-start(s32[1,1,512]{2,1,0:T(1,128)} %get-tuple-element.87) | copy-start | bytes 6148
  66.6 15.4 %copy-start.17 = (s32[1,1,512]{2,1,0:T(1,128)S(1)}, s32[1,1,512]{2,1,0:T(1,128)}, u32[]{:S(2)}) copy-start(s32[1,1,512]{2,1,0:T(1,128)} %get-tuple-element.88) | copy-start | bytes 6148
  66.7 15.4 %copy-start.18 = (s32[1,1,512]{2,1,0:T(1,128)S(1)}, s32[1,1,512]{2,1,0:T(1,128)}, u32[]{:S(2)}) copy-start(s32[1,1,512]{2,1,0:T(1,128)} %get-tuple-element.89) | copy-start | bytes 6148
  82.1 14.9 %copy-start.1 = (bf16[128,1,2,2048]{3,2,1,0:T(2,128)(2,1)S(1)}, bf16[128,1,2,2048]{3,2,1,0:T(2,128)(2,1)}, u32[]{:S(2)}) copy-start(bf16[128,1,2,2048]{3,2,1,0:T(2,128)(2,1)} %get-tuple-element.21) | copy-start | bytes 3145732
  82.1 15.3 %copy-start.44 = (pred[512]{0:T(512)(128)(4,1)S(1)}, pred[512]{0:T(512)(128)(4,1)}, u32[]{:S(2)}) copy-start(pred[512]{0:T(512)(128)(4,1)} %fusion.421) | copy-start | bytes 1540
  111.5 35.0 %copy-start.43 = (s32[64]{0:T(128)S(1)}, s32[64]{0:T(128)}, u32[]{:S(2)}) copy-start(s32[64]{0:T(128)} %get-tuple-element.121) | copy-start | bytes 772
  113.1 15.1 %all-to-all-start.1 = ((f32[128,3,2]{1,2,0:T(2,128)}), f32[128,3,2]{1,2,0:T(2,128)S(1)}, u32[]{:S(2)}, u32[]{:S(2)}) async-start(f32[128,3,2]{1,2,0:T(2,128)} %copy.60), calls=%async_computation.1 | async-start | bytes 262144 | tf_op jit(solution)/shard_map/all_to_all | solution.py:84
  128.2 14.2 %all-to-all-start.2 = ((f32[128,3,2]{1,2,0:T(2,128)}), f32[128,3,2]{1,2,0:T(2,128)S(1)}, u32[]{:S(2)}, u32[]{:S(2)}) async-start(f32[128,3,2]{1,2,0:T(2,128)} %copy.64), calls=%async_computation.2 | async-start | bytes 262144 | tf_op jit(solution)/shard_map/all_to_all | solution.py:85
  142.5 14.2 %all-to-all-start.3 = ((f32[128,3,2]{1,2,0:T(2,128)}), f32[128,3,2]{1,2,0:T(2,128)S(1)}, u32[]{:S(2)}, u32[]{:S(2)}) async-start(f32[128,3,2]{1,2,0:T(2,128)} %copy.67), calls=%async_computation.3 | async-start | bytes 262144 | tf_op jit(solution)/shard_map/all_to_all | solution.py:86
  (1 other events, 11.6 us)
where the time goes:
time: 159 us
  waiting for transfers between devices  55.9 us (35%)
  matrix products  45.5 us (29%)
  local copies, waits for them, and re-layouts  26.3 us (17%)
  starting transfers between devices  24.4 us (15%)
  other arithmetic  4.93 us (3%)
  between operations  1.6 us (1%)
    dot_general x3, matrix products, window_stats(): jnp.dot(rows_now, theory, preferred_element_type=jnp.float32) / frags  43.4 us
    all_to_all x1, waiting for transfers between devices, per_device(): lax.all_to_all(copies, ('spec', 'mass'), split_axis=0, concat_axis=0, til...  32.8 us
    all_to_all x1, starting transfers between devices, per_device(): lax.all_to_all(copies, ('spec', 'mass'), split_axis=0, concat_axis=0, til...  11.5 us
    all_to_all x1, waiting for transfers between devices, per_device(): lax.all_to_all(summed, ('spec', 'mass'), split_axis=0, concat_axis=0, til...  8.67 us
    all_to_all x1, waiting for transfers between devices, per_device(): lax.all_to_all(highest, ('spec', 'mass'), split_axis=0, concat_axis=0, ti...  7.83 us
    all_to_all x1, waiting for transfers between devices, per_device(): lax.all_to_all(squared, ('spec', 'mass'), split_axis=0, concat_axis=0, ti...  6.55 us
    all_to_all x1, starting transfers between devices, per_device(): lax.all_to_all(highest, ('spec', 'mass'), split_axis=0, concat_axis=0, ti...  4.88 us
    broadcast_in_dim x2, local copies, waits for them, and re-layouts, per_device(): copies = jnp.broadcast_to(outgoing[None], (spec_count,) + outgoing.shape)  4.12 us
  transfers between devices with their start and end apart: 4, of which 4 were waited for; matrix products, arithmetic and copies ran while one was open for 9% of the time, Pallas kernels for 0%

commit v1 on v0

v1 whole, which is shorter than its diff:
```python
import functools

import jax
import jax.numpy as jnp
from jax import lax
from jax.experimental import pallas as pl
from jax.experimental.pallas import tpu as pltpu
from jax.sharding import PartitionSpec as P

LAG = 75
EPS = 1e-06
PAD = 128
SLOTS = 8
LOW = 128
HIGH = 16
F8 = jnp.float8_e4m3fn
VMEM = pltpu.VMEM
SMEM = pltpu.SMEM


def iota(shape, axis):
    return lax.broadcasted_iota(jnp.int32, shape, axis)


def prepare_kernel(spectra_ref, routes_ref, pep_ref, out_ref, flat_ref, padded, turned):
    rows, width = spectra_ref.shape
    rooted = jnp.sqrt(spectra_ref[...].astype(jnp.float32)).astype(jnp.bfloat16)
    padded[:, :PAD] = jnp.zeros((rows, PAD), jnp.bfloat16)
    padded[:, PAD + width :] = jnp.zeros((rows, PAD), jnp.bfloat16)
    padded[:, PAD : PAD + width] = rooted
    block = 256
    gap = jnp.abs(iota((block + 2 * PAD, block), 0) - PAD - iota((block + 2 * PAD, block), 1))
    band = jnp.where((gap > 0) & (gap <= LAG), 1.0, 0.0).astype(jnp.bfloat16)
    total = out_ref.shape[0]
    place = iota((total, rows), 0)
    inner = place % SLOTS
    window = (place // SLOTS) * 3 + inner // 2
    named = (routes_ref[0:1, :] == window) | (routes_ref[1:2, :] == window)
    named = named & (inner < 6)
    before = jnp.where(iota((rows, rows), 0) < iota((rows, rows), 1), 1.0, 0.0)
    earlier = jnp.dot(
        jnp.where(named, 1.0, 0.0).astype(jnp.bfloat16),
        before.astype(jnp.bfloat16),
        preferred_element_type=jnp.float32,
    )
    taken = named & (earlier == (inner % 2).astype(jnp.float32))
    routing = jnp.where(taken, 1.0, 0.0).astype(jnp.bfloat16)
    for start in range(0, width, block):
        background = jnp.dot(
            padded[:, start : start + block + 2 * PAD], band, preferred_element_type=jnp.float32
        )
        values = rooted[:, start : start + block].astype(jnp.float32)
        prepared = (values - background / (2.0 * LAG)).astype(jnp.bfloat16)
        out_ref[:, start : start + block] = jnp.dot(
            routing, prepared, preferred_element_type=jnp.float32
        ).astype(jnp.bfloat16)
    lane = iota((128, 128), 1) // 32
    for step in range(pep_ref.shape[0]):
        table = pep_ref[step]
        turned[...] = jnp.concatenate([table] * 4, axis=0).T
        flat = jnp.zeros((128, 128), jnp.int32)
        for part in range(4):
            flat = jnp.where(lane == part, turned[pl.ds(part, 128, stride=4), :], flat)
        flat_ref[step] = flat.astype(jnp.int16)


def theory_kernel(flat_ref, theory_ref):
    width = flat_ref.shape[2]
    high_place = iota((HIGH * 8, 2 * width), 0).astype(jnp.float32).astype(jnp.bfloat16)
    low_place = iota((LOW, 2 * width), 0).astype(jnp.float32).astype(jnp.bfloat16)
    one = jnp.ones((), F8)
    zero = jnp.zeros((), F8)
    member = iota((128, 128), 1) // 32 + 4 * (iota((128, 128), 0) % 2)

    def window(step, carry):
        bins = flat_ref[step].astype(jnp.int32)
        low = (bins & (LOW - 1)).astype(jnp.float32).astype(jnp.bfloat16)
        high = ((bins >> 7) * 8 + member).astype(jnp.float32).astype(jnp.bfloat16)
        for pair in range(32):
            parts = []
            for half in range(2):
                row = 4 * pair + 2 * half
                high_row = jnp.concatenate([high[row : row + 1], high[row + 1 : row + 2]], axis=1)
                low_row = jnp.concatenate([low[row : row + 1], low[row + 1 : row + 2]], axis=1)
                parts.append(
                    lax.dot_general(
                        jnp.where(high_place == high_row, one, zero),
                        jnp.where(low_place == low_row, one, zero),
                        (((1,), (1,)), ((), ())),
                        preferred_element_type=jnp.float32,
                    )
                )
            for part in range(HIGH):
                tile = jnp.concatenate([item[part * 8 : part * 8 + 8] for item in parts], axis=0)
                theory_ref[step, pair * 16 : pair * 16 + 16, part * LOW : (part + 1) * LOW] = (
                    tile.astype(jnp.bfloat16)
                )
        return carry

    lax.fori_loop(0, flat_ref.shape[0], window, 0)


def build_theory(flat, width):
    steps = flat.shape[0]
    return pl.pallas_call(
        theory_kernel,
        out_shape=jax.ShapeDtypeStruct((steps, 512, width), jnp.bfloat16),
        in_specs=[pl.BlockSpec(memory_space=VMEM)],
        out_specs=pl.BlockSpec(memory_space=VMEM),
        compiler_params=pltpu.CompilerParams(vmem_limit_bytes=16 << 20),
        cost_estimate=pl.CostEstimate(
            flops=3_000_000_000, bytes_accessed=6_400_000, transcendentals=0
        ),
        name="theory",
    )(flat)


def score_kernel(counts_ref, t0, t1, t2, t3, own_ref, other_ref, out_ref):
    y = lax.axis_index("spec") // 2
    core = lax.axis_index("spec") % 2
    mass = lax.axis_index("mass")
    steps = t0.shape[0]
    rows = own_ref.shape[0] * 2
    spectra = jnp.concatenate([own_ref[...], other_ref[...]], axis=0)
    slot = (iota((1, rows), 1) % SLOTS) // 2
    local = iota((512, 1), 0)
    best = jnp.zeros((1, rows), jnp.float32)
    total = jnp.zeros((1, rows), jnp.float32)
    square = jnp.zeros((1, rows), jnp.float32)
    for step in range(steps):
        live = counts_ref[mass * steps + step]
        now_best, now_total, now_square = [], [], []
        for turn, theory in enumerate((t0, t1, t2, t3)):
            base = (((y + turn) % 4) * 2 + core) * 512
            scores = lax.dot_general(
                theory[step],
                spectra,
                (((1,), (1,)), ((), ())),
                preferred_element_type=jnp.float32,
            )
            valid = local < (live - base)
            now_best.append(
                jnp.max(jnp.where(valid, scores, -1e30), axis=0, keepdims=True)
            )
            scores = jnp.where(valid, scores, 0.0)
            now_total.append(jnp.sum(scores, axis=0, keepdims=True))
            now_square.append(jnp.sum(scores * scores, axis=0, keepdims=True))
        here = slot == step
        best = jnp.where(here, functools.reduce(jnp.maximum, now_best), best)
        total = jnp.where(here, sum(now_total[1:], now_total[0]), total)
        square = jnp.where(here, sum(now_square[1:], now_square[0]), square)
    stats = jnp.concatenate(
        [best / 32.0, total / 32.0, square / 1024.0, jnp.zeros((5, rows), jnp.float32)], axis=0
    )
    own, other = stats[:, : rows // 2], stats[:, rows // 2 :]
    first = jnp.where(core == 0, own, other)
    second = jnp.where(core == 0, other, own)
    peers = out_ref.shape[0] // 16
    for peer in range(peers):
        out_ref[peer * 8 : peer * 8 + 8, :] = first
        out_ref[(peers + peer) * 8 : (peers + peer) * 8 + 8, :] = second


def finish_kernel(counts_ref, routes_ref, stats_ref, best_ref, z_ref):
    rows = routes_ref.shape[1]
    mass = lax.axis_index("mass")
    windows = counts_ref.shape[1]
    picks = [routes_ref[0:1, :], routes_ref[1:2, :]]
    flat = jnp.concatenate(picks, axis=1)
    named_by = iota((windows, rows), 0)
    named = (picks[0] == named_by) | (picks[1] == named_by)
    before = jnp.where(iota((rows, rows), 0) < iota((rows, rows), 1), 1.0, 0.0)
    earlier = jnp.dot(
        jnp.where(named, 1.0, 0.0).astype(jnp.bfloat16),
        before.astype(jnp.bfloat16),
        preferred_element_type=jnp.float32,
    )
    slot = jnp.concatenate(
        [
            jnp.sum(jnp.where(pick == named_by, earlier, 0.0), axis=0, keepdims=True)
            for pick in picks
        ],
        axis=1,
    ).astype(jnp.int32)
    shard = flat // 3
    wanted = mass * SLOTS + (flat - shard * 3) * 2 + slot
    entries = 2 * rows
    lanes = stats_ref.shape[1]
    pick_lane = jnp.where(iota((lanes, entries), 0) == wanted, 1.0, 0.0)
    found = lax.dot_general(
        stats_ref[...],
        pick_lane,
        (((1,), (0,)), ((), ())),
        precision=lax.Precision.HIGHEST,
        preferred_element_type=jnp.float32,
    )
    peers = stats_ref.shape[0] // 16
    halves = []
    for half in range(2):
        chosen = jnp.zeros((8, entries), jnp.float32)
        for peer in range(peers):
            at = (half * peers + peer) * 8
            chosen = jnp.where(shard == peer, found[at : at + 8, :], chosen)
        halves.append(chosen)
    best = jnp.maximum(halves[0][0:1], halves[1][0:1])
    total = halves[0][1:2] + halves[1][1:2]
    square = halves[0][2:3] + halves[1][2:3]
    column = counts_ref[...].astype(jnp.float32)
    here = iota((entries, windows), 1)
    live = jnp.zeros((1, entries), jnp.float32)
    del here
    live = lax.dot_general(
        column,
        jnp.where(iota((windows, entries), 0) == flat, 1.0, 0.0),
        (((1,), (0,)), ((), ())),
        precision=lax.Precision.HIGHEST,
        preferred_element_type=jnp.float32,
    )
    mean = total / live
    spread = square / live - mean * mean
    z = (best - mean) / jnp.sqrt(spread + EPS)
    best_ref[0:1, :] = best[:, :rows]
    best_ref[1:2, :] = best[:, rows:]
    z_ref[0:1, :] = z[:, :rows]
    z_ref[1:2, :] = z[:, rows:]


def per_device(spectra, routes, pep_bins, counts):
    rows, width = spectra.shape
    mass_count = lax.axis_size("mass")
    spec_count = lax.axis_size("spec")
    steps = pep_bins.shape[0]
    routes_t = routes.T
    vmem = pl.BlockSpec(memory_space=VMEM)
    smem = pl.BlockSpec(memory_space=SMEM)
    outgoing, flat = pl.pallas_call(
        prepare_kernel,
        out_shape=(
            jax.ShapeDtypeStruct((mass_count * SLOTS, width), jnp.bfloat16),
            jax.ShapeDtypeStruct((steps, 128, 128), jnp.int16),
        ),
        in_specs=[vmem] * 3,
        out_specs=(vmem, vmem),
        scratch_shapes=[
            pltpu.VMEM((rows, width + 2 * PAD), jnp.bfloat16),
            pltpu.VMEM((512, 128), jnp.int32),
        ],
        compiler_params=pltpu.CompilerParams(vmem_limit_bytes=16 << 20),
        name="prepare",
    )(spectra, routes_t, pep_bins)
    flats = [flat] + [
        lax.ppermute(
            flat, "spec", [((i + 2 * turn) % spec_count, i) for i in range(spec_count)]
        )
        for turn in range(1, 4)
    ]
    own = lax.all_to_all(outgoing, "mass", split_axis=0, concat_axis=0, tiled=True)
    other = lax.ppermute(own, "spec", [(i, i ^ 1) for i in range(spec_count)])
    theories = [build_theory(item, width) for item in flats]
    stats = pl.pallas_call(
        score_kernel,
        out_shape=jax.ShapeDtypeStruct((2 * mass_count * 8, 128), jnp.float32),
        in_specs=[smem] + [vmem] * 6,
        out_specs=vmem,
        compiler_params=pltpu.CompilerParams(vmem_limit_bytes=48 << 20),
        name="score",
    )(counts, *theories, own, other)
    groups = [
        [(y * 2 + core) * mass_count + m for core in range(2) for m in range(mass_count)]
        for y in range(spec_count // 2)
    ]
    back = lax.all_to_all(
        stats,
        ("spec", "mass"),
        split_axis=0,
        concat_axis=0,
        tiled=True,
        axis_index_groups=groups,
    )
    best, z = pl.pallas_call(
        finish_kernel,
        out_shape=(jax.ShapeDtypeStruct((2, rows), jnp.float32),) * 2,
        in_specs=[vmem] * 3,
        out_specs=(vmem, vmem),
        name="finish",
    )(counts.reshape(1, -1), routes_t, back)
    return best.T, z.T


def solution(mesh):
    return jax.shard_map(
        per_device,
        mesh=mesh,
        in_specs=(
            P(("spec", "mass"), None),
            P(("spec", "mass"), None),
            P("mass", None, "spec"),
            P(),
        ),
        out_specs=(P(("spec", "mass"), None), P(("spec", "mass"), None)),
        check_vma=False,
    )
```

time: 159 us -> 72.6 us (0.46)
  waiting for transfers between devices: 55.9 us -> 0.58 us
  matrix products: 45.5 us -> 0 us
  Pallas kernels: 0 us -> 28.6 us
  blocking collectives: 0 us -> 13.5 us
  local copies, waits for them, and re-layouts: 26.3 us -> 13 us
  starting transfers between devices: 24.4 us -> 16 us
  other arithmetic: 4.93 us -> 0 us
    all_to_all x4 -> x1, waiting for transfers between devices: 55.9 us -> 0.57 us  [per_device(): lax.all_to_all(outgoing, 'mass', split_axis=0, concat_axis=0, tiled=True)]
    dot_general x4 -> x0, matrix products: 45.5 us -> none  [the longest x3 43.4 us: window_stats(): jnp.dot(rows_now, theory, preferred_element_type=jnp.float32) / frags]
    pallas_call x0 -> x7, Pallas kernels: none -> 28.6 us  [the longest x1 15.7 us: per_device(): pl.pallas_call(score_kernel, out_shape=jax.ShapeDtypeStruct((2 * mass_cou...]
    all_to_all x4 -> x1, starting transfers between devices: 24.4 us -> 7.6 us  [per_device(): lax.all_to_all(outgoing, 'mass', split_axis=0, concat_axis=0, tiled=True)]
    all_to_all x0 -> x1, blocking collectives: none -> 13.5 us  [per_device(): lax.all_to_all(stats, ('spec', 'mass'), split_axis=0, concat_axis=0, tile...]
    unnamed x93 -> x16, local copies, waits for them, and re-layouts: 2.23 us -> 13 us
    ppermute x0 -> x4, starting transfers between devices: none -> 8.38 us  [the longest x3 5.82 us: per_device(): lax.ppermute(flat, 'spec', [((i + 2 * turn) % spec_count, i) for i in ran...]
    another operation x15 -> x0, local copies, waits for them, and re-layouts: 8.07 us -> none  [the longest x3 2.34 us: per_device(): rows_now = incoming[:, window_step].reshape(-1, width)]
  transfers between devices with their start and end apart: 4 -> 5, of which waited for: 4 -> 1; matrix products, arithmetic and copies ran while one was open for 9% -> 0% of each run, Pallas kernels for 0% -> 11%
where the time goes in v1:
time: 72.6 us; the launch traced here: 72.3 us
  Pallas kernels  28.6 us (39%)
  starting transfers between devices  16 us (22%)
  blocking collectives  13.5 us (19%)
  local copies, waits for them, and re-layouts  13 us (18%)
  between operations  0.73 us (1%)
    pallas_call x1, Pallas kernels, per_device(): pl.pallas_call(score_kernel, out_shape=jax.ShapeDtypeStruct((2 * mass_cou...  15.7 us
    all_to_all x1, blocking collectives, per_device(): lax.all_to_all(stats, ('spec', 'mass'), split_axis=0, concat_axis=0, tile...  13.5 us
    unnamed x16, local copies, waits for them, and re-layouts  13 us
    pallas_call x4, Pallas kernels, build_theory(): pl.pallas_call(theory_kernel, out_shape=jax.ShapeDtypeStruct((steps, 512,...  8.14 us
    all_to_all x1, starting transfers between devices, per_device(): lax.all_to_all(outgoing, 'mass', split_axis=0, concat_axis=0, tiled=True)  7.6 us
    ppermute x3, starting transfers between devices, per_device(): lax.ppermute(flat, 'spec', [((i + 2 * turn) % spec_count, i) for i in ran...  5.82 us
    pallas_call x1, Pallas kernels, per_device(): pl.pallas_call(prepare_kernel, out_shape=(jax.ShapeDtypeStruct((mass_coun...  2.6 us
    ppermute x1, starting transfers between devices, per_device(): other = lax.ppermute(own, 'spec', [(i, i ^ 1) for i in range(spec_count)])  2.57 us
  transfers between devices with their start and end apart: 5, of which 1 were waited for; matrix products, arithmetic and copies ran while one was open for 0% of the time, Pallas kernels for 11%

profile of v1, /device:TPU:1, one launch (start us, length us, event | category | flops | bytes accessed | tf_op | source)
XLA Modules:
  0.0 72.3 jit_solution(5826360897777747962)
XLA Ops:
  0.6 0.0 copy-start.4
  0.6 0.9 %copy-done.4 = s32[3,32,512]{2,1,0:T(8,128)S(1)} copy-done((s32[3,32,512]{2,1,0:T(8,128)S(1)}, s32[3,32,512]{2,1,0:T(8,128)}, u32[]{:S(2)}) %copy-start.4) | copy-done | bytes 196632
  1.6 0.0 copy-start.5
  1.6 0.9 %copy-done.5 = bf16[32,2048]{1,0:T(8,128)(2,1)S(1)} copy-done((bf16[32,2048]{1,0:T(8,128)(2,1)S(1)}, bf16[32,2048]{1,0:T(8,128)(2,1)}, u32[]{:S(2)}) %copy-start.5) | copy-done | bytes 131096
  2.5 0.0 copy-start.6
  2.5 0.7 copy-done.6
  3.1 2.6 %prepare.1 = (bf16[128,2048]{1,0:T(8,128)(2,1)}, s16[3,128,128]{2,1,0:T(8,128)(2,1)S(1)}) custom-call(bf16[32,2048]{1,0:T(8,128)(2,1)S(1)} %copy-done.5, s32[2,32]{1,0:T(2,128)S(1)} %bitcast.12, s32[3,32,512]{2,1,0:T(8,128)S(1)} %copy-done.4), custom_call_target="tpu_custom_call" | custom-call | tf_op jit(solution)/shard_map/prepare/pallas_call | solution.py:236
  5.7 2.1 %collective-permute-start.2 = (s16[3,128,128]{2,1,0:T(8,128)(2,1)S(1)}, s16[3,128,128]{2,1,0:T(8,128)(2,1)S(1)}, u32[]{:S(2)}, u32[]{:S(2)}) collective-permute-start(s16[3,128,128]{2,1,0:T(8,128)(2,1)S(1)} %get-tuple-element.6.flat_ref), channel_id=1, source_target_pairs={{96,0},{112,16},{0,32},{16,48},{32,64},{48,80},{64,96},{80,112},{9... | collective-permute-start | bytes 294920 | tf_op jit(solution)/shard_map/ppermute | solution.py:252
  7.9 2.6 %collective-permute-start.1 = (s16[3,128,128]{2,1,0:T(8,128)(2,1)S(1)}, s16[3,128,128]{2,1,0:T(8,128)(2,1)S(1)}, u32[]{:S(2)}, u32[]{:S(2)}) collective-permute-start(s16[3,128,128]{2,1,0:T(8,128)(2,1)S(1)} %get-tuple-element.6.flat_ref), channel_id=1, source_target_pairs={{64,0},{80,16},{96,32},{112,48},{0,64},{16,80},{32,96},{48,112},{6... | collective-permute-start | bytes 294920 | tf_op jit(solution)/shard_map/ppermute | solution.py:252
  10.5 1.1 %collective-permute-start = (s16[3,128,128]{2,1,0:T(8,128)(2,1)S(1)}, s16[3,128,128]{2,1,0:T(8,128)(2,1)S(1)}, u32[]{:S(2)}, u32[]{:S(2)}) collective-permute-start(s16[3,128,128]{2,1,0:T(8,128)(2,1)S(1)} %get-tuple-element.6.flat_ref), channel_id=1, source_target_pairs={{32,0},{48,16},{64,32},{80,48},{96,64},{112,80},{0,96},{16,112},{3... | collective-permute-start | bytes 294920 | tf_op jit(solution)/shard_map/ppermute | solution.py:252
  11.6 7.6 %all-to-all-start = ((bf16[16,8,2048]{2,1,0:T(8,128)(2,1)}), bf16[16,8,2048]{2,1,0:T(8,128)(2,1)S(1)}, u32[]{:S(2)}, u32[]{:S(2)}) async-start(bf16[16,8,2048]{2,1,0:T(8,128)(2,1)} %bitcast.2), calls=%async_computation | async-start | bytes 1048576 | tf_op jit(solution)/shard_map/all_to_all | solution.py:257
  19.2 2.0 %theory.4.t0 = bf16[3,512,2048]{2,1,0:T(8,128)(2,1)S(1)} custom-call(s16[3,128,128]{2,1,0:T(8,128)(2,1)S(1)} %get-tuple-element.6.flat_ref), custom_call_target="tpu_custom_call" | custom-call | flops 3000000000 | bytes 6400000 | tf_op jit(solution)/shard_map/theory/pallas_call | solution.py:105
  21.2 0.0 copy-start
  21.2 2.6 %copy-done = bf16[3,512,2048]{2,1,0:T(8,128)(2,1)} copy-done((bf16[3,512,2048]{2,1,0:T(8,128)(2,1)}, bf16[3,512,2048]{2,1,0:T(8,128)(2,1)S(1)}, u32[]{:S(2)}) %copy-start) | copy-done | bytes 6291480
  23.9 0.0 collective-permute-done.flat_ref
  23.9 2.0 %theory.5.t1 = bf16[3,512,2048]{2,1,0:T(8,128)(2,1)S(1)} custom-call(s16[3,128,128]{2,1,0:T(8,128)(2,1)S(1)} %collective-permute-done.flat_ref), custom_call_target="tpu_custom_call" | custom-call | flops 3000000000 | bytes 6400000 | tf_op jit(solution)/shard_map/theory/pallas_call | solution.py:105
  25.9 0.0 copy-start.1
  25.9 2.6 %copy-done.1 = bf16[3,512,2048]{2,1,0:T(8,128)(2,1)} copy-done((bf16[3,512,2048]{2,1,0:T(8,128)(2,1)}, bf16[3,512,2048]{2,1,0:T(8,128)(2,1)S(1)}, u32[]{:S(2)}) %copy-start.1) | copy-done | bytes 6291480
  28.6 0.6 all-to-all-done
  29.1 2.6 %collective-permute-start.3 = (bf16[128,2048]{1,0:T(8,128)(2,1)S(1)}, bf16[128,2048]{1,0:T(8,128)(2,1)S(1)}, u32[]{:S(2)}, u32[]{:S(2)}) collective-permute-start(bf16[128,2048]{1,0:T(8,128)(2,1)S(1)} %bitcast.8), channel_id=1, source_target_pairs={{0,16},{16,0},{32,48},{48,32},{64,80},{80,64},{96,112},{112,96},{1... | collective-permute-start | bytes 1572872 | tf_op jit(solution)/shard_map/ppermute | solution.py:258
  31.7 0.0 collective-permute-done.1.flat_ref
  31.7 2.0 %theory.6.t2 = bf16[3,512,2048]{2,1,0:T(8,128)(2,1)S(1)} custom-call(s16[3,128,128]{2,1,0:T(8,128)(2,1)S(1)} %collective-permute-done.1.flat_ref), custom_call_target="tpu_custom_call" | custom-call | flops 3000000000 | bytes 6400000 | tf_op jit(solution)/shard_map/theory/pallas_call | solution.py:105
  33.7 0.0 copy-start.2
  33.8 2.6 %copy-done.2 = bf16[3,512,2048]{2,1,0:T(8,128)(2,1)} copy-done((bf16[3,512,2048]{2,1,0:T(8,128)(2,1)}, bf16[3,512,2048]{2,1,0:T(8,128)(2,1)S(1)}, u32[]{:S(2)}) %copy-start.2) | copy-done | bytes 6291480
  36.3 0.0 copy-start.7
  36.3 0.0 collective-permute-done.2.flat_ref
  36.3 2.0 %theory.7.t3 = bf16[3,512,2048]{2,1,0:T(8,128)(2,1)S(1)} custom-call(s16[3,128,128]{2,1,0:T(8,128)(2,1)S(1)} %collective-permute-done.2.flat_ref), custom_call_target="tpu_custom_call" | custom-call | flops 3000000000 | bytes 6400000 | tf_op jit(solution)/shard_map/theory/pallas_call | solution.py:105
  38.4 0.0 copy-start.3
  38.4 2.6 %copy-done.3 = bf16[3,512,2048]{2,1,0:T(8,128)(2,1)} copy-done((bf16[3,512,2048]{2,1,0:T(8,128)(2,1)}, bf16[3,512,2048]{2,1,0:T(8,128)(2,1)S(1)}, u32[]{:S(2)}) %copy-start.3) | copy-done | bytes 6291480
  41.0 0.0 collective-permute-done.3.other_ref
  41.0 0.0 copy-done.7
  41.0 15.7 %score.1 = f32[256,128]{1,0:T(8,128)S(1)} custom-call(s32[48]{0:T(128)S(1)} %copy-done.7, bf16[3,512,2048]{2,1,0:T(8,128)(2,1)} %copy-done, bf16[3,512,2048]{2,1,0:T(8,128)(2,1)} %copy-done.1, bf16[3,512,2048]{2,1,0:T(8,128)(2,1)} %copy-done.2, bf16[3,512,2048]{2,1,0:T(8,128)(2,1)} %copy-done.3, bf16[128,2048]{1,0:T(8,128)(2,1)S(1)} %bitcast.9, ...), custom_call_target="tpu_custom_call" | custom-call | tf_op jit(solution)/shard_map/score/pallas_call | solution.py:260
  56.7 13.5 %all_to_all.22 = f32[32,8,128]{2,1,0:T(8,128)} all-to-all(f32[32,8,128]{2,1,0:T(8,128)S(1)} %bitcast.10), channel_id=1, replica_groups={{0,1,2,3,4,5,6,7,8,9,10,11,12,13,14,15,16,17,18,19,20,21,22,23,24,25,26..., dimensions={0} | all-to-all | bytes 262144 | tf_op jit(solution)/shard_map/all_to_all | solution.py:272
  70.2 2.1 %finish.1 = (f32[2,32]{1,0:T(2,128)}, f32[2,32]{1,0:T(2,128)}) custom-call(s32[1,48]{1,0:T(1,128)} %bitcast.13, s32[2,32]{1,0:T(2,128)} %bitcast.11, f32[256,128]{1,0:T(8,128)} %bitcast.14), custom_call_target="tpu_custom_call" | custom-call | tf_op jit(solution)/shard_map/finish/pallas_call | solution.py:280
Async XLA Ops:
  0.6 0.9 %copy-start.4 = (s32[3,32,512]{2,1,0:T(8,128)S(1)}, s32[3,32,512]{2,1,0:T(8,128)}, u32[]{:S(2)}) copy-start(s32[3,32,512]{2,1,0:T(8,128)} %pep_ref.1) | copy-start | bytes 589828
  1.6 0.9 %copy-start.5 = (bf16[32,2048]{1,0:T(8,128)(2,1)S(1)}, bf16[32,2048]{1,0:T(8,128)(2,1)}, u32[]{:S(2)}) copy-start(bf16[32,2048]{1,0:T(8,128)(2,1)} %spectra_ref.1) | copy-start | bytes 393220
  2.5 0.7 copy-start.6
  5.7 30.6 %collective-permute-start.2 = (s16[3,128,128]{2,1,0:T(8,128)(2,1)S(1)}, s16[3,128,128]{2,1,0:T(8,128)(2,1)S(1)}, u32[]{:S(2)}, u32[]{:S(2)}) collective-permute-start(s16[3,128,128]{2,1,0:T(8,128)(2,1)S(1)} %get-tuple-element.6.flat_ref), channel_id=1, source_target_pairs={{96,0},{112,16},{0,32},{16,48},{32,64},{48,80},{64,96},{80,112},{9... | collective-permute-start | bytes 294920 | tf_op jit(solution)/shard_map/ppermute | solution.py:252
  7.9 23.8 %collective-permute-start.1 = (s16[3,128,128]{2,1,0:T(8,128)(2,1)S(1)}, s16[3,128,128]{2,1,0:T(8,128)(2,1)S(1)}, u32[]{:S(2)}, u32[]{:S(2)}) collective-permute-start(s16[3,128,128]{2,1,0:T(8,128)(2,1)S(1)} %get-tuple-element.6.flat_ref), channel_id=1, source_target_pairs={{64,0},{80,16},{96,32},{112,48},{0,64},{16,80},{32,96},{48,112},{6... | collective-permute-start | bytes 294920 | tf_op jit(solution)/shard_map/ppermute | solution.py:252
  10.5 13.4 %collective-permute-start = (s16[3,128,128]{2,1,0:T(8,128)(2,1)S(1)}, s16[3,128,128]{2,1,0:T(8,128)(2,1)S(1)}, u32[]{:S(2)}, u32[]{:S(2)}) collective-permute-start(s16[3,128,128]{2,1,0:T(8,128)(2,1)S(1)} %get-tuple-element.6.flat_ref), channel_id=1, source_target_pairs={{32,0},{48,16},{64,32},{80,48},{96,64},{112,80},{0,96},{16,112},{3... | collective-permute-start | bytes 294920 | tf_op jit(solution)/shard_map/ppermute | solution.py:252
  11.6 17.6 %all-to-all-start = ((bf16[16,8,2048]{2,1,0:T(8,128)(2,1)}), bf16[16,8,2048]{2,1,0:T(8,128)(2,1)S(1)}, u32[]{:S(2)}, u32[]{:S(2)}) async-start(bf16[16,8,2048]{2,1,0:T(8,128)(2,1)} %bitcast.2), calls=%async_computation | async-start | bytes 1048576 | tf_op jit(solution)/shard_map/all_to_all | solution.py:257
  21.2 2.7 %copy-start = (bf16[3,512,2048]{2,1,0:T(8,128)(2,1)}, bf16[3,512,2048]{2,1,0:T(8,128)(2,1)S(1)}, u32[]{:S(2)}) copy-start(bf16[3,512,2048]{2,1,0:T(8,128)(2,1)S(1)} %theory.4.t0) | copy-start | bytes 18874372
  25.9 2.6 %copy-start.1 = (bf16[3,512,2048]{2,1,0:T(8,128)(2,1)}, bf16[3,512,2048]{2,1,0:T(8,128)(2,1)S(1)}, u32[]{:S(2)}) copy-start(bf16[3,512,2048]{2,1,0:T(8,128)(2,1)S(1)} %theory.5.t1) | copy-start | bytes 18874372
  29.1 11.8 %collective-permute-start.3 = (bf16[128,2048]{1,0:T(8,128)(2,1)S(1)}, bf16[128,2048]{1,0:T(8,128)(2,1)S(1)}, u32[]{:S(2)}, u32[]{:S(2)}) collective-permute-start(bf16[128,2048]{1,0:T(8,128)(2,1)S(1)} %bitcast.8), channel_id=1, source_target_pairs={{0,16},{16,0},{32,48},{48,32},{64,80},{80,64},{96,112},{112,96},{1... | collective-permute-start | bytes 1572872 | tf_op jit(solution)/shard_map/ppermute | solution.py:258
  33.7 2.6 %copy-start.2 = (bf16[3,512,2048]{2,1,0:T(8,128)(2,1)}, bf16[3,512,2048]{2,1,0:T(8,128)(2,1)S(1)}, u32[]{:S(2)}) copy-start(bf16[3,512,2048]{2,1,0:T(8,128)(2,1)S(1)} %theory.6.t2) | copy-start | bytes 18874372
  36.3 4.6 %copy-start.7 = (s32[48]{0:T(128)S(1)}, s32[48]{0:T(128)}, u32[]{:S(2)}) copy-start(s32[48]{0:T(128)} %counts_ref.1) | copy-start | bytes 580
  38.4 2.6 %copy-start.3 = (bf16[3,512,2048]{2,1,0:T(8,128)(2,1)}, bf16[3,512,2048]{2,1,0:T(8,128)(2,1)S(1)}, u32[]{:S(2)}) copy-start(bf16[3,512,2048]{2,1,0:T(8,128)(2,1)S(1)} %theory.7.t3) | copy-start | bytes 18874372

commit v2 on v1

--- a/solution.py
+++ b/solution.py
@@ -13,6 +13,7 @@
 SLOTS = 8
 LOW = 128
 HIGH = 16
+BUILT = 2
 F8 = jnp.float8_e4m3fn
 VMEM = pltpu.VMEM
 SMEM = pltpu.SMEM
@@ -22,15 +23,36 @@
     return lax.broadcasted_iota(jnp.int32, shape, axis)
 
 
-def prepare_kernel(spectra_ref, routes_ref, pep_ref, out_ref, flat_ref, padded, turned):
+def prepare_kernel(
+    spectra_hbm,
+    routes_hbm,
+    pep_hbm,
+    out_ref,
+    flat_ref,
+    spectra_ref,
+    routes_ref,
+    pep_ref,
+    padded,
+    turned,
+    sems,
+):
+    copies = [
+        pltpu.make_async_copy(spectra_hbm, spectra_ref, sems.at[0]),
+        pltpu.make_async_copy(routes_hbm, routes_ref, sems.at[1]),
+        pltpu.make_async_copy(pep_hbm, pep_ref, sems.at[2]),
+    ]
+    for copy in copies:
+        copy.start()
     rows, width = spectra_ref.shape
+    block = 256
+    gap = jnp.abs(iota((block + 2 * PAD, block), 0) - PAD - iota((block + 2 * PAD, block), 1))
+    band = jnp.where((gap > 0) & (gap <= LAG), 1.0, 0.0).astype(jnp.bfloat16)
+    copies[0].wait()
     rooted = jnp.sqrt(spectra_ref[...].astype(jnp.float32)).astype(jnp.bfloat16)
     padded[:, :PAD] = jnp.zeros((rows, PAD), jnp.bfloat16)
     padded[:, PAD + width :] = jnp.zeros((rows, PAD), jnp.bfloat16)
     padded[:, PAD : PAD + width] = rooted
-    block = 256
-    gap = jnp.abs(iota((block + 2 * PAD, block), 0) - PAD - iota((block + 2 * PAD, block), 1))
-    band = jnp.where((gap > 0) & (gap <= LAG), 1.0, 0.0).astype(jnp.bfloat16)
+    copies[1].wait()
     total = out_ref.shape[0]
     place = iota((total, rows), 0)
     inner = place % SLOTS
@@ -54,6 +76,7 @@
         out_ref[:, start : start + block] = jnp.dot(
             routing, prepared, preferred_element_type=jnp.float32
         ).astype(jnp.bfloat16)
+    copies[2].wait()
     lane = iota((128, 128), 1) // 32
     for step in range(pep_ref.shape[0]):
         table = pep_ref[step]
@@ -64,84 +87,113 @@
         flat_ref[step] = flat.astype(jnp.int16)
 
 
-def theory_kernel(flat_ref, theory_ref):
-    width = flat_ref.shape[2]
+def theory_of(bins, theory_ref):
+    width = bins.shape[1]
     high_place = iota((HIGH * 8, 2 * width), 0).astype(jnp.float32).astype(jnp.bfloat16)
     low_place = iota((LOW, 2 * width), 0).astype(jnp.float32).astype(jnp.bfloat16)
     one = jnp.ones((), F8)
     zero = jnp.zeros((), F8)
     member = iota((128, 128), 1) // 32 + 4 * (iota((128, 128), 0) % 2)
+    low = (bins & (LOW - 1)).astype(jnp.float32).astype(jnp.bfloat16)
+    high = ((bins >> 7) * 8 + member).astype(jnp.float32).astype(jnp.bfloat16)
+    for pair in range(32):
+        parts = []
+        for half in range(2):
+            row = 4 * pair + 2 * half
+            high_row = jnp.concatenate([high[row : row + 1], high[row + 1 : row + 2]], axis=1)
+            low_row = jnp.concatenate([low[row : row + 1], low[row + 1 : row + 2]], axis=1)
+            parts.append(
+                lax.dot_general(
+                    jnp.where(high_place == high_row, one, zero),
+                    jnp.where(low_place == low_row, one, zero),
+                    (((1,), (1,)), ((), ())),
+                    preferred_element_type=jnp.float32,
+                )
+            )
+        for part in range(HIGH):
+            tile = jnp.concatenate([item[part * 8 : part * 8 + 8] for item in parts], axis=0)
+            theory_ref[pair * 16 : pair * 16 + 16, part * LOW : (part + 1) * LOW] = tile.astype(
+                jnp.bfloat16
+            )
+
+
+def theory_kernel(flat_ref, theory_ref, held, sems):
+    steps = flat_ref.shape[0]
+
+    def copy_of(step):
+        return pltpu.make_async_copy(held.at[step], theory_ref.at[step], sems.at[step])
 
     def window(step, carry):
-        bins = flat_ref[step].astype(jnp.int32)
-        low = (bins & (LOW - 1)).astype(jnp.float32).astype(jnp.bfloat16)
-        high = ((bins >> 7) * 8 + member).astype(jnp.float32).astype(jnp.bfloat16)
-        for pair in range(32):
-            parts = []
-            for half in range(2):
-                row = 4 * pair + 2 * half
-                high_row = jnp.concatenate([high[row : row + 1], high[row + 1 : row + 2]], axis=1)
-                low_row = jnp.concatenate([low[row : row + 1], low[row + 1 : row + 2]], axis=1)
-                parts.append(
-                    lax.dot_general(
-                        jnp.where(high_place == high_row, one, zero),
-                        jnp.where(low_place == low_row, one, zero),
-                        (((1,), (1,)), ((), ())),
-                        preferred_element_type=jnp.float32,
-                    )
-                )
-            for part in range(HIGH):
-                tile = jnp.concatenate([item[part * 8 : part * 8 + 8] for item in parts], axis=0)
-                theory_ref[step, pair * 16 : pair * 16 + 16, part * LOW : (part + 1) * LOW] = (
-                    tile.astype(jnp.bfloat16)
-                )
+        theory_of(flat_ref[step].astype(jnp.int32), held.at[step])
+        copy_of(step).start()
         return carry
 
-    lax.fori_loop(0, flat_ref.shape[0], window, 0)
+    lax.fori_loop(0, steps, window, 0)
+    for step in range(steps):
+        copy_of(step).wait()
 
 
 def build_theory(flat, width):
     steps = flat.shape[0]
     return pl.pallas_call(
         theory_kernel,
-        out_shape=jax.ShapeDtypeStruct((steps, 512, width), jnp.bfloat16),
+        out_shape=pltpu.HBM((steps, 512, width), jnp.bfloat16),
         in_specs=[pl.BlockSpec(memory_space=VMEM)],
-        out_specs=pl.BlockSpec(memory_space=VMEM),
-        compiler_params=pltpu.CompilerParams(vmem_limit_bytes=16 << 20),
+        out_specs=pl.BlockSpec(memory_space=pltpu.HBM),
+        scratch_shapes=[
+            pltpu.VMEM((steps, 512, width), jnp.bfloat16),
+            pltpu.SemaphoreType.DMA((steps,)),
+        ],
+        compiler_params=pltpu.CompilerParams(vmem_limit_bytes=10 << 20),
         cost_estimate=pl.CostEstimate(
-            flops=3_000_000_000, bytes_accessed=6_400_000, transcendentals=0
+            flops=2_000_000_000, bytes_accessed=6_400_000, transcendentals=0
         ),
         name="theory",
     )(flat)
 
 
-def score_kernel(counts_ref, t0, t1, t2, t3, own_ref, other_ref, out_ref):
+def score_kernel(built, counts_ref, *refs):
+    theories = refs[:built]
+    flats = refs[built:4]
+    own_ref, other_ref, out_ref = refs[4:7]
+    scratch, (held, sems) = refs[7:-2], refs[-2:]
+    copies = [
+        pltpu.make_async_copy(theories[i].at[step], held.at[i, step], sems.at[i, step])
+        for step in range(theories[0].shape[0])
+        for i in range(built)
+    ]
+    for copy in copies:
+        copy.start()
     y = lax.axis_index("spec") // 2
     core = lax.axis_index("spec") % 2
     mass = lax.axis_index("mass")
-    steps = t0.shape[0]
+    steps = flats[0].shape[0]
     rows = own_ref.shape[0] * 2
     spectra = jnp.concatenate([own_ref[...], other_ref[...]], axis=0)
     slot = (iota((1, rows), 1) % SLOTS) // 2
     local = iota((512, 1), 0)
-    best = jnp.zeros((1, rows), jnp.float32)
-    total = jnp.zeros((1, rows), jnp.float32)
-    square = jnp.zeros((1, rows), jnp.float32)
-    for step in range(steps):
+
+    def window(step, carry):
+        best, total, square = carry
         live = counts_ref[mass * steps + step]
+        for flat, place in zip(flats, scratch):
+            theory_of(flat[step].astype(jnp.int32), place)
+        for i in range(built):
+            pltpu.make_async_copy(
+                theories[i].at[step], held.at[i, step], sems.at[i, step]
+            ).wait()
         now_best, now_total, now_square = [], [], []
-        for turn, theory in enumerate((t0, t1, t2, t3)):
+        tables = [held.at[i, step] for i in range(built)] + list(scratch)
+        for turn, theory in enumerate(tables):
             base = (((y + turn) % 4) * 2 + core) * 512
             scores = lax.dot_general(
-                theory[step],
+                theory[...],
                 spectra,
                 (((1,), (1,)), ((), ())),
                 preferred_element_type=jnp.float32,
             )
             valid = local < (live - base)
-            now_best.append(
-                jnp.max(jnp.where(valid, scores, -1e30), axis=0, keepdims=True)
-            )
+            now_best.append(jnp.max(jnp.where(valid, scores, -1e30), axis=0, keepdims=True))
             scores = jnp.where(valid, scores, 0.0)
             now_total.append(jnp.sum(scores, axis=0, keepdims=True))
             now_square.append(jnp.sum(scores * scores, axis=0, keepdims=True))
@@ -149,6 +201,10 @@
         best = jnp.where(here, functools.reduce(jnp.maximum, now_best), best)
         total = jnp.where(here, sum(now_total[1:], now_total[0]), total)
         square = jnp.where(here, sum(now_square[1:], now_square[0]), square)
+        return best, total, square
+
+    zeros = jnp.zeros((1, rows), jnp.float32)
+    best, total, square = lax.fori_loop(0, steps, window, (zeros, zeros, zeros))
     stats = jnp.concatenate(
         [best / 32.0, total / 32.0, square / 1024.0, jnp.zeros((5, rows), jnp.float32)], axis=0
     )
@@ -206,9 +262,6 @@
     total = halves[0][1:2] + halves[1][1:2]
     square = halves[0][2:3] + halves[1][2:3]
     column = counts_ref[...].astype(jnp.float32)
-    here = iota((entries, windows), 1)
-    live = jnp.zeros((1, entries), jnp.float32)
-    del here
     live = lax.dot_general(
         column,
         jnp.where(iota((windows, entries), 0) == flat, 1.0, 0.0),
@@ -233,21 +286,31 @@
     routes_t = routes.T
     vmem = pl.BlockSpec(memory_space=VMEM)
     smem = pl.BlockSpec(memory_space=SMEM)
+    hbm = pl.BlockSpec(memory_space=pltpu.HBM)
     outgoing, flat = pl.pallas_call(
         prepare_kernel,
         out_shape=(
             jax.ShapeDtypeStruct((mass_count * SLOTS, width), jnp.bfloat16),
             jax.ShapeDtypeStruct((steps, 128, 128), jnp.int16),
         ),
-        in_specs=[vmem] * 3,
+        in_specs=[hbm] * 3,
         out_specs=(vmem, vmem),
         scratch_shapes=[
+            pltpu.VMEM((rows, width), spectra.dtype),
+            pltpu.VMEM(routes_t.shape, routes_t.dtype),
+            pltpu.VMEM(pep_bins.shape, pep_bins.dtype),
             pltpu.VMEM((rows, width + 2 * PAD), jnp.bfloat16),
             pltpu.VMEM((512, 128), jnp.int32),
+            pltpu.SemaphoreType.DMA((3,)),
         ],
-        compiler_params=pltpu.CompilerParams(vmem_limit_bytes=16 << 20),
+        compiler_params=pltpu.CompilerParams(vmem_limit_bytes=8 << 20),
         name="prepare",
-    )(spectra, routes_t, pep_bins)
+    )(
+        *[
+            pltpu.with_memory_space_constraint(item, pltpu.HBM)
+            for item in (spectra, routes_t, pep_bins)
+        ]
+    )
     flats = [flat] + [
         lax.ppermute(
             flat, "spec", [((i + 2 * turn) % spec_count, i) for i in range(spec_count)]
@@ -255,16 +318,29 @@
         for turn in range(1, 4)
     ]
     own = lax.all_to_all(outgoing, "mass", split_axis=0, concat_axis=0, tiled=True)
+    first = build_theory(flats[0], width)
+    own, first, flats = lax.optimization_barrier((own, first, flats))
     other = lax.ppermute(own, "spec", [(i, i ^ 1) for i in range(spec_count)])
-    theories = [build_theory(item, width) for item in flats]
+    theories = [first] + [build_theory(item, width) for item in flats[1:BUILT]]
     stats = pl.pallas_call(
-        score_kernel,
+        functools.partial(score_kernel, BUILT),
         out_shape=jax.ShapeDtypeStruct((2 * mass_count * 8, 128), jnp.float32),
-        in_specs=[smem] + [vmem] * 6,
+        in_specs=[smem] + [hbm] * BUILT + [vmem] * (6 - BUILT),
         out_specs=vmem,
-        compiler_params=pltpu.CompilerParams(vmem_limit_bytes=48 << 20),
+        scratch_shapes=[pltpu.VMEM((512, width), jnp.bfloat16)] * (4 - BUILT)
+        + [
+            pltpu.VMEM((BUILT, steps, 512, width), jnp.bfloat16),
+            pltpu.SemaphoreType.DMA((BUILT, steps)),
+        ],
+        compiler_params=pltpu.CompilerParams(vmem_limit_bytes=32 << 20),
         name="score",
-    )(counts, *theories, own, other)
+    )(
+        counts,
+        *[pltpu.with_memory_space_constraint(item, pltpu.HBM) for item in theories],
+        *flats[BUILT:],
+        own,
+        other,
+    )
     groups = [
         [(y * 2 + core) * mass_count + m for core in range(2) for m in range(mass_count)]
         for y in range(spec_count // 2)

time: 72.6 us -> 56.8 us (0.78)
  local copies, waits for them, and re-layouts: 13 us -> 0.01 us
  Pallas kernels: 28.6 us -> 25.6 us
  waiting for transfers between devices: 0.58 us -> 1.99 us
  blocking collectives: 13.5 us -> 12.7 us
    unnamed x16 -> x2, local copies, waits for them, and re-layouts: 13 us -> 0.01 us
    pallas_call x5 -> x3, Pallas kernels: 23.9 us -> 20 us  [the longest x1 13.2 us: per_device(): pl.pallas_call(functools.partial(score_kernel, BUILT), out_shape=jax.Shap...]
    all_to_all x1, waiting for transfers between devices: 0.57 us -> 1.98 us  [per_device(): lax.all_to_all(outgoing, 'mass', split_axis=0, concat_axis=0, tiled=True)]
    pallas_call x1, Pallas kernels: 2.6 us -> 3.52 us  [per_device(): pl.pallas_call(prepare_kernel, out_shape=(jax.ShapeDtypeStruct((mass_coun...]
    all_to_all x1, starting transfers between devices: 7.6 us -> 8.44 us  [per_device(): lax.all_to_all(outgoing, 'mass', split_axis=0, concat_axis=0, tiled=True)]
    ppermute x3, starting transfers between devices: 5.82 us -> 5.06 us  [per_device(): lax.ppermute(flat, 'spec', [((i + 2 * turn) % spec_count, i) for i in ran...]
  transfers between devices with their start and end apart: 5 -> 5, of which waited for: 1 -> 1; matrix products, arithmetic and copies ran while one was open for 0% -> 0% of each run, Pallas kernels for 11% -> 12%
where the time goes in v2:
time: 56.8 us; the launch traced here: 56.5 us
  Pallas kernels  25.6 us (45%)
  starting transfers between devices  15.5 us (27%)
  blocking collectives  12.7 us (22%)
  waiting for transfers between devices  1.99 us (4%)
  between operations  0.72 us (1%)
    pallas_call x1, Pallas kernels, per_device(): pl.pallas_call(functools.partial(score_kernel, BUILT), out_shape=jax.Shap...  13.2 us
    all_to_all x1, blocking collectives, per_device(): lax.all_to_all(stats, ('spec', 'mass'), split_axis=0, concat_axis=0, tile...  12.7 us
    all_to_all x1, starting transfers between devices, per_device(): lax.all_to_all(outgoing, 'mass', split_axis=0, concat_axis=0, tiled=True)  8.44 us
    pallas_call x2, Pallas kernels, build_theory(): pl.pallas_call(theory_kernel, out_shape=pltpu.HBM((steps, 512, width), jn...  6.8 us
    ppermute x3, starting transfers between devices, per_device(): lax.ppermute(flat, 'spec', [((i + 2 * turn) % spec_count, i) for i in ran...  5.06 us
    pallas_call x1, Pallas kernels, per_device(): pl.pallas_call(prepare_kernel, out_shape=(jax.ShapeDtypeStruct((mass_coun...  3.52 us
    pallas_call x1, Pallas kernels, per_device(): pl.pallas_call(finish_kernel, out_shape=(jax.ShapeDtypeStruct((2, rows),...  2.09 us
    all_to_all x1, waiting for transfers between devices, per_device(): lax.all_to_all(outgoing, 'mass', split_axis=0, concat_axis=0, tiled=True)  1.98 us
  transfers between devices with their start and end apart: 5, of which 1 were waited for; matrix products, arithmetic and copies ran while one was open for 0% of the time, Pallas kernels for 12%

profile of v2, /device:TPU:1, one launch (start us, length us, event | category | flops | bytes accessed | tf_op | source)
XLA Modules:
  0.0 56.5 jit_solution(7629757593268854792)
XLA Ops:
  0.6 3.5 %prepare.1 = (bf16[128,2048]{1,0:T(8,128)(2,1)}, s16[3,128,128]{2,1,0:T(8,128)(2,1)S(1)}) custom-call(bf16[32,2048]{1,0:T(8,128)(2,1)} %spectra_hbm.1, s32[2,32]{1,0:T(2,128)} %bitcast.13, s32[3,32,512]{2,1,0:T(8,128)} %pep_hbm.1), custom_call_target="tpu_custom_call" | custom-call | tf_op jit(solution)/shard_map/prepare/pallas_call | solution.py:290
  4.2 8.4 %all-to-all-start = ((bf16[16,8,2048]{2,1,0:T(8,128)(2,1)}), bf16[16,8,2048]{2,1,0:T(8,128)(2,1)S(1)}, u32[]{:S(2)}, u32[]{:S(2)}) async-start(bf16[16,8,2048]{2,1,0:T(8,128)(2,1)} %bitcast.2), calls=%async_computation | async-start | bytes 1048576 | tf_op jit(solution)/shard_map/all_to_all | solution.py:320
  12.6 0.0 copy-start
  12.6 1.4 %collective-permute-start.2 = (s16[3,128,128]{2,1,0:T(8,128)(2,1)S(1)}, s16[3,128,128]{2,1,0:T(8,128)(2,1)S(1)}, u32[]{:S(2)}, u32[]{:S(2)}) collective-permute-start(s16[3,128,128]{2,1,0:T(8,128)(2,1)S(1)} %get-tuple-element.12.flat_ref), channel_id=1, source_target_pairs={{96,0},{112,16},{0,32},{16,48},{32,64},{48,80},{64,96},{80,112},{9... | collective-permute-start | bytes 294920 | tf_op jit(solution)/shard_map/ppermute | solution.py:315
  14.0 2.6 %collective-permute-start.1 = (s16[3,128,128]{2,1,0:T(8,128)(2,1)S(1)}, s16[3,128,128]{2,1,0:T(8,128)(2,1)S(1)}, u32[]{:S(2)}, u32[]{:S(2)}) collective-permute-start(s16[3,128,128]{2,1,0:T(8,128)(2,1)S(1)} %get-tuple-element.12.flat_ref), channel_id=1, source_target_pairs={{64,0},{80,16},{96,32},{112,48},{0,64},{16,80},{32,96},{48,112},{6... | collective-permute-start | bytes 294920 | tf_op jit(solution)/shard_map/ppermute | solution.py:315
  16.6 1.1 %collective-permute-start = (s16[3,128,128]{2,1,0:T(8,128)(2,1)S(1)}, s16[3,128,128]{2,1,0:T(8,128)(2,1)S(1)}, u32[]{:S(2)}, u32[]{:S(2)}) collective-permute-start(s16[3,128,128]{2,1,0:T(8,128)(2,1)S(1)} %get-tuple-element.12.flat_ref), channel_id=1, source_target_pairs={{32,0},{48,16},{64,32},{80,48},{96,64},{112,80},{0,96},{16,112},{3... | collective-permute-start | bytes 294920 | tf_op jit(solution)/shard_map/ppermute | solution.py:315
  17.7 3.4 %theory.2.refs_0_ = bf16[3,512,2048]{2,1,0:T(8,128)(2,1)} custom-call(s16[3,128,128]{2,1,0:T(8,128)(2,1)S(1)} %get-tuple-element.12.flat_ref), custom_call_target="tpu_custom_call" | custom-call | flops 2000000000 | bytes 6400000 | tf_op jit(solution)/shard_map/theory/pallas_call | solution.py:138
  21.1 0.0 collective-permute-done.2.refs_3_
  21.1 0.0 collective-permute-done.1.refs_2_
  21.1 0.0 collective-permute-done.flat_ref
  21.1 2.0 %all-to-all-done = bf16[16,8,2048]{2,1,0:T(8,128)(2,1)S(1)} async-done(((bf16[16,8,2048]{2,1,0:T(8,128)(2,1)}), bf16[16,8,2048]{2,1,0:T(8,128)(2,1)S(1)}, u32[]{:S(2)}, u32[]{:S(2)}) %all-to-all-start) | async-done | bytes 524320 | tf_op jit(solution)/shard_map/all_to_all | solution.py:320
  23.1 2.0 %collective-permute-start.3 = (bf16[128,2048]{1,0:T(8,128)(2,1)S(1)}, bf16[128,2048]{1,0:T(8,128)(2,1)S(1)}, u32[]{:S(2)}, u32[]{:S(2)}) collective-permute-start(bf16[128,2048]{1,0:T(8,128)(2,1)S(1)} %bitcast.8), channel_id=1, source_target_pairs={{0,16},{16,0},{32,48},{48,32},{64,80},{80,64},{96,112},{112,96},{1... | collective-permute-start | bytes 1572872 | tf_op jit(solution)/shard_map/ppermute | solution.py:323
  25.1 3.4 %theory.3.refs_1_ = bf16[3,512,2048]{2,1,0:T(8,128)(2,1)} custom-call(s16[3,128,128]{2,1,0:T(8,128)(2,1)S(1)} %collective-permute-done.flat_ref), custom_call_target="tpu_custom_call" | custom-call | flops 2000000000 | bytes 6400000 | tf_op jit(solution)/shard_map/theory/pallas_call | solution.py:138
  28.5 0.0 collective-permute-done.3.refs_5_
  28.5 0.0 copy-done
  28.5 13.2 %score.1 = f32[256,128]{1,0:T(8,128)S(1)} custom-call(s32[48]{0:T(128)S(1)} %copy-done, bf16[3,512,2048]{2,1,0:T(8,128)(2,1)} %theory.2.refs_0_, bf16[3,512,2048]{2,1,0:T(8,128)(2,1)} %theory.3.refs_1_, s16[3,128,128]{2,1,0:T(8,128)(2,1)S(1)} %collective-permute-done.1.refs_2_, s16[3,128,128]{2,1,0:T(8,128)(2,1)S(1)} %collective-permute-done.2.refs_3_, ...), custom_call_target="tpu_custom_call" | custom-call | tf_op jit(solution)/shard_map/score/pallas_call | solution.py:325
  41.7 12.7 %all_to_all.23 = f32[32,8,128]{2,1,0:T(8,128)} all-to-all(f32[32,8,128]{2,1,0:T(8,128)S(1)} %bitcast.10), channel_id=1, replica_groups={{0,1,2,3,4,5,6,7,8,9,10,11,12,13,14,15,16,17,18,19,20,21,22,23,24,25,26..., dimensions={0} | all-to-all | bytes 262144 | tf_op jit(solution)/shard_map/all_to_all | solution.py:348
  54.5 2.1 %finish.1 = (f32[2,32]{1,0:T(2,128)}, f32[2,32]{1,0:T(2,128)}) custom-call(s32[1,48]{1,0:T(1,128)} %bitcast.11, s32[2,32]{1,0:T(2,128)} %bitcast.14, f32[256,128]{1,0:T(8,128)} %bitcast.12), custom_call_target="tpu_custom_call" | custom-call | tf_op jit(solution)/shard_map/finish/pallas_call | solution.py:356
Async XLA Ops:
  4.2 19.0 %all-to-all-start = ((bf16[16,8,2048]{2,1,0:T(8,128)(2,1)}), bf16[16,8,2048]{2,1,0:T(8,128)(2,1)S(1)}, u32[]{:S(2)}, u32[]{:S(2)}) async-start(bf16[16,8,2048]{2,1,0:T(8,128)(2,1)} %bitcast.2), calls=%async_computation | async-start | bytes 1048576 | tf_op jit(solution)/shard_map/all_to_all | solution.py:320
  12.6 15.9 %copy-start = (s32[48]{0:T(128)S(1)}, s32[48]{0:T(128)}, u32[]{:S(2)}) copy-start(s32[48]{0:T(128)} %counts_ref.1) | copy-start | bytes 580
  12.6 8.5 %collective-permute-start.2 = (s16[3,128,128]{2,1,0:T(8,128)(2,1)S(1)}, s16[3,128,128]{2,1,0:T(8,128)(2,1)S(1)}, u32[]{:S(2)}, u32[]{:S(2)}) collective-permute-start(s16[3,128,128]{2,1,0:T(8,128)(2,1)S(1)} %get-tuple-element.12.flat_ref), channel_id=1, source_target_pairs={{96,0},{112,16},{0,32},{16,48},{32,64},{48,80},{64,96},{80,112},{9... | collective-permute-start | bytes 294920 | tf_op jit(solution)/shard_map/ppermute | solution.py:315
  14.0 7.1 %collective-permute-start.1 = (s16[3,128,128]{2,1,0:T(8,128)(2,1)S(1)}, s16[3,128,128]{2,1,0:T(8,128)(2,1)S(1)}, u32[]{:S(2)}, u32[]{:S(2)}) collective-permute-start(s16[3,128,128]{2,1,0:T(8,128)(2,1)S(1)} %get-tuple-element.12.flat_ref), channel_id=1, source_target_pairs={{64,0},{80,16},{96,32},{112,48},{0,64},{16,80},{32,96},{48,112},{6... | collective-permute-start | bytes 294920 | tf_op jit(solution)/shard_map/ppermute | solution.py:315
  16.6 4.5 %collective-permute-start = (s16[3,128,128]{2,1,0:T(8,128)(2,1)S(1)}, s16[3,128,128]{2,1,0:T(8,128)(2,1)S(1)}, u32[]{:S(2)}, u32[]{:S(2)}) collective-permute-start(s16[3,128,128]{2,1,0:T(8,128)(2,1)S(1)} %get-tuple-element.12.flat_ref), channel_id=1, source_target_pairs={{32,0},{48,16},{64,32},{80,48},{96,64},{112,80},{0,96},{16,112},{3... | collective-permute-start | bytes 294920 | tf_op jit(solution)/shard_map/ppermute | solution.py:315
  23.1 5.4 %collective-permute-start.3 = (bf16[128,2048]{1,0:T(8,128)(2,1)S(1)}, bf16[128,2048]{1,0:T(8,128)(2,1)S(1)}, u32[]{:S(2)}, u32[]{:S(2)}) collective-permute-start(bf16[128,2048]{1,0:T(8,128)(2,1)S(1)} %bitcast.8), channel_id=1, source_target_pairs={{0,16},{16,0},{32,48},{48,32},{64,80},{80,64},{96,112},{112,96},{1... | collective-permute-start | bytes 1572872 | tf_op jit(solution)/shard_map/ppermute | solution.py:323

commit v3 on v2

v3 whole, which is shorter than its diff:
```python
import functools

import jax
import jax.numpy as jnp
from jax import lax
from jax.experimental import pallas as pl
from jax.experimental.pallas import tpu as pltpu
from jax.sharding import PartitionSpec as P

LAG = 75
EPS = 1e-06
PAD = 128
SLOTS = 8
LOW = 128
HIGH = 16
F8 = jnp.float8_e4m3fn
VMEM = pltpu.VMEM
SMEM = pltpu.SMEM


def iota(shape, axis):
    return lax.broadcasted_iota(jnp.int32, shape, axis)


def prepare_kernel(
    spectra_hbm,
    routes_hbm,
    pep_hbm,
    counts_hbm,
    out_hbm,
    flat_ref,
    where_hbm,
    out_ref,
    where_ref,
    counts_ref,
    spectra_ref,
    routes_ref,
    pep_ref,
    padded,
    turned,
    sems,
):
    copies = [
        pltpu.make_async_copy(spectra_hbm, spectra_ref, sems.at[0]),
        pltpu.make_async_copy(routes_hbm, routes_ref, sems.at[1]),
        pltpu.make_async_copy(pep_hbm, pep_ref, sems.at[2]),
        pltpu.make_async_copy(counts_hbm, counts_ref, sems.at[3]),
    ]
    for copy in copies:
        copy.start()
    rows, width = spectra_ref.shape
    block = 256
    gap = jnp.abs(iota((block + 2 * PAD, block), 0) - PAD - iota((block + 2 * PAD, block), 1))
    band = jnp.where((gap > 0) & (gap <= LAG), 1.0, 0.0).astype(jnp.bfloat16)
    copies[0].wait()
    rooted = jnp.sqrt(spectra_ref[...].astype(jnp.float32)).astype(jnp.bfloat16)
    padded[:, :PAD] = jnp.zeros((rows, PAD), jnp.bfloat16)
    padded[:, PAD + width :] = jnp.zeros((rows, PAD), jnp.bfloat16)
    padded[:, PAD : PAD + width] = rooted
    copies[1].wait()
    place = iota((out_ref.shape[0], rows), 0)
    inner = place % SLOTS
    window = (place // SLOTS) * 3 + inner // 2
    named = (routes_ref[0:1, :] == window) | (routes_ref[1:2, :] == window)
    named = named & (inner < 6)
    before = jnp.where(iota((rows, rows), 0) < iota((rows, rows), 1), 1.0, 0.0)
    earlier = jnp.dot(
        jnp.where(named, 1.0, 0.0).astype(jnp.bfloat16),
        before.astype(jnp.bfloat16),
        preferred_element_type=jnp.float32,
    )
    taken = named & (earlier == (inner % 2).astype(jnp.float32))
    routing = jnp.where(taken, 1.0, 0.0).astype(jnp.bfloat16)
    leaving = []
    for start in range(0, width, block):
        background = jnp.dot(
            padded[:, start : start + block + 2 * PAD], band, preferred_element_type=jnp.float32
        )
        values = rooted[:, start : start + block].astype(jnp.float32)
        prepared = (values - background / (2.0 * LAG)).astype(jnp.bfloat16)
        out_ref[:, start : start + block] = jnp.dot(
            routing, prepared, preferred_element_type=jnp.float32
        ).astype(jnp.bfloat16)
        columns = pl.ds(start, block)
        leaving.append(
            pltpu.make_async_copy(
                out_ref.at[:, columns], out_hbm.at[:, columns], sems.at[5 + start // block]
            )
        )
        leaving[-1].start()
    copies[3].wait()
    mass = lax.axis_index("mass")
    windows = counts_ref.shape[0]
    counted = jnp.zeros((windows, rows), jnp.int32)
    at_window = iota((windows, rows), 0)
    for index in range(windows):
        counted = jnp.where(at_window == index, counts_ref[index], counted)
    where_ref[...] = jnp.zeros_like(where_ref)
    for pick in range(2):
        here = routes_ref[pick : pick + 1, :]
        mine = taken & (window == here)
        found = jnp.sum(jnp.where(mine, place, 0), axis=0, keepdims=True)
        lanes = slice(pick * rows, (pick + 1) * rows)
        where_ref[0:1, lanes] = mass * SLOTS + found % SLOTS
        where_ref[1:2, lanes] = found // SLOTS
        where_ref[2:3, lanes] = jnp.sum(
            jnp.where(at_window == here, counted, 0), axis=0, keepdims=True
        )
    leaving.append(pltpu.make_async_copy(where_ref, where_hbm, sems.at[4]))
    leaving[-1].start()
    copies[2].wait()
    lane = iota((128, 128), 1) // 32
    for step in range(pep_ref.shape[0]):
        table = pep_ref[step]
        turned[...] = jnp.concatenate([table] * 4, axis=0).T
        flat = jnp.zeros((128, 128), jnp.int32)
        for part in range(4):
            flat = jnp.where(lane == part, turned[pl.ds(part, 128, stride=4), :], flat)
        flat_ref[step] = flat.astype(jnp.int16)
    for copy in leaving:
        copy.wait()


def theory_of(bins, theory_ref, finished=None):
    width = bins.shape[1]
    high_place = iota((HIGH * 8, 2 * width), 0).astype(jnp.float32).astype(jnp.bfloat16)
    low_place = iota((LOW, 2 * width), 0).astype(jnp.float32).astype(jnp.bfloat16)
    one = jnp.ones((), F8)
    zero = jnp.zeros((), F8)
    member = iota((128, 128), 1) // 32 + 4 * (iota((128, 128), 0) % 2)
    low = (bins & (LOW - 1)).astype(jnp.float32).astype(jnp.bfloat16)
    high = ((bins >> 7) * 8 + member).astype(jnp.float32).astype(jnp.bfloat16)
    for pair in range(32):
        parts = []
        for half in range(2):
            row = 4 * pair + 2 * half
            high_row = jnp.concatenate([high[row : row + 1], high[row + 1 : row + 2]], axis=1)
            low_row = jnp.concatenate([low[row : row + 1], low[row + 1 : row + 2]], axis=1)
            parts.append(
                lax.dot_general(
                    jnp.where(high_place == high_row, one, zero),
                    jnp.where(low_place == low_row, one, zero),
                    (((1,), (1,)), ((), ())),
                    preferred_element_type=jnp.float32,
                )
            )
        for part in range(HIGH):
            tile = jnp.concatenate([item[part * 8 : part * 8 + 8] for item in parts], axis=0)
            theory_ref[pair * 16 : pair * 16 + 16, part * LOW : (part + 1) * LOW] = tile.astype(
                jnp.bfloat16
            )
        if finished is not None and pair % 8 == 7:
            finished(pair // 8)


def theory_kernel(flat_ref, theory_ref):
    def window(step, carry):
        theory_of(flat_ref[step].astype(jnp.int32), theory_ref.at[step])
        return carry

    lax.fori_loop(0, flat_ref.shape[0], window, 0)


def stored_theory_kernel(flat_ref, theory_ref, held, sems):
    steps = flat_ref.shape[0]

    def copy_of(step, quarter):
        rows = pl.ds(quarter * 128, 128)
        return pltpu.make_async_copy(
            held.at[step, rows], theory_ref.at[step, rows], sems.at[step, quarter]
        )

    def window(step, carry):
        theory_of(
            flat_ref[step].astype(jnp.int32),
            held.at[step],
            lambda quarter: copy_of(step, quarter).start(),
        )
        return carry

    lax.fori_loop(0, steps, window, 0)
    for step in range(steps):
        for quarter in range(4):
            copy_of(step, quarter).wait()


def build_theory(flat, width, stored):
    steps = flat.shape[0]
    shape = (steps, 512, width)
    space = pltpu.HBM if stored else VMEM
    scratch = [pltpu.VMEM(shape, jnp.bfloat16), pltpu.SemaphoreType.DMA((steps, 4))]
    return pl.pallas_call(
        stored_theory_kernel if stored else theory_kernel,
        out_shape=space(shape, jnp.bfloat16),
        in_specs=[pl.BlockSpec(memory_space=VMEM)],
        out_specs=pl.BlockSpec(memory_space=space),
        scratch_shapes=scratch if stored else [],
        compiler_params=pltpu.CompilerParams(vmem_limit_bytes=(10 if stored else 4) << 20),
        cost_estimate=pl.CostEstimate(
            flops=2_000_000_000, bytes_accessed=6_400_000, transcendentals=0
        ),
        name="theory",
    )(flat)


def score_kernel(
    counts_ref,
    stored_ref,
    theory_ref,
    flat2_ref,
    flat3_ref,
    own_ref,
    other_ref,
    out_ref,
    held,
    built2,
    built3,
    sems,
):
    steps = theory_ref.shape[0]

    def copy_of(step):
        return pltpu.make_async_copy(stored_ref.at[step], held.at[step], sems.at[step])

    for step in range(steps):
        copy_of(step).start()
    y = lax.axis_index("spec") // 2
    core = lax.axis_index("spec") % 2
    mass = lax.axis_index("mass")
    rows = own_ref.shape[0] * 2
    spectra = jnp.concatenate([own_ref[...], other_ref[...]], axis=0)
    slot = (iota((1, rows), 1) % SLOTS) // 2
    local = iota((512, 1), 0)

    def window(step, carry):
        best, total, square = carry
        live = counts_ref[mass * steps + step]
        theory_of(flat2_ref[step].astype(jnp.int32), built2)
        theory_of(flat3_ref[step].astype(jnp.int32), built3)
        copy_of(step).wait()
        now_best, now_total, now_square = [], [], []
        tables = [held.at[step], theory_ref.at[step], built2, built3]
        for turn, theory in enumerate(tables):
            base = (((y + turn) % 4) * 2 + core) * 512
            scores = lax.dot_general(
                theory[...],
                spectra,
                (((1,), (1,)), ((), ())),
                preferred_element_type=jnp.float32,
            )
            valid = local < (live - base)
            now_best.append(jnp.max(jnp.where(valid, scores, -1e30), axis=0, keepdims=True))
            scores = jnp.where(valid, scores, 0.0)
            now_total.append(jnp.sum(scores, axis=0, keepdims=True))
            now_square.append(jnp.sum(scores * scores, axis=0, keepdims=True))
        here = slot == step
        best = jnp.where(here, functools.reduce(jnp.maximum, now_best), best)
        total = jnp.where(here, sum(now_total[1:], now_total[0]), total)
        square = jnp.where(here, sum(now_square[1:], now_square[0]), square)
        return best, total, square

    zeros = jnp.zeros((1, rows), jnp.float32)
    best, total, square = lax.fori_loop(0, steps, window, (zeros, zeros, zeros))
    stats = jnp.concatenate(
        [best / 32.0, total / 32.0, square / 1024.0, jnp.zeros((5, rows), jnp.float32)], axis=0
    )
    own, other = stats[:, : rows // 2], stats[:, rows // 2 :]
    first = jnp.where(core == 0, own, other)
    second = jnp.where(core == 0, other, own)
    peers = out_ref.shape[0] // 16
    for peer in range(peers):
        out_ref[peer * 8 : peer * 8 + 8, :] = first
        out_ref[(peers + peer) * 8 : (peers + peer) * 8 + 8, :] = second


def finish_kernel(where_hbm, stats_hbm, best_ref, z_ref, where_ref, stats_ref, sems):
    copies = [
        pltpu.make_async_copy(stats_hbm, stats_ref, sems.at[0]),
        pltpu.make_async_copy(where_hbm, where_ref, sems.at[1]),
    ]
    for copy in copies:
        copy.start()
    for copy in copies:
        copy.wait()
    rows = best_ref.shape[1]
    peers = stats_ref.shape[0] // 16
    lane = jnp.broadcast_to(where_ref[0:1, :], (8, 128))
    shard = where_ref[1:2, :]
    live = where_ref[2:3, :].astype(jnp.float32)
    halves = []
    for half in range(2):
        chosen = jnp.zeros((8, 128), jnp.float32)
        for peer in range(peers):
            at = (half * peers + peer) * 8
            found = jnp.take_along_axis(stats_ref[at : at + 8, :], lane, axis=1)
            chosen = jnp.where(shard == peer, found, chosen)
        halves.append(chosen)
    best = jnp.maximum(halves[0][0:1], halves[1][0:1])
    total = halves[0][1:2] + halves[1][1:2]
    square = halves[0][2:3] + halves[1][2:3]
    mean = total / live
    spread = square / live - mean * mean
    z = (best - mean) / jnp.sqrt(spread + EPS)
    best_ref[0:1, :] = best[:, :rows]
    best_ref[1:2, :] = best[:, rows : 2 * rows]
    z_ref[0:1, :] = z[:, :rows]
    z_ref[1:2, :] = z[:, rows : 2 * rows]


def per_device(spectra, routes, pep_bins, counts):
    rows, width = spectra.shape
    mass_count = lax.axis_size("mass")
    spec_count = lax.axis_size("spec")
    steps = pep_bins.shape[0]
    routes_t = routes.T
    vmem = pl.BlockSpec(memory_space=VMEM)
    smem = pl.BlockSpec(memory_space=SMEM)
    hbm = pl.BlockSpec(memory_space=pltpu.HBM)
    outgoing, flat, where = pl.pallas_call(
        prepare_kernel,
        out_shape=(
            pltpu.HBM((mass_count * SLOTS, width), jnp.bfloat16),
            jax.ShapeDtypeStruct((steps, 128, 128), jnp.int16),
            pltpu.HBM((8, 128), jnp.int32),
        ),
        in_specs=[hbm] * 4,
        out_specs=(hbm, vmem, hbm),
        scratch_shapes=[
            pltpu.VMEM((mass_count * SLOTS, width), jnp.bfloat16),
            pltpu.VMEM((8, 128), jnp.int32),
            pltpu.SMEM(counts.shape, counts.dtype),
            pltpu.VMEM((rows, width), spectra.dtype),
            pltpu.VMEM(routes_t.shape, routes_t.dtype),
            pltpu.VMEM(pep_bins.shape, pep_bins.dtype),
            pltpu.VMEM((rows, width + 2 * PAD), jnp.bfloat16),
            pltpu.VMEM((512, 128), jnp.int32),
            pltpu.SemaphoreType.DMA((5 + width // 256,)),
        ],
        compiler_params=pltpu.CompilerParams(vmem_limit_bytes=8 << 20),
        name="prepare",
    )(
        *[
            pltpu.with_memory_space_constraint(item, pltpu.HBM)
            for item in (spectra, routes_t, pep_bins, counts)
        ]
    )
    flats = [flat] + [
        lax.ppermute(
            flat, "spec", [((i + 2 * turn) % spec_count, i) for i in range(spec_count)]
        )
        for turn in range(1, 4)
    ]
    own = lax.all_to_all(outgoing, "mass", split_axis=0, concat_axis=0, tiled=True)
    first = build_theory(flats[0], width, True)
    own, first, flats = lax.optimization_barrier((own, first, flats))
    other = lax.ppermute(own, "spec", [(i, i ^ 1) for i in range(spec_count)])
    second = build_theory(flats[1], width, False)
    stats = pl.pallas_call(
        score_kernel,
        out_shape=jax.ShapeDtypeStruct((2 * mass_count * 8, 128), jnp.float32),
        in_specs=[smem, hbm] + [vmem] * 5,
        out_specs=vmem,
        scratch_shapes=[
            pltpu.VMEM((steps, 512, width), jnp.bfloat16),
            pltpu.VMEM((512, width), jnp.bfloat16),
            pltpu.VMEM((512, width), jnp.bfloat16),
            pltpu.SemaphoreType.DMA((steps,)),
        ],
        compiler_params=pltpu.CompilerParams(vmem_limit_bytes=24 << 20),
        name="score",
    )(
        counts,
        pltpu.with_memory_space_constraint(first, pltpu.HBM),
        second,
        flats[2],
        flats[3],
        own,
        other,
    )
    groups = [
        [(y * 2 + core) * mass_count + m for core in range(2) for m in range(mass_count)]
        for y in range(spec_count // 2)
    ]
    back = lax.all_to_all(
        stats,
        ("spec", "mass"),
        split_axis=0,
        concat_axis=0,
        tiled=True,
        axis_index_groups=groups,
    )
    best, z = pl.pallas_call(
        finish_kernel,
        out_shape=(jax.ShapeDtypeStruct((2, rows), jnp.float32),) * 2,
        in_specs=[hbm] * 2,
        out_specs=(vmem, vmem),
        scratch_shapes=[
            pltpu.VMEM((8, 128), jnp.int32),
            pltpu.VMEM(back.shape, jnp.float32),
            pltpu.SemaphoreType.DMA((2,)),
        ],
        name="finish",
    )(*[pltpu.with_memory_space_constraint(item, pltpu.HBM) for item in (where, back)])
    return best.T, z.T


def solution(mesh):
    return jax.shard_map(
        per_device,
        mesh=mesh,
        in_specs=(
            P(("spec", "mass"), None),
            P(("spec", "mass"), None),
            P("mass", None, "spec"),
            P(),
        ),
        out_specs=(P(("spec", "mass"), None), P(("spec", "mass"), None)),
        check_vma=False,
    )
```

time: 56.8 us -> 54.1 us (0.952)
  Pallas kernels: 25.6 us -> 22.9 us
    pallas_call x4, Pallas kernels: 23.5 us -> 21.2 us  [the longest x1 12.5 us: per_device(): pl.pallas_call(score_kernel, out_shape=jax.ShapeDtypeStruct((2 * mass_cou...]
  transfers between devices with their start and end apart: 5 -> 5, of which waited for: 1 -> 2; matrix products, arithmetic and copies ran while one was open for 0% -> 0% of each run, Pallas kernels for 12% -> 10%
where the time goes in v3:
time: 54.1 us; the launch traced here: 53.9 us
  Pallas kernels  22.9 us (42%)
  starting transfers between devices  15.5 us (29%)
  blocking collectives  12.5 us (23%)
  waiting for transfers between devices  2.32 us (4%)
  between operations  0.71 us (1%)
    pallas_call x1, Pallas kernels, per_device(): pl.pallas_call(score_kernel, out_shape=jax.ShapeDtypeStruct((2 * mass_cou...  12.5 us
    all_to_all x1, blocking collectives, per_device(): lax.all_to_all(stats, ('spec', 'mass'), split_axis=0, concat_axis=0, tile...  12.5 us
    all_to_all x1, starting transfers between devices, per_device(): lax.all_to_all(outgoing, 'mass', split_axis=0, concat_axis=0, tiled=True)  8.44 us
    pallas_call x2, Pallas kernels, build_theory(): pl.pallas_call(stored_theory_kernel if stored else theory_kernel, out_sha...  5.12 us
    ppermute x3, starting transfers between devices, per_device(): lax.ppermute(flat, 'spec', [((i + 2 * turn) % spec_count, i) for i in ran...  5.06 us
    pallas_call x1, Pallas kernels, per_device(): pl.pallas_call(prepare_kernel, out_shape=(pltpu.HBM((mass_count * SLOTS,...  3.52 us
    all_to_all x1, waiting for transfers between devices, per_device(): lax.all_to_all(outgoing, 'mass', split_axis=0, concat_axis=0, tiled=True)  2.13 us
    ppermute x1, starting transfers between devices, per_device(): other = lax.ppermute(own, 'spec', [(i, i ^ 1) for i in range(spec_count)])  1.98 us
  transfers between devices with their start and end apart: 5, of which 2 were waited for; matrix products, arithmetic and copies ran while one was open for 0% of the time, Pallas kernels for 10%

profile of v3, /device:TPU:1, one launch (start us, length us, event | category | flops | bytes accessed | tf_op | source)
XLA Modules:
  0.0 53.9 jit_solution(15307084060695839462)
XLA Ops:
  0.6 3.5 %prepare.1 = (bf16[128,2048]{1,0:T(8,128)(2,1)}, s16[3,128,128]{2,1,0:T(8,128)(2,1)S(1)}, s32[8,128]{1,0:T(8,128)}) custom-call(bf16[32,2048]{1,0:T(8,128)(2,1)} %spectra_hbm.1, s32[2,32]{1,0:T(2,128)} %bitcast.12, s32[3,32,512]{2,1,0:T(8,128)} %pep_hbm.1, s32[48]{0:T(128)} %counts_ref.1), custom_call_target="tpu_custom_call" | custom-call | tf_op jit(solution)/shard_map/prepare/pallas_call | solution.py:319
  4.2 8.4 %all-to-all-start = ((bf16[16,8,2048]{2,1,0:T(8,128)(2,1)}), bf16[16,8,2048]{2,1,0:T(8,128)(2,1)S(1)}, u32[]{:S(2)}, u32[]{:S(2)}) async-start(bf16[16,8,2048]{2,1,0:T(8,128)(2,1)} %bitcast.10), calls=%async_computation | async-start | bytes 1048576 | tf_op jit(solution)/shard_map/all_to_all | solution.py:353
  12.6 0.0 copy-start
  12.6 1.4 %collective-permute-start.2 = (s16[3,128,128]{2,1,0:T(8,128)(2,1)S(1)}, s16[3,128,128]{2,1,0:T(8,128)(2,1)S(1)}, u32[]{:S(2)}, u32[]{:S(2)}) collective-permute-start(s16[3,128,128]{2,1,0:T(8,128)(2,1)S(1)} %get-tuple-element.14.flat_ref), channel_id=1, source_target_pairs={{96,0},{112,16},{0,32},{16,48},{32,64},{48,80},{64,96},{80,112},{9... | collective-permute-start | bytes 294920 | tf_op jit(solution)/shard_map/ppermute | solution.py:348
  14.0 2.6 %collective-permute-start.1 = (s16[3,128,128]{2,1,0:T(8,128)(2,1)S(1)}, s16[3,128,128]{2,1,0:T(8,128)(2,1)S(1)}, u32[]{:S(2)}, u32[]{:S(2)}) collective-permute-start(s16[3,128,128]{2,1,0:T(8,128)(2,1)S(1)} %get-tuple-element.14.flat_ref), channel_id=1, source_target_pairs={{64,0},{80,16},{96,32},{112,48},{0,64},{16,80},{32,96},{48,112},{6... | collective-permute-start | bytes 294920 | tf_op jit(solution)/shard_map/ppermute | solution.py:348
  16.6 1.1 %collective-permute-start = (s16[3,128,128]{2,1,0:T(8,128)(2,1)S(1)}, s16[3,128,128]{2,1,0:T(8,128)(2,1)S(1)}, u32[]{:S(2)}, u32[]{:S(2)}) collective-permute-start(s16[3,128,128]{2,1,0:T(8,128)(2,1)S(1)} %get-tuple-element.14.flat_ref), channel_id=1, source_target_pairs={{32,0},{48,16},{64,32},{80,48},{96,64},{112,80},{0,96},{16,112},{3... | collective-permute-start | bytes 294920 | tf_op jit(solution)/shard_map/ppermute | solution.py:348
  17.7 3.1 %theory.2.stored_ref = bf16[3,512,2048]{2,1,0:T(8,128)(2,1)} custom-call(s16[3,128,128]{2,1,0:T(8,128)(2,1)S(1)} %get-tuple-element.14.flat_ref), custom_call_target="tpu_custom_call" | custom-call | flops 2000000000 | bytes 6400000 | tf_op jit(solution)/shard_map/theory/pallas_call | solution.py:192
  20.8 0.0 collective-permute-done.2.flat3_ref
  20.8 0.0 collective-permute-done.1.flat2_ref
  20.8 0.2 collective-permute-done.flat_ref
  21.0 2.1 %all-to-all-done = bf16[16,8,2048]{2,1,0:T(8,128)(2,1)S(1)} async-done(((bf16[16,8,2048]{2,1,0:T(8,128)(2,1)}), bf16[16,8,2048]{2,1,0:T(8,128)(2,1)S(1)}, u32[]{:S(2)}, u32[]{:S(2)}) %all-to-all-start) | async-done | bytes 524320 | tf_op jit(solution)/shard_map/all_to_all | solution.py:353
  23.1 2.0 %collective-permute-start.3 = (bf16[128,2048]{1,0:T(8,128)(2,1)S(1)}, bf16[128,2048]{1,0:T(8,128)(2,1)S(1)}, u32[]{:S(2)}, u32[]{:S(2)}) collective-permute-start(bf16[128,2048]{1,0:T(8,128)(2,1)S(1)} %bitcast.7), channel_id=1, source_target_pairs={{0,16},{16,0},{32,48},{48,32},{64,80},{80,64},{96,112},{112,96},{1... | collective-permute-start | bytes 1572872 | tf_op jit(solution)/shard_map/ppermute | solution.py:356
  25.1 2.0 %theory.3.theory_ref = bf16[3,512,2048]{2,1,0:T(8,128)(2,1)S(1)} custom-call(s16[3,128,128]{2,1,0:T(8,128)(2,1)S(1)} %collective-permute-done.flat_ref), custom_call_target="tpu_custom_call" | custom-call | flops 2000000000 | bytes 6400000 | tf_op jit(solution)/shard_map/theory/pallas_call | solution.py:192
  27.1 0.0 collective-permute-done.3.other_ref
  27.1 0.0 copy-done
  27.1 12.5 %score.1 = f32[256,128]{1,0:T(8,128)S(1)} custom-call(s32[48]{0:T(128)S(1)} %copy-done, bf16[3,512,2048]{2,1,0:T(8,128)(2,1)} %theory.2.stored_ref, bf16[3,512,2048]{2,1,0:T(8,128)(2,1)S(1)} %theory.3.theory_ref, s16[3,128,128]{2,1,0:T(8,128)(2,1)S(1)} %collective-permute-done.1.flat2_ref, s16[3,128,128]{2,1,0:T(8,128)(2,1)S(1)} %collective-permute-done.2.flat3_ref, ...), custom_call_target="tpu_custom_call" | custom-call | tf_op jit(solution)/shard_map/score/pallas_call | solution.py:358
  39.7 12.5 %all_to_all.23 = f32[32,8,128]{2,1,0:T(8,128)} all-to-all(f32[32,8,128]{2,1,0:T(8,128)S(1)} %bitcast.9), channel_id=1, replica_groups={{0,1,2,3,4,5,6,7,8,9,10,11,12,13,14,15,16,17,18,19,20,21,22,23,24,25,26..., dimensions={0} | all-to-all | bytes 262144 | tf_op jit(solution)/shard_map/all_to_all | solution.py:384
  52.2 1.7 %finish.1 = (f32[2,32]{1,0:T(2,128)}, f32[2,32]{1,0:T(2,128)}) custom-call(s32[8,128]{1,0:T(8,128)} %get-tuple-element.12.where_hbm, f32[256,128]{1,0:T(8,128)} %bitcast.11), custom_call_target="tpu_custom_call" | custom-call | tf_op jit(solution)/shard_map/finish/pallas_call | solution.py:392
Async XLA Ops:
  4.2 19.0 %all-to-all-start = ((bf16[16,8,2048]{2,1,0:T(8,128)(2,1)}), bf16[16,8,2048]{2,1,0:T(8,128)(2,1)S(1)}, u32[]{:S(2)}, u32[]{:S(2)}) async-start(bf16[16,8,2048]{2,1,0:T(8,128)(2,1)} %bitcast.10), calls=%async_computation | async-start | bytes 1048576 | tf_op jit(solution)/shard_map/all_to_all | solution.py:353
  12.6 14.5 %copy-start = (s32[48]{0:T(128)S(1)}, s32[48]{0:T(128)}, u32[]{:S(2)}) copy-start(s32[48]{0:T(128)} %counts_ref.1) | copy-start | bytes 580
  12.6 8.2 %collective-permute-start.2 = (s16[3,128,128]{2,1,0:T(8,128)(2,1)S(1)}, s16[3,128,128]{2,1,0:T(8,128)(2,1)S(1)}, u32[]{:S(2)}, u32[]{:S(2)}) collective-permute-start(s16[3,128,128]{2,1,0:T(8,128)(2,1)S(1)} %get-tuple-element.14.flat_ref), channel_id=1, source_target_pairs={{96,0},{112,16},{0,32},{16,48},{32,64},{48,80},{64,96},{80,112},{9... | collective-permute-start | bytes 294920 | tf_op jit(solution)/shard_map/ppermute | solution.py:348
  14.0 6.8 %collective-permute-start.1 = (s16[3,128,128]{2,1,0:T(8,128)(2,1)S(1)}, s16[3,128,128]{2,1,0:T(8,128)(2,1)S(1)}, u32[]{:S(2)}, u32[]{:S(2)}) collective-permute-start(s16[3,128,128]{2,1,0:T(8,128)(2,1)S(1)} %get-tuple-element.14.flat_ref), channel_id=1, source_target_pairs={{64,0},{80,16},{96,32},{112,48},{0,64},{16,80},{32,96},{48,112},{6... | collective-permute-start | bytes 294920 | tf_op jit(solution)/shard_map/ppermute | solution.py:348
  16.6 4.4 %collective-permute-start = (s16[3,128,128]{2,1,0:T(8,128)(2,1)S(1)}, s16[3,128,128]{2,1,0:T(8,128)(2,1)S(1)}, u32[]{:S(2)}, u32[]{:S(2)}) collective-permute-start(s16[3,128,128]{2,1,0:T(8,128)(2,1)S(1)} %get-tuple-element.14.flat_ref), channel_id=1, source_target_pairs={{32,0},{48,16},{64,32},{80,48},{96,64},{112,80},{0,96},{16,112},{3... | collective-permute-start | bytes 294920 | tf_op jit(solution)/shard_map/ppermute | solution.py:348
  23.1 4.0 %collective-permute-start.3 = (bf16[128,2048]{1,0:T(8,128)(2,1)S(1)}, bf16[128,2048]{1,0:T(8,128)(2,1)S(1)}, u32[]{:S(2)}, u32[]{:S(2)}) collective-permute-start(bf16[128,2048]{1,0:T(8,128)(2,1)S(1)} %bitcast.7), channel_id=1, source_target_pairs={{0,16},{16,0},{32,48},{48,32},{64,80},{80,64},{96,112},{112,96},{1... | collective-permute-start | bytes 1572872 | tf_op jit(solution)/shard_map/ppermute | solution.py:356

commit v4 on v3

--- a/solution.py
+++ b/solution.py
@@ -57,6 +57,11 @@
     padded[:, :PAD] = jnp.zeros((rows, PAD), jnp.bfloat16)
     padded[:, PAD + width :] = jnp.zeros((rows, PAD), jnp.bfloat16)
     padded[:, PAD : PAD + width] = rooted
+    peak = jnp.max(rooted.astype(jnp.float32), axis=1, keepdims=True)
+    scale = jnp.ones((rows, 1), jnp.float32)
+    for power in (16, 8, 4, 2, 1):
+        larger = scale * 2.0**power
+        scale = jnp.where(peak * larger <= 256.0, larger, scale)
     copies[1].wait()
     place = iota((out_ref.shape[0], rows), 0)
     inner = place % SLOTS
@@ -78,6 +83,7 @@
         )
         values = rooted[:, start : start + block].astype(jnp.float32)
         prepared = (values - background / (2.0 * LAG)).astype(jnp.bfloat16)
+        prepared = (prepared.astype(jnp.float32) * scale).astype(jnp.bfloat16)
         out_ref[:, start : start + block] = jnp.dot(
             routing, prepared, preferred_element_type=jnp.float32
         ).astype(jnp.bfloat16)
@@ -91,21 +97,25 @@
     copies[3].wait()
     mass = lax.axis_index("mass")
     windows = counts_ref.shape[0]
-    counted = jnp.zeros((windows, rows), jnp.int32)
+    counted = jnp.zeros((windows, rows), jnp.float32)
     at_window = iota((windows, rows), 0)
     for index in range(windows):
-        counted = jnp.where(at_window == index, counts_ref[index], counted)
+        counted = jnp.where(at_window == index, counts_ref[index].astype(jnp.float32), counted)
     where_ref[...] = jnp.zeros_like(where_ref)
+    diagonal = iota((rows, rows), 0) == iota((rows, rows), 1)
+    turned_scale = jnp.sum(jnp.where(diagonal, scale, 0.0), axis=0, keepdims=True)
     for pick in range(2):
         here = routes_ref[pick : pick + 1, :]
         mine = taken & (window == here)
         found = jnp.sum(jnp.where(mine, place, 0), axis=0, keepdims=True)
         lanes = slice(pick * rows, (pick + 1) * rows)
-        where_ref[0:1, lanes] = mass * SLOTS + found % SLOTS
-        where_ref[1:2, lanes] = found // SLOTS
+        inside = found % SLOTS
+        where_ref[0:1, lanes] = ((inside // 2) * 32 + mass * 2 + inside % 2).astype(jnp.float32)
+        where_ref[1:2, lanes] = (found // SLOTS).astype(jnp.float32)
         where_ref[2:3, lanes] = jnp.sum(
-            jnp.where(at_window == here, counted, 0), axis=0, keepdims=True
-        )
+            jnp.where(at_window == here, counted, 0.0), axis=0, keepdims=True
+        )
+        where_ref[3:4, lanes] = turned_scale
     leaving.append(pltpu.make_async_copy(where_ref, where_hbm, sems.at[4]))
     leaving[-1].start()
     copies[2].wait()
@@ -130,10 +140,11 @@
     member = iota((128, 128), 1) // 32 + 4 * (iota((128, 128), 0) % 2)
     low = (bins & (LOW - 1)).astype(jnp.float32).astype(jnp.bfloat16)
     high = ((bins >> 7) * 8 + member).astype(jnp.float32).astype(jnp.bfloat16)
-    for pair in range(32):
+    largest = jnp.zeros((8, 128), jnp.float32)
+    for quad in range(16):
         parts = []
-        for half in range(2):
-            row = 4 * pair + 2 * half
+        for item in range(4):
+            row = 8 * quad + 2 * item
             high_row = jnp.concatenate([high[row : row + 1], high[row + 1 : row + 2]], axis=1)
             low_row = jnp.concatenate([low[row : row + 1], low[row + 1 : row + 2]], axis=1)
             parts.append(
@@ -145,33 +156,38 @@
                 )
             )
         for part in range(HIGH):
-            tile = jnp.concatenate([item[part * 8 : part * 8 + 8] for item in parts], axis=0)
-            theory_ref[pair * 16 : pair * 16 + 16, part * LOW : (part + 1) * LOW] = tile.astype(
-                jnp.bfloat16
-            )
-        if finished is not None and pair % 8 == 7:
-            finished(pair // 8)
-
-
-def theory_kernel(flat_ref, theory_ref):
+            pieces = [item[part * 8 : part * 8 + 8] for item in parts]
+            theory_ref[quad * 32 : quad * 32 + 32, part * LOW : (part + 1) * LOW] = (
+                jnp.concatenate(pieces, axis=0).astype(theory_ref.dtype)
+            )
+            more = jnp.maximum(
+                jnp.maximum(pieces[0], pieces[1]), jnp.maximum(pieces[2], pieces[3])
+            )
+            largest = jnp.maximum(largest, more)
+        if finished is not None and quad % 4 == 3:
+            finished(quad // 4)
+    return largest
+
+
+def theory_kernel(flat_ref, theory_ref, largest_ref):
     def window(step, carry):
-        theory_of(flat_ref[step].astype(jnp.int32), theory_ref.at[step])
+        largest_ref[step] = theory_of(flat_ref[step].astype(jnp.int32), theory_ref.at[step])
         return carry
 
     lax.fori_loop(0, flat_ref.shape[0], window, 0)
 
 
-def stored_theory_kernel(flat_ref, theory_ref, held, sems):
+def stored_theory_kernel(flat_ref, theory_hbm, largest_hbm, held, largest, sems):
     steps = flat_ref.shape[0]
 
     def copy_of(step, quarter):
         rows = pl.ds(quarter * 128, 128)
         return pltpu.make_async_copy(
-            held.at[step, rows], theory_ref.at[step, rows], sems.at[step, quarter]
+            held.at[step, rows], theory_hbm.at[step, rows], sems.at[step, quarter]
         )
 
     def window(step, carry):
-        theory_of(
+        largest[step] = theory_of(
             flat_ref[step].astype(jnp.int32),
             held.at[step],
             lambda quarter: copy_of(step, quarter).start(),
@@ -179,23 +195,30 @@
         return carry
 
     lax.fori_loop(0, steps, window, 0)
+    last = pltpu.make_async_copy(largest, largest_hbm, sems.at[steps, 0])
+    last.start()
     for step in range(steps):
         for quarter in range(4):
             copy_of(step, quarter).wait()
+    last.wait()
 
 
 def build_theory(flat, width, stored):
     steps = flat.shape[0]
-    shape = (steps, 512, width)
+    shape, small = (steps, 512, width), (steps, 8, 128)
     space = pltpu.HBM if stored else VMEM
-    scratch = [pltpu.VMEM(shape, jnp.bfloat16), pltpu.SemaphoreType.DMA((steps, 4))]
+    scratch = [
+        pltpu.VMEM(shape, F8),
+        pltpu.VMEM(small, jnp.float32),
+        pltpu.SemaphoreType.DMA((steps + 1, 4)),
+    ]
     return pl.pallas_call(
         stored_theory_kernel if stored else theory_kernel,
-        out_shape=space(shape, jnp.bfloat16),
+        out_shape=(space(shape, F8), space(small, jnp.float32)),
         in_specs=[pl.BlockSpec(memory_space=VMEM)],
-        out_specs=pl.BlockSpec(memory_space=space),
+        out_specs=(pl.BlockSpec(memory_space=space),) * 2,
         scratch_shapes=scratch if stored else [],
-        compiler_params=pltpu.CompilerParams(vmem_limit_bytes=(10 if stored else 4) << 20),
+        compiler_params=pltpu.CompilerParams(vmem_limit_bytes=(8 if stored else 4) << 20),
         cost_estimate=pl.CostEstimate(
             flops=2_000_000_000, bytes_accessed=6_400_000, transcendentals=0
         ),
@@ -205,68 +228,144 @@
 
 def score_kernel(
     counts_ref,
-    stored_ref,
+    stored_hbm,
+    stored_largest_hbm,
     theory_ref,
+    largest_ref,
+    flat0_ref,
+    flat1_ref,
     flat2_ref,
     flat3_ref,
     own_ref,
     other_ref,
     out_ref,
     held,
+    held_largest,
     built2,
     built3,
+    halves,
+    stats_ref,
+    exact,
+    tables_ref,
     sems,
 ):
-    steps = theory_ref.shape[0]
+    steps, width = theory_ref.shape[0], theory_ref.shape[2]
+    flats = (flat0_ref, flat1_ref, flat2_ref, flat3_ref)
 
     def copy_of(step):
-        return pltpu.make_async_copy(stored_ref.at[step], held.at[step], sems.at[step])
-
+        return pltpu.make_async_copy(stored_hbm.at[step], held.at[step], sems.at[step])
+
+    small = pltpu.make_async_copy(stored_largest_hbm, held_largest, sems.at[steps])
+    small.start()
     for step in range(steps):
         copy_of(step).start()
     y = lax.axis_index("spec") // 2
     core = lax.axis_index("spec") % 2
     mass = lax.axis_index("mass")
-    rows = own_ref.shape[0] * 2
-    spectra = jnp.concatenate([own_ref[...], other_ref[...]], axis=0)
-    slot = (iota((1, rows), 1) % SLOTS) // 2
+    rows = own_ref.shape[0]
     local = iota((512, 1), 0)
+    entry = iota((64, rows), 0) % 32
+    source = (entry // 2) * SLOTS + entry % 2
+    first_half = iota((64, rows), 0) < 32
+
+    def chosen(step):
+        mine = iota((64, rows), 1) == source + 2 * step
+        return sum(
+            jnp.dot(
+                jnp.where(mine & (first_half == first), 1.0, 0.0).astype(jnp.bfloat16),
+                ref[...],
+                preferred_element_type=jnp.float32,
+            )
+            for first, ref in ((True, own_ref), (False, other_ref))
+        )
+
+    for step in range(steps):
+        values = chosen(step)
+        upper = values.astype(F8)
+        halves[step, :64, :] = upper
+        halves[step, 64:, :] = (values - upper.astype(jnp.float32)).astype(F8)
+    small.wait()
+
+    def reduced(scores, limit):
+        valid = local < limit
+        best = jnp.max(jnp.where(valid, scores, -1e30), axis=0, keepdims=True)
+        scores = jnp.where(valid, scores, 0.0)
+        return (
+            best,
+            jnp.sum(scores, axis=0, keepdims=True),
+            jnp.sum(scores * scores, axis=0, keepdims=True),
+        )
+
+    def base_of(turn):
+        return (lax.rem(y + turn, 4) * 2 + core) * 512
+
+    def keep(step, found):
+        stats_ref[step, 0:1, :] = functools.reduce(jnp.maximum, [item[0] for item in found])
+        for row in (1, 2):
+            stats_ref[step, row : row + 1, :] = functools.reduce(
+                jnp.add, [item[row] for item in found]
+            )
 
     def window(step, carry):
-        best, total, square = carry
         live = counts_ref[mass * steps + step]
-        theory_of(flat2_ref[step].astype(jnp.int32), built2)
-        theory_of(flat3_ref[step].astype(jnp.int32), built3)
+        largest = jnp.maximum(
+            theory_of(flat2_ref[step].astype(jnp.int32), built2),
+            theory_of(flat3_ref[step].astype(jnp.int32), built3),
+        )
+        largest = jnp.maximum(largest, jnp.maximum(held_largest[step], largest_ref[step]))
+        beyond = jnp.max(largest) > 16.0
         copy_of(step).wait()
-        now_best, now_total, now_square = [], [], []
-        tables = [held.at[step], theory_ref.at[step], built2, built3]
-        for turn, theory in enumerate(tables):
-            base = (((y + turn) % 4) * 2 + core) * 512
+        found = []
+        for turn, theory in enumerate((held.at[step], theory_ref.at[step], built2, built3)):
             scores = lax.dot_general(
                 theory[...],
-                spectra,
+                halves[step],
                 (((1,), (1,)), ((), ())),
                 preferred_element_type=jnp.float32,
             )
-            valid = local < (live - base)
-            now_best.append(jnp.max(jnp.where(valid, scores, -1e30), axis=0, keepdims=True))
-            scores = jnp.where(valid, scores, 0.0)
-            now_total.append(jnp.sum(scores, axis=0, keepdims=True))
-            now_square.append(jnp.sum(scores * scores, axis=0, keepdims=True))
-        here = slot == step
-        best = jnp.where(here, functools.reduce(jnp.maximum, now_best), best)
-        total = jnp.where(here, sum(now_total[1:], now_total[0]), total)
-        square = jnp.where(here, sum(now_square[1:], now_square[0]), square)
-        return best, total, square
-
-    zeros = jnp.zeros((1, rows), jnp.float32)
-    best, total, square = lax.fori_loop(0, steps, window, (zeros, zeros, zeros))
-    stats = jnp.concatenate(
-        [best / 32.0, total / 32.0, square / 1024.0, jnp.zeros((5, rows), jnp.float32)], axis=0
-    )
-    own, other = stats[:, : rows // 2], stats[:, rows // 2 :]
-    first = jnp.where(core == 0, own, other)
-    second = jnp.where(core == 0, other, own)
+            scores = scores + pltpu.roll(scores, 64, 1)
+            found.append(reduced(scores, live - base_of(turn)))
+        keep(step, found)
+
+        @pl.when(beyond)
+        def _():
+            for turn in range(4):
+                tables_ref[turn] = flats[turn][step].astype(jnp.int32)
+            values = chosen(step).astype(jnp.bfloat16)
+            values = jnp.concatenate([values, jnp.zeros_like(values)], axis=0)
+
+            def piece(turn, found):
+                theory_of(tables_ref[turn], exact)
+                scores = lax.dot_general(
+                    exact[...],
+                    values,
+                    (((1,), (1,)), ((), ())),
+                    preferred_element_type=jnp.float32,
+                )
+                more = reduced(scores, live - base_of(turn))
+                return (
+                    jnp.maximum(found[0], more[0]),
+                    found[1] + more[1],
+                    found[2] + more[2],
+                )
+
+            zeros = jnp.zeros((1, 128), jnp.float32)
+            keep(step, [lax.fori_loop(0, 4, piece, (zeros - 1e30, zeros, zeros))])
+
+        return carry
+
+    stats_ref[...] = jnp.zeros_like(stats_ref)
+    lax.fori_loop(0, steps, window, 0)
+    part = iota((8, 128), 1) // 32
+    tiles = []
+    for half in range(2):
+        tile = jnp.zeros((8, 128), jnp.float32)
+        for step in range(steps):
+            moved = pltpu.roll(stats_ref[step], (step * 32 - half * 32) % 128, 1)
+            tile = jnp.where(part == step, moved, tile)
+        tiles.append(tile)
+    first = jnp.where(core == 0, tiles[0], tiles[1])
+    second = jnp.where(core == 0, tiles[1], tiles[0])
     peers = out_ref.shape[0] // 16
     for peer in range(peers):
         out_ref[peer * 8 : peer * 8 + 8, :] = first
@@ -284,9 +383,10 @@
         copy.wait()
     rows = best_ref.shape[1]
     peers = stats_ref.shape[0] // 16
-    lane = jnp.broadcast_to(where_ref[0:1, :], (8, 128))
-    shard = where_ref[1:2, :]
-    live = where_ref[2:3, :].astype(jnp.float32)
+    lane = jnp.broadcast_to(where_ref[0:1, :].astype(jnp.int32), (8, 128))
+    shard = where_ref[1:2, :].astype(jnp.int32)
+    live = where_ref[2:3, :]
+    unscale = 1.0 / (where_ref[3:4, :] * 32.0)
     halves = []
     for half in range(2):
         chosen = jnp.zeros((8, 128), jnp.float32)
@@ -295,9 +395,9 @@
             found = jnp.take_along_axis(stats_ref[at : at + 8, :], lane, axis=1)
             chosen = jnp.where(shard == peer, found, chosen)
         halves.append(chosen)
-    best = jnp.maximum(halves[0][0:1], halves[1][0:1])
-    total = halves[0][1:2] + halves[1][1:2]
-    square = halves[0][2:3] + halves[1][2:3]
+    best = jnp.maximum(halves[0][0:1], halves[1][0:1]) * unscale
+    total = (halves[0][1:2] + halves[1][1:2]) * unscale
+    square = (halves[0][2:3] + halves[1][2:3]) * unscale * unscale
     mean = total / live
     spread = square / live - mean * mean
     z = (best - mean) / jnp.sqrt(spread + EPS)
@@ -321,13 +421,13 @@
         out_shape=(
             pltpu.HBM((mass_count * SLOTS, width), jnp.bfloat16),
             jax.ShapeDtypeStruct((steps, 128, 128), jnp.int16),
-            pltpu.HBM((8, 128), jnp.int32),
+            pltpu.HBM((8, 128), jnp.float32),
         ),
         in_specs=[hbm] * 4,
         out_specs=(hbm, vmem, hbm),
         scratch_shapes=[
             pltpu.VMEM((mass_count * SLOTS, width), jnp.bfloat16),
-            pltpu.VMEM((8, 128), jnp.int32),
+            pltpu.VMEM((8, 128), jnp.float32),
             pltpu.SMEM(counts.shape, counts.dtype),
             pltpu.VMEM((rows, width), spectra.dtype),
             pltpu.VMEM(routes_t.shape, routes_t.dtype),
@@ -351,29 +451,35 @@
         for turn in range(1, 4)
     ]
     own = lax.all_to_all(outgoing, "mass", split_axis=0, concat_axis=0, tiled=True)
-    first = build_theory(flats[0], width, True)
+    first, first_largest = build_theory(flats[0], width, True)
     own, first, flats = lax.optimization_barrier((own, first, flats))
     other = lax.ppermute(own, "spec", [(i, i ^ 1) for i in range(spec_count)])
-    second = build_theory(flats[1], width, False)
+    second, second_largest = build_theory(flats[1], width, False)
     stats = pl.pallas_call(
         score_kernel,
         out_shape=jax.ShapeDtypeStruct((2 * mass_count * 8, 128), jnp.float32),
-        in_specs=[smem, hbm] + [vmem] * 5,
+        in_specs=[smem, hbm, hbm] + [vmem] * 8,
         out_specs=vmem,
         scratch_shapes=[
-            pltpu.VMEM((steps, 512, width), jnp.bfloat16),
+            pltpu.VMEM((steps, 512, width), F8),
+            pltpu.VMEM((steps, 8, 128), jnp.float32),
+            pltpu.VMEM((512, width), F8),
+            pltpu.VMEM((512, width), F8),
+            pltpu.VMEM((steps, 128, width), F8),
+            pltpu.VMEM((steps, 8, 128), jnp.float32),
             pltpu.VMEM((512, width), jnp.bfloat16),
-            pltpu.VMEM((512, width), jnp.bfloat16),
-            pltpu.SemaphoreType.DMA((steps,)),
+            pltpu.VMEM((4, 128, 128), jnp.int32),
+            pltpu.SemaphoreType.DMA((steps + 1,)),
         ],
         compiler_params=pltpu.CompilerParams(vmem_limit_bytes=24 << 20),
         name="score",
     )(
         counts,
         pltpu.with_memory_space_constraint(first, pltpu.HBM),
+        pltpu.with_memory_space_constraint(first_largest, pltpu.HBM),
         second,
-        flats[2],
-        flats[3],
+        second_largest,
+        *flats,
         own,
         other,
     )
@@ -395,7 +501,7 @@
         in_specs=[hbm] * 2,
         out_specs=(vmem, vmem),
         scratch_shapes=[
-            pltpu.VMEM((8, 128), jnp.int32),
+            pltpu.VMEM((8, 128), jnp.float32),
             pltpu.VMEM(back.shape, jnp.float32),
             pltpu.SemaphoreType.DMA((2,)),
         ],

time: 54.1 us -> 51.9 us (0.959)
  Pallas kernels: 22.9 us -> 20.8 us
    pallas_call x1, Pallas kernels: 12.5 us -> 10.1 us  [per_device(): pl.pallas_call(score_kernel, out_shape=jax.ShapeDtypeStruct((2 * mass_cou...]
where the time goes in v4:
time: 51.9 us; the launch traced here: 51.7 us
  Pallas kernels  20.8 us (40%)
  starting transfers between devices  15.5 us (30%)
  blocking collectives  12.4 us (24%)
  waiting for transfers between devices  2.33 us (4%)
  between operations  0.7 us (1%)
    all_to_all x1, blocking collectives, per_device(): lax.all_to_all(stats, ('spec', 'mass'), split_axis=0, concat_axis=0, tile...  12.4 us
    pallas_call x1, Pallas kernels, per_device(): pl.pallas_call(score_kernel, out_shape=jax.ShapeDtypeStruct((2 * mass_cou...  10.1 us
    all_to_all x1, starting transfers between devices, per_device(): lax.all_to_all(outgoing, 'mass', split_axis=0, concat_axis=0, tiled=True)  8.44 us
    pallas_call x2, Pallas kernels, build_theory(): pl.pallas_call(stored_theory_kernel if stored else theory_kernel, out_sha...  5.32 us
    ppermute x3, starting transfers between devices, per_device(): lax.ppermute(flat, 'spec', [((i + 2 * turn) % spec_count, i) for i in ran...  5.06 us
    pallas_call x1, Pallas kernels, per_device(): pl.pallas_call(prepare_kernel, out_shape=(pltpu.HBM((mass_count * SLOTS,...  3.67 us
    all_to_all x1, waiting for transfers between devices, per_device(): lax.all_to_all(outgoing, 'mass', split_axis=0, concat_axis=0, tiled=True)  2.14 us
    ppermute x1, starting transfers between devices, per_device(): other = lax.ppermute(own, 'spec', [(i, i ^ 1) for i in range(spec_count)])  1.98 us
  transfers between devices with their start and end apart: 5, of which 2 were waited for; matrix products, arithmetic and copies ran while one was open for 0% of the time, Pallas kernels for 10%

profile of v4, /device:TPU:1, one launch (start us, length us, event | category | flops | bytes accessed | tf_op | source)
XLA Modules:
  0.0 51.7 jit_solution(10553131304276000295)
XLA Ops:
  0.6 3.7 %prepare.1 = (bf16[128,2048]{1,0:T(8,128)(2,1)}, s16[3,128,128]{2,1,0:T(8,128)(2,1)S(1)}, f32[8,128]{1,0:T(8,128)}) custom-call(bf16[32,2048]{1,0:T(8,128)(2,1)} %spectra_hbm.1, s32[2,32]{1,0:T(2,128)} %bitcast.12, s32[3,32,512]{2,1,0:T(8,128)} %pep_hbm.1, s32[48]{0:T(128)} %counts_ref.1), custom_call_target="tpu_custom_call" | custom-call | tf_op jit(solution)/shard_map/prepare/pallas_call | solution.py:419
  4.3 8.4 %all-to-all-start = ((bf16[16,8,2048]{2,1,0:T(8,128)(2,1)}), bf16[16,8,2048]{2,1,0:T(8,128)(2,1)S(1)}, u32[]{:S(2)}, u32[]{:S(2)}) async-start(bf16[16,8,2048]{2,1,0:T(8,128)(2,1)} %bitcast.10), calls=%async_computation | async-start | bytes 1048576 | tf_op jit(solution)/shard_map/all_to_all | solution.py:453
  12.8 1.4 %collective-permute-start.2 = (s16[3,128,128]{2,1,0:T(8,128)(2,1)S(1)}, s16[3,128,128]{2,1,0:T(8,128)(2,1)S(1)}, u32[]{:S(2)}, u32[]{:S(2)}) collective-permute-start(s16[3,128,128]{2,1,0:T(8,128)(2,1)S(1)} %get-tuple-element.26.flat_ref.flat0_ref), channel_id=1, source_target_pairs={{96,0},{112,16},{0,32},{16,48},{32,64},{48,80},{64,96},{80,112},{9... | collective-permute-start | bytes 294920 | tf_op jit(solution)/shard_map/ppermute | solution.py:448
  14.1 2.6 %collective-permute-start.1 = (s16[3,128,128]{2,1,0:T(8,128)(2,1)S(1)}, s16[3,128,128]{2,1,0:T(8,128)(2,1)S(1)}, u32[]{:S(2)}, u32[]{:S(2)}) collective-permute-start(s16[3,128,128]{2,1,0:T(8,128)(2,1)S(1)} %get-tuple-element.26.flat_ref.flat0_ref), channel_id=1, source_target_pairs={{64,0},{80,16},{96,32},{112,48},{0,64},{16,80},{32,96},{48,112},{6... | collective-permute-start | bytes 294920 | tf_op jit(solution)/shard_map/ppermute | solution.py:448
  16.7 1.1 %collective-permute-start = (s16[3,128,128]{2,1,0:T(8,128)(2,1)S(1)}, s16[3,128,128]{2,1,0:T(8,128)(2,1)S(1)}, u32[]{:S(2)}, u32[]{:S(2)}) collective-permute-start(s16[3,128,128]{2,1,0:T(8,128)(2,1)S(1)} %get-tuple-element.26.flat_ref.flat0_ref), channel_id=1, source_target_pairs={{32,0},{48,16},{64,32},{80,48},{96,64},{112,80},{0,96},{16,112},{3... | collective-permute-start | bytes 294920 | tf_op jit(solution)/shard_map/ppermute | solution.py:448
  17.8 3.1 %theory.2 = (f8e4m3fn[3,512,2048]{2,1,0:T(32,128)(4,1)}, f32[3,8,128]{2,1,0:T(8,128)}) custom-call(s16[3,128,128]{2,1,0:T(8,128)(2,1)S(1)} %get-tuple-element.26.flat_ref.flat0_ref), custom_call_target="tpu_custom_call" | custom-call | flops 2000000000 | bytes 6400000 | tf_op jit(solution)/shard_map/theory/pallas_call | solution.py:215
  20.9 0.0 collective-permute-done.2.flat3_ref
  20.9 0.0 collective-permute-done.1.flat2_ref
  20.9 0.2 collective-permute-done.flat_ref.flat1_ref
  21.1 2.1 %all-to-all-done = bf16[16,8,2048]{2,1,0:T(8,128)(2,1)S(1)} async-done(((bf16[16,8,2048]{2,1,0:T(8,128)(2,1)}), bf16[16,8,2048]{2,1,0:T(8,128)(2,1)S(1)}, u32[]{:S(2)}, u32[]{:S(2)}) %all-to-all-start) | async-done | bytes 524320 | tf_op jit(solution)/shard_map/all_to_all | solution.py:453
  23.3 0.0 copy-start
  23.3 2.0 %collective-permute-start.3 = (bf16[128,2048]{1,0:T(8,128)(2,1)S(1)}, bf16[128,2048]{1,0:T(8,128)(2,1)S(1)}, u32[]{:S(2)}, u32[]{:S(2)}) collective-permute-start(bf16[128,2048]{1,0:T(8,128)(2,1)S(1)} %bitcast.7), channel_id=1, source_target_pairs={{0,16},{16,0},{32,48},{48,32},{64,80},{80,64},{96,112},{112,96},{1... | collective-permute-start | bytes 1572872 | tf_op jit(solution)/shard_map/ppermute | solution.py:456
  25.2 2.2 %theory.3 = (f8e4m3fn[3,512,2048]{2,1,0:T(32,128)(4,1)S(1)}, f32[3,8,128]{2,1,0:T(8,128)S(1)}) custom-call(s16[3,128,128]{2,1,0:T(8,128)(2,1)S(1)} %collective-permute-done.flat_ref.flat1_ref), custom_call_target="tpu_custom_call" | custom-call | flops 2000000000 | bytes 6400000 | tf_op jit(solution)/shard_map/theory/pallas_call | solution.py:215
  27.5 0.0 collective-permute-done.3.other_ref
  27.5 0.0 copy-done
  27.5 10.1 %score.1 = f32[256,128]{1,0:T(8,128)S(1)} custom-call(s32[48]{0:T(128)S(1)} %copy-done, f8e4m3fn[3,512,2048]{2,1,0:T(32,128)(4,1)} %get-tuple-element.21.stored_hbm, f32[3,8,128]{2,1,0:T(8,128)} %get-tuple-element.22.stored_largest_hbm, f8e4m3fn[3,512,2048]{2,1,0:T(32,128)(4,1)S(1)} %get-tuple-element.24.theory_ref, ...), custom_call_target="tpu_custom_call" | custom-call | tf_op jit(solution)/shard_map/score/pallas_call | solution.py:458
  37.6 12.4 %all_to_all.23 = f32[32,8,128]{2,1,0:T(8,128)} all-to-all(f32[32,8,128]{2,1,0:T(8,128)S(1)} %bitcast.9), channel_id=1, replica_groups={{0,1,2,3,4,5,6,7,8,9,10,11,12,13,14,15,16,17,18,19,20,21,22,23,24,25,26..., dimensions={0} | all-to-all | bytes 262144 | tf_op jit(solution)/shard_map/all_to_all | solution.py:490
  50.0 1.7 %finish.1 = (f32[2,32]{1,0:T(2,128)}, f32[2,32]{1,0:T(2,128)}) custom-call(f32[8,128]{1,0:T(8,128)} %get-tuple-element.17.where_hbm, f32[256,128]{1,0:T(8,128)} %bitcast.11), custom_call_target="tpu_custom_call" | custom-call | tf_op jit(solution)/shard_map/finish/pallas_call | solution.py:498
Async XLA Ops:
  4.3 18.9 %all-to-all-start = ((bf16[16,8,2048]{2,1,0:T(8,128)(2,1)}), bf16[16,8,2048]{2,1,0:T(8,128)(2,1)S(1)}, u32[]{:S(2)}, u32[]{:S(2)}) async-start(bf16[16,8,2048]{2,1,0:T(8,128)(2,1)} %bitcast.10), calls=%async_computation | async-start | bytes 1048576 | tf_op jit(solution)/shard_map/all_to_all | solution.py:453
  12.8 8.2 %collective-permute-start.2 = (s16[3,128,128]{2,1,0:T(8,128)(2,1)S(1)}, s16[3,128,128]{2,1,0:T(8,128)(2,1)S(1)}, u32[]{:S(2)}, u32[]{:S(2)}) collective-permute-start(s16[3,128,128]{2,1,0:T(8,128)(2,1)S(1)} %get-tuple-element.26.flat_ref.flat0_ref), channel_id=1, source_target_pairs={{96,0},{112,16},{0,32},{16,48},{32,64},{48,80},{64,96},{80,112},{9... | collective-permute-start | bytes 294920 | tf_op jit(solution)/shard_map/ppermute | solution.py:448
  14.1 6.8 %collective-permute-start.1 = (s16[3,128,128]{2,1,0:T(8,128)(2,1)S(1)}, s16[3,128,128]{2,1,0:T(8,128)(2,1)S(1)}, u32[]{:S(2)}, u32[]{:S(2)}) collective-permute-start(s16[3,128,128]{2,1,0:T(8,128)(2,1)S(1)} %get-tuple-element.26.flat_ref.flat0_ref), channel_id=1, source_target_pairs={{64,0},{80,16},{96,32},{112,48},{0,64},{16,80},{32,96},{48,112},{6... | collective-permute-start | bytes 294920 | tf_op jit(solution)/shard_map/ppermute | solution.py:448
  16.7 4.4 %collective-permute-start = (s16[3,128,128]{2,1,0:T(8,128)(2,1)S(1)}, s16[3,128,128]{2,1,0:T(8,128)(2,1)S(1)}, u32[]{:S(2)}, u32[]{:S(2)}) collective-permute-start(s16[3,128,128]{2,1,0:T(8,128)(2,1)S(1)} %get-tuple-element.26.flat_ref.flat0_ref), channel_id=1, source_target_pairs={{32,0},{48,16},{64,32},{80,48},{96,64},{112,80},{0,96},{16,112},{3... | collective-permute-start | bytes 294920 | tf_op jit(solution)/shard_map/ppermute | solution.py:448
  23.3 4.2 %copy-start = (s32[48]{0:T(128)S(1)}, s32[48]{0:T(128)}, u32[]{:S(2)}) copy-start(s32[48]{0:T(128)} %counts_ref.1) | copy-start | bytes 580
  23.3 4.2 %collective-permute-start.3 = (bf16[128,2048]{1,0:T(8,128)(2,1)S(1)}, bf16[128,2048]{1,0:T(8,128)(2,1)S(1)}, u32[]{:S(2)}, u32[]{:S(2)}) collective-permute-start(bf16[128,2048]{1,0:T(8,128)(2,1)S(1)} %bitcast.7), channel_id=1, source_target_pairs={{0,16},{16,0},{32,48},{48,32},{64,80},{80,64},{96,112},{112,96},{1... | collective-permute-start | bytes 1572872 | tf_op jit(solution)/shard_map/ppermute | solution.py:456

commit v5 on v4

--- a/solution.py
+++ b/solution.py
@@ -37,7 +37,6 @@
     routes_ref,
     pep_ref,
     padded,
-    turned,
     sems,
 ):
     copies = [
@@ -97,10 +96,10 @@
     copies[3].wait()
     mass = lax.axis_index("mass")
     windows = counts_ref.shape[0]
-    counted = jnp.zeros((windows, rows), jnp.float32)
-    at_window = iota((windows, rows), 0)
+    named_by = routes_ref[...]
+    live = jnp.zeros(named_by.shape, jnp.int32)
     for index in range(windows):
-        counted = jnp.where(at_window == index, counts_ref[index].astype(jnp.float32), counted)
+        live = jnp.where(named_by == index, counts_ref[index], live)
     where_ref[...] = jnp.zeros_like(where_ref)
     diagonal = iota((rows, rows), 0) == iota((rows, rows), 1)
     turned_scale = jnp.sum(jnp.where(diagonal, scale, 0.0), axis=0, keepdims=True)
@@ -112,21 +111,15 @@
         inside = found % SLOTS
         where_ref[0:1, lanes] = ((inside // 2) * 32 + mass * 2 + inside % 2).astype(jnp.float32)
         where_ref[1:2, lanes] = (found // SLOTS).astype(jnp.float32)
-        where_ref[2:3, lanes] = jnp.sum(
-            jnp.where(at_window == here, counted, 0.0), axis=0, keepdims=True
-        )
+        where_ref[2:3, lanes] = live[pick : pick + 1].astype(jnp.float32)
         where_ref[3:4, lanes] = turned_scale
     leaving.append(pltpu.make_async_copy(where_ref, where_hbm, sems.at[4]))
     leaving[-1].start()
     copies[2].wait()
-    lane = iota((128, 128), 1) // 32
     for step in range(pep_ref.shape[0]):
         table = pep_ref[step]
-        turned[...] = jnp.concatenate([table] * 4, axis=0).T
-        flat = jnp.zeros((128, 128), jnp.int32)
-        for part in range(4):
-            flat = jnp.where(lane == part, turned[pl.ds(part, 128, stride=4), :], flat)
-        flat_ref[step] = flat.astype(jnp.int16)
+        parts = [table[:, part * 128 : part * 128 + 128] for part in range(4)]
+        flat_ref[step] = jnp.concatenate(parts, axis=0).T.astype(jnp.int16)
     for copy in leaving:
         copy.wait()
 
@@ -246,6 +239,7 @@
     halves,
     stats_ref,
     exact,
+    exact_rows,
     tables_ref,
     sems,
 ):
@@ -263,27 +257,20 @@
     core = lax.axis_index("spec") % 2
     mass = lax.axis_index("mass")
     rows = own_ref.shape[0]
-    local = iota((512, 1), 0)
-    entry = iota((64, rows), 0) % 32
-    source = (entry // 2) * SLOTS + entry % 2
-    first_half = iota((64, rows), 0) < 32
-
-    def chosen(step):
-        mine = iota((64, rows), 1) == source + 2 * step
-        return sum(
-            jnp.dot(
-                jnp.where(mine & (first_half == first), 1.0, 0.0).astype(jnp.bfloat16),
-                ref[...],
-                preferred_element_type=jnp.float32,
-            )
-            for first, ref in ((True, own_ref), (False, other_ref))
-        )
-
-    for step in range(steps):
-        values = chosen(step)
+    local = (iota((512, 1), 0) % 4) * 128 + iota((512, 1), 0) // 4
+    entry = iota((32 * steps, rows), 0)
+    source = (entry % 32 // 2) * SLOTS + entry // 32 * 2 + entry % 2
+    pick = jnp.where(iota((32 * steps, rows), 1) == source, 1.0, 0.0).astype(jnp.bfloat16)
+    for half, ref in enumerate((own_ref, other_ref)):
+        values = jnp.dot(pick, ref[...], preferred_element_type=jnp.float32)
         upper = values.astype(F8)
-        halves[step, :64, :] = upper
-        halves[step, 64:, :] = (values - upper.astype(jnp.float32)).astype(F8)
+        lower = ((values - upper.astype(jnp.float32)) * 32.0).astype(F8)
+        for step in range(steps):
+            rows_now = slice(step * 32, step * 32 + 32)
+            at = half * 32
+            halves[step, at : at + 32, :] = upper[rows_now]
+            halves[step, 64 + at : 96 + at, :] = lower[rows_now]
+            exact_rows[step, at : at + 32, :] = values[rows_now].astype(jnp.bfloat16)
     small.wait()
 
     def reduced(scores, limit):
@@ -323,7 +310,7 @@
                 (((1,), (1,)), ((), ())),
                 preferred_element_type=jnp.float32,
             )
-            scores = scores + pltpu.roll(scores, 64, 1)
+            scores = scores + pltpu.roll(scores, 64, 1) * (1.0 / 32.0)
             found.append(reduced(scores, live - base_of(turn)))
         keep(step, found)
 
@@ -331,7 +318,7 @@
         def _():
             for turn in range(4):
                 tables_ref[turn] = flats[turn][step].astype(jnp.int32)
-            values = chosen(step).astype(jnp.bfloat16)
+            values = exact_rows[step]
             values = jnp.concatenate([values, jnp.zeros_like(values)], axis=0)
 
             def piece(turn, found):
@@ -433,7 +420,6 @@
             pltpu.VMEM(routes_t.shape, routes_t.dtype),
             pltpu.VMEM(pep_bins.shape, pep_bins.dtype),
             pltpu.VMEM((rows, width + 2 * PAD), jnp.bfloat16),
-            pltpu.VMEM((512, 128), jnp.int32),
             pltpu.SemaphoreType.DMA((5 + width // 256,)),
         ],
         compiler_params=pltpu.CompilerParams(vmem_limit_bytes=8 << 20),
@@ -468,6 +454,7 @@
             pltpu.VMEM((steps, 128, width), F8),
             pltpu.VMEM((steps, 8, 128), jnp.float32),
             pltpu.VMEM((512, width), jnp.bfloat16),
+            pltpu.VMEM((steps, 64, width), jnp.bfloat16),
             pltpu.VMEM((4, 128, 128), jnp.int32),
             pltpu.SemaphoreType.DMA((steps + 1,)),
         ],

time: 51.9 us -> 52.2 us (level)
  no operation moved by 1% of the time
where the time goes in v5:
time: 52.2 us; the launch traced here: 51.9 us
  Pallas kernels  21 us (40%)
  starting transfers between devices  15.5 us (30%)
  blocking collectives  12.4 us (24%)
  waiting for transfers between devices  2.33 us (4%)
  between operations  0.7 us (1%)
    all_to_all x1, blocking collectives, per_device(): lax.all_to_all(stats, ('spec', 'mass'), split_axis=0, concat_axis=0, tile...  12.4 us
    pallas_call x1, Pallas kernels, per_device(): pl.pallas_call(score_kernel, out_shape=jax.ShapeDtypeStruct((2 * mass_cou...  10.3 us
    all_to_all x1, starting transfers between devices, per_device(): lax.all_to_all(outgoing, 'mass', split_axis=0, concat_axis=0, tiled=True)  8.44 us
    pallas_call x2, Pallas kernels, build_theory(): pl.pallas_call(stored_theory_kernel if stored else theory_kernel, out_sha...  5.32 us
    ppermute x3, starting transfers between devices, per_device(): lax.ppermute(flat, 'spec', [((i + 2 * turn) % spec_count, i) for i in ran...  5.06 us
    pallas_call x1, Pallas kernels, per_device(): pl.pallas_call(prepare_kernel, out_shape=(pltpu.HBM((mass_count * SLOTS,...  3.68 us
    all_to_all x1, waiting for transfers between devices, per_device(): lax.all_to_all(outgoing, 'mass', split_axis=0, concat_axis=0, tiled=True)  2.14 us
    ppermute x1, starting transfers between devices, per_device(): other = lax.ppermute(own, 'spec', [(i, i ^ 1) for i in range(spec_count)])  1.98 us
  transfers between devices with their start and end apart: 5, of which 2 were waited for; matrix products, arithmetic and copies ran while one was open for 0% of the time, Pallas kernels for 10%

profile of v5, /device:TPU:1, one launch (start us, length us, event | category | flops | bytes accessed | tf_op | source)
XLA Modules:
  0.0 51.9 jit_solution(3814677713516446301)
XLA Ops:
  0.6 3.7 %prepare.1 = (bf16[128,2048]{1,0:T(8,128)(2,1)}, s16[3,128,128]{2,1,0:T(8,128)(2,1)S(1)}, f32[8,128]{1,0:T(8,128)}) custom-call(bf16[32,2048]{1,0:T(8,128)(2,1)} %spectra_hbm.1, s32[2,32]{1,0:T(2,128)} %bitcast.12, s32[3,32,512]{2,1,0:T(8,128)} %pep_hbm.1, s32[48]{0:T(128)} %counts_ref.1), custom_call_target="tpu_custom_call" | custom-call | tf_op jit(solution)/shard_map/prepare/pallas_call | solution.py:406
  4.3 8.4 %all-to-all-start = ((bf16[16,8,2048]{2,1,0:T(8,128)(2,1)}), bf16[16,8,2048]{2,1,0:T(8,128)(2,1)S(1)}, u32[]{:S(2)}, u32[]{:S(2)}) async-start(bf16[16,8,2048]{2,1,0:T(8,128)(2,1)} %bitcast.10), calls=%async_computation | async-start | bytes 1048576 | tf_op jit(solution)/shard_map/all_to_all | solution.py:439
  12.8 1.4 %collective-permute-start.2 = (s16[3,128,128]{2,1,0:T(8,128)(2,1)S(1)}, s16[3,128,128]{2,1,0:T(8,128)(2,1)S(1)}, u32[]{:S(2)}, u32[]{:S(2)}) collective-permute-start(s16[3,128,128]{2,1,0:T(8,128)(2,1)S(1)} %get-tuple-element.26.flat_ref.flat0_ref), channel_id=1, source_target_pairs={{96,0},{112,16},{0,32},{16,48},{32,64},{48,80},{64,96},{80,112},{9... | collective-permute-start | bytes 294920 | tf_op jit(solution)/shard_map/ppermute | solution.py:434
  14.1 2.6 %collective-permute-start.1 = (s16[3,128,128]{2,1,0:T(8,128)(2,1)S(1)}, s16[3,128,128]{2,1,0:T(8,128)(2,1)S(1)}, u32[]{:S(2)}, u32[]{:S(2)}) collective-permute-start(s16[3,128,128]{2,1,0:T(8,128)(2,1)S(1)} %get-tuple-element.26.flat_ref.flat0_ref), channel_id=1, source_target_pairs={{64,0},{80,16},{96,32},{112,48},{0,64},{16,80},{32,96},{48,112},{6... | collective-permute-start | bytes 294920 | tf_op jit(solution)/shard_map/ppermute | solution.py:434
  16.8 1.1 %collective-permute-start = (s16[3,128,128]{2,1,0:T(8,128)(2,1)S(1)}, s16[3,128,128]{2,1,0:T(8,128)(2,1)S(1)}, u32[]{:S(2)}, u32[]{:S(2)}) collective-permute-start(s16[3,128,128]{2,1,0:T(8,128)(2,1)S(1)} %get-tuple-element.26.flat_ref.flat0_ref), channel_id=1, source_target_pairs={{32,0},{48,16},{64,32},{80,48},{96,64},{112,80},{0,96},{16,112},{3... | collective-permute-start | bytes 294920 | tf_op jit(solution)/shard_map/ppermute | solution.py:434
  17.8 3.1 %theory.2 = (f8e4m3fn[3,512,2048]{2,1,0:T(32,128)(4,1)}, f32[3,8,128]{2,1,0:T(8,128)}) custom-call(s16[3,128,128]{2,1,0:T(8,128)(2,1)S(1)} %get-tuple-element.26.flat_ref.flat0_ref), custom_call_target="tpu_custom_call" | custom-call | flops 2000000000 | bytes 6400000 | tf_op jit(solution)/shard_map/theory/pallas_call | solution.py:208
  20.9 0.0 collective-permute-done.2.flat3_ref
  20.9 0.0 collective-permute-done.1.flat2_ref
  20.9 0.2 collective-permute-done.flat_ref.flat1_ref
  21.1 2.1 %all-to-all-done = bf16[16,8,2048]{2,1,0:T(8,128)(2,1)S(1)} async-done(((bf16[16,8,2048]{2,1,0:T(8,128)(2,1)}), bf16[16,8,2048]{2,1,0:T(8,128)(2,1)S(1)}, u32[]{:S(2)}, u32[]{:S(2)}) %all-to-all-start) | async-done | bytes 524320 | tf_op jit(solution)/shard_map/all_to_all | solution.py:439
  23.3 0.0 copy-start
  23.3 2.0 %collective-permute-start.3 = (bf16[128,2048]{1,0:T(8,128)(2,1)S(1)}, bf16[128,2048]{1,0:T(8,128)(2,1)S(1)}, u32[]{:S(2)}, u32[]{:S(2)}) collective-permute-start(bf16[128,2048]{1,0:T(8,128)(2,1)S(1)} %bitcast.7), channel_id=1, source_target_pairs={{0,16},{16,0},{32,48},{48,32},{64,80},{80,64},{96,112},{112,96},{1... | collective-permute-start | bytes 1572872 | tf_op jit(solution)/shard_map/ppermute | solution.py:442
  25.3 2.2 %theory.3 = (f8e4m3fn[3,512,2048]{2,1,0:T(32,128)(4,1)S(1)}, f32[3,8,128]{2,1,0:T(8,128)S(1)}) custom-call(s16[3,128,128]{2,1,0:T(8,128)(2,1)S(1)} %collective-permute-done.flat_ref.flat1_ref), custom_call_target="tpu_custom_call" | custom-call | flops 2000000000 | bytes 6400000 | tf_op jit(solution)/shard_map/theory/pallas_call | solution.py:208
  27.5 0.0 collective-permute-done.3.other_ref
  27.5 0.0 copy-done
  27.5 10.3 %score.1 = f32[256,128]{1,0:T(8,128)S(1)} custom-call(s32[48]{0:T(128)S(1)} %copy-done, f8e4m3fn[3,512,2048]{2,1,0:T(32,128)(4,1)} %get-tuple-element.21.stored_hbm, f32[3,8,128]{2,1,0:T(8,128)} %get-tuple-element.22.stored_largest_hbm, f8e4m3fn[3,512,2048]{2,1,0:T(32,128)(4,1)S(1)} %get-tuple-element.24.theory_ref, ...), custom_call_target="tpu_custom_call" | custom-call | tf_op jit(solution)/shard_map/score/pallas_call | solution.py:444
  37.8 12.4 %all_to_all.23 = f32[32,8,128]{2,1,0:T(8,128)} all-to-all(f32[32,8,128]{2,1,0:T(8,128)S(1)} %bitcast.9), channel_id=1, replica_groups={{0,1,2,3,4,5,6,7,8,9,10,11,12,13,14,15,16,17,18,19,20,21,22,23,24,25,26..., dimensions={0} | all-to-all | bytes 262144 | tf_op jit(solution)/shard_map/all_to_all | solution.py:477
  50.2 1.7 %finish.1 = (f32[2,32]{1,0:T(2,128)}, f32[2,32]{1,0:T(2,128)}) custom-call(f32[8,128]{1,0:T(8,128)} %get-tuple-element.17.where_hbm, f32[256,128]{1,0:T(8,128)} %bitcast.11), custom_call_target="tpu_custom_call" | custom-call | tf_op jit(solution)/shard_map/finish/pallas_call | solution.py:485
Async XLA Ops:
  4.3 18.9 %all-to-all-start = ((bf16[16,8,2048]{2,1,0:T(8,128)(2,1)}), bf16[16,8,2048]{2,1,0:T(8,128)(2,1)S(1)}, u32[]{:S(2)}, u32[]{:S(2)}) async-start(bf16[16,8,2048]{2,1,0:T(8,128)(2,1)} %bitcast.10), calls=%async_computation | async-start | bytes 1048576 | tf_op jit(solution)/shard_map/all_to_all | solution.py:439
  12.8 8.2 %collective-permute-start.2 = (s16[3,128,128]{2,1,0:T(8,128)(2,1)S(1)}, s16[3,128,128]{2,1,0:T(8,128)(2,1)S(1)}, u32[]{:S(2)}, u32[]{:S(2)}) collective-permute-start(s16[3,128,128]{2,1,0:T(8,128)(2,1)S(1)} %get-tuple-element.26.flat_ref.flat0_ref), channel_id=1, source_target_pairs={{96,0},{112,16},{0,32},{16,48},{32,64},{48,80},{64,96},{80,112},{9... | collective-permute-start | bytes 294920 | tf_op jit(solution)/shard_map/ppermute | solution.py:434
  14.1 6.8 %collective-permute-start.1 = (s16[3,128,128]{2,1,0:T(8,128)(2,1)S(1)}, s16[3,128,128]{2,1,0:T(8,128)(2,1)S(1)}, u32[]{:S(2)}, u32[]{:S(2)}) collective-permute-start(s16[3,128,128]{2,1,0:T(8,128)(2,1)S(1)} %get-tuple-element.26.flat_ref.flat0_ref), channel_id=1, source_target_pairs={{64,0},{80,16},{96,32},{112,48},{0,64},{16,80},{32,96},{48,112},{6... | collective-permute-start | bytes 294920 | tf_op jit(solution)/shard_map/ppermute | solution.py:434
  16.8 4.4 %collective-permute-start = (s16[3,128,128]{2,1,0:T(8,128)(2,1)S(1)}, s16[3,128,128]{2,1,0:T(8,128)(2,1)S(1)}, u32[]{:S(2)}, u32[]{:S(2)}) collective-permute-start(s16[3,128,128]{2,1,0:T(8,128)(2,1)S(1)} %get-tuple-element.26.flat_ref.flat0_ref), channel_id=1, source_target_pairs={{32,0},{48,16},{64,32},{80,48},{96,64},{112,80},{0,96},{16,112},{3... | collective-permute-start | bytes 294920 | tf_op jit(solution)/shard_map/ppermute | solution.py:434
  23.3 4.2 %copy-start = (s32[48]{0:T(128)S(1)}, s32[48]{0:T(128)}, u32[]{:S(2)}) copy-start(s32[48]{0:T(128)} %counts_ref.1) | copy-start | bytes 580
  23.3 4.2 %collective-permute-start.3 = (bf16[128,2048]{1,0:T(8,128)(2,1)S(1)}, bf16[128,2048]{1,0:T(8,128)(2,1)S(1)}, u32[]{:S(2)}, u32[]{:S(2)}) collective-permute-start(bf16[128,2048]{1,0:T(8,128)(2,1)S(1)} %bitcast.7), channel_id=1, source_target_pairs={{0,16},{16,0},{32,48},{48,32},{64,80},{80,64},{96,112},{112,96},{1... | collective-permute-start | bytes 1572872 | tf_op jit(solution)/shard_map/ppermute | solution.py:442

commit v6 on v5

--- a/solution.py
+++ b/solution.py
@@ -75,13 +75,16 @@
     )
     taken = named & (earlier == (inner % 2).astype(jnp.float32))
     routing = jnp.where(taken, 1.0, 0.0).astype(jnp.bfloat16)
+    blocks = [padded[:, start : start + block + 2 * PAD] for start in range(0, width, block)]
+    background = jnp.dot(
+        jnp.concatenate(blocks, axis=0), band, preferred_element_type=jnp.float32
+    )
     leaving = []
     for start in range(0, width, block):
-        background = jnp.dot(
-            padded[:, start : start + block + 2 * PAD], band, preferred_element_type=jnp.float32
-        )
+        at = start // block * rows
         values = rooted[:, start : start + block].astype(jnp.float32)
-        prepared = (values - background / (2.0 * LAG)).astype(jnp.bfloat16)
+        prepared = values - background[at : at + rows] / (2.0 * LAG)
+        prepared = prepared.astype(jnp.bfloat16)
         prepared = (prepared.astype(jnp.float32) * scale).astype(jnp.bfloat16)
         out_ref[:, start : start + block] = jnp.dot(
             routing, prepared, preferred_element_type=jnp.float32
@@ -239,7 +242,6 @@
     halves,
     stats_ref,
     exact,
-    exact_rows,
     tables_ref,
     sems,
 ):
@@ -270,7 +272,6 @@
             at = half * 32
             halves[step, at : at + 32, :] = upper[rows_now]
             halves[step, 64 + at : 96 + at, :] = lower[rows_now]
-            exact_rows[step, at : at + 32, :] = values[rows_now].astype(jnp.bfloat16)
     small.wait()
 
     def reduced(scores, limit):
@@ -293,14 +294,11 @@
                 jnp.add, [item[row] for item in found]
             )
 
-    def window(step, carry):
+    def window(step, largest):
         live = counts_ref[mass * steps + step]
-        largest = jnp.maximum(
-            theory_of(flat2_ref[step].astype(jnp.int32), built2),
-            theory_of(flat3_ref[step].astype(jnp.int32), built3),
-        )
+        largest = jnp.maximum(largest, theory_of(flat2_ref[step].astype(jnp.int32), built2))
+        largest = jnp.maximum(largest, theory_of(flat3_ref[step].astype(jnp.int32), built3))
         largest = jnp.maximum(largest, jnp.maximum(held_largest[step], largest_ref[step]))
-        beyond = jnp.max(largest) > 16.0
         copy_of(step).wait()
         found = []
         for turn, theory in enumerate((held.at[step], theory_ref.at[step], built2, built3)):
@@ -313,36 +311,51 @@
             scores = scores + pltpu.roll(scores, 64, 1) * (1.0 / 32.0)
             found.append(reduced(scores, live - base_of(turn)))
         keep(step, found)
-
-        @pl.when(beyond)
-        def _():
-            for turn in range(4):
-                tables_ref[turn] = flats[turn][step].astype(jnp.int32)
-            values = exact_rows[step]
-            values = jnp.concatenate([values, jnp.zeros_like(values)], axis=0)
-
-            def piece(turn, found):
-                theory_of(tables_ref[turn], exact)
-                scores = lax.dot_general(
-                    exact[...],
-                    values,
-                    (((1,), (1,)), ((), ())),
-                    preferred_element_type=jnp.float32,
-                )
-                more = reduced(scores, live - base_of(turn))
-                return (
-                    jnp.maximum(found[0], more[0]),
-                    found[1] + more[1],
-                    found[2] + more[2],
-                )
-
-            zeros = jnp.zeros((1, 128), jnp.float32)
-            keep(step, [lax.fori_loop(0, 4, piece, (zeros - 1e30, zeros, zeros))])
-
+        return largest
+
+    def exact_window(step, carry):
+        live = counts_ref[mass * steps + step]
+        for turn in range(4):
+            tables_ref[turn] = flats[turn][step].astype(jnp.int32)
+        own_entry = iota((64, rows), 0)
+        mine = (own_entry % 32 // 2) * SLOTS + step * 2 + own_entry % 2
+        mine = iota((64, rows), 1) == mine
+        values = sum(
+            jnp.dot(
+                jnp.where(mine & (own_entry // 32 == half), 1.0, 0.0).astype(jnp.bfloat16),
+                ref[...],
+                preferred_element_type=jnp.float32,
+            )
+            for half, ref in enumerate((own_ref, other_ref))
+        ).astype(jnp.bfloat16)
+        values = jnp.concatenate([values, jnp.zeros_like(values)], axis=0)
+
+        def piece(turn, found):
+            theory_of(tables_ref[turn], exact)
+            scores = lax.dot_general(
+                exact[...],
+                values,
+                (((1,), (1,)), ((), ())),
+                preferred_element_type=jnp.float32,
+            )
+            more = reduced(scores, live - base_of(turn))
+            return (
+                jnp.maximum(found[0], more[0]),
+                found[1] + more[1],
+                found[2] + more[2],
+            )
+
+        zeros = jnp.zeros((1, 128), jnp.float32)
+        keep(step, [lax.fori_loop(0, 4, piece, (zeros - 1e30, zeros, zeros))])
         return carry
 
     stats_ref[...] = jnp.zeros_like(stats_ref)
-    lax.fori_loop(0, steps, window, 0)
+    largest = lax.fori_loop(0, steps, window, jnp.zeros((8, 128), jnp.float32))
+
+    @pl.when(jnp.max(largest) > 16.0)
+    def _():
+        lax.fori_loop(0, steps, exact_window, 0)
+
     part = iota((8, 128), 1) // 32
     tiles = []
     for half in range(2):
@@ -454,7 +467,6 @@
             pltpu.VMEM((steps, 128, width), F8),
             pltpu.VMEM((steps, 8, 128), jnp.float32),
             pltpu.VMEM((512, width), jnp.bfloat16),
-            pltpu.VMEM((steps, 64, width), jnp.bfloat16),
             pltpu.VMEM((4, 128, 128), jnp.int32),
             pltpu.SemaphoreType.DMA((steps + 1,)),
         ],

time: 52.2 us -> 50.5 us (0.967)
  Pallas kernels: 21 us -> 19.4 us
    pallas_call x1, Pallas kernels: 3.68 us -> 2.54 us  [per_device(): pl.pallas_call(prepare_kernel, out_shape=(pltpu.HBM((mass_count * SLOTS,...]
  transfers between devices with their start and end apart: 5 -> 5, of which waited for: 2 -> 2; matrix products, arithmetic and copies ran while one was open for 0% -> 0% of each run, Pallas kernels for 10% -> 11%
where the time goes in v6:
time: 50.5 us; the launch traced here: 50.3 us
  Pallas kernels  19.4 us (38%)
  starting transfers between devices  15.5 us (31%)
  blocking collectives  12.4 us (25%)
  waiting for transfers between devices  2.34 us (5%)
  between operations  0.7 us (1%)
    all_to_all x1, blocking collectives, per_device(): lax.all_to_all(stats, ('spec', 'mass'), split_axis=0, concat_axis=0, tile...  12.4 us
    pallas_call x1, Pallas kernels, per_device(): pl.pallas_call(score_kernel, out_shape=jax.ShapeDtypeStruct((2 * mass_cou...  9.81 us
    all_to_all x1, starting transfers between devices, per_device(): lax.all_to_all(outgoing, 'mass', split_axis=0, concat_axis=0, tiled=True)  8.44 us
    pallas_call x2, Pallas kernels, build_theory(): pl.pallas_call(stored_theory_kernel if stored else theory_kernel, out_sha...  5.32 us
    ppermute x3, starting transfers between devices, per_device(): lax.ppermute(flat, 'spec', [((i + 2 * turn) % spec_count, i) for i in ran...  5.06 us
    pallas_call x1, Pallas kernels, per_device(): pl.pallas_call(prepare_kernel, out_shape=(pltpu.HBM((mass_count * SLOTS,...  2.54 us
    all_to_all x1, waiting for transfers between devices, per_device(): lax.all_to_all(outgoing, 'mass', split_axis=0, concat_axis=0, tiled=True)  2.14 us
    ppermute x1, starting transfers between devices, per_device(): other = lax.ppermute(own, 'spec', [(i, i ^ 1) for i in range(spec_count)])  1.98 us
  transfers between devices with their start and end apart: 5, of which 2 were waited for; matrix products, arithmetic and copies ran while one was open for 0% of the time, Pallas kernels for 11%

profile of v6, /device:TPU:1, one launch (start us, length us, event | category | flops | bytes accessed | tf_op | source)
XLA Modules:
  0.0 50.3 jit_solution(11391788798564835606)
XLA Ops:
  0.6 2.5 %prepare.1 = (bf16[128,2048]{1,0:T(8,128)(2,1)}, s16[3,128,128]{2,1,0:T(8,128)(2,1)S(1)}, f32[8,128]{1,0:T(8,128)}) custom-call(bf16[32,2048]{1,0:T(8,128)(2,1)} %spectra_hbm.1, s32[2,32]{1,0:T(2,128)} %bitcast.12, s32[3,32,512]{2,1,0:T(8,128)} %pep_hbm.1, s32[48]{0:T(128)} %counts_ref.1), custom_call_target="tpu_custom_call" | custom-call | tf_op jit(solution)/shard_map/prepare/pallas_call | solution.py:419
  3.2 8.4 %all-to-all-start = ((bf16[16,8,2048]{2,1,0:T(8,128)(2,1)}), bf16[16,8,2048]{2,1,0:T(8,128)(2,1)S(1)}, u32[]{:S(2)}, u32[]{:S(2)}) async-start(bf16[16,8,2048]{2,1,0:T(8,128)(2,1)} %bitcast.10), calls=%async_computation | async-start | bytes 1048576 | tf_op jit(solution)/shard_map/all_to_all | solution.py:452
  11.6 1.4 %collective-permute-start.2 = (s16[3,128,128]{2,1,0:T(8,128)(2,1)S(1)}, s16[3,128,128]{2,1,0:T(8,128)(2,1)S(1)}, u32[]{:S(2)}, u32[]{:S(2)}) collective-permute-start(s16[3,128,128]{2,1,0:T(8,128)(2,1)S(1)} %get-tuple-element.26.flat_ref.flat0_ref), channel_id=1, source_target_pairs={{96,0},{112,16},{0,32},{16,48},{32,64},{48,80},{64,96},{80,112},{9... | collective-permute-start | bytes 294920 | tf_op jit(solution)/shard_map/ppermute | solution.py:447
  13.0 2.6 %collective-permute-start.1 = (s16[3,128,128]{2,1,0:T(8,128)(2,1)S(1)}, s16[3,128,128]{2,1,0:T(8,128)(2,1)S(1)}, u32[]{:S(2)}, u32[]{:S(2)}) collective-permute-start(s16[3,128,128]{2,1,0:T(8,128)(2,1)S(1)} %get-tuple-element.26.flat_ref.flat0_ref), channel_id=1, source_target_pairs={{64,0},{80,16},{96,32},{112,48},{0,64},{16,80},{32,96},{48,112},{6... | collective-permute-start | bytes 294920 | tf_op jit(solution)/shard_map/ppermute | solution.py:447
  15.6 1.1 %collective-permute-start = (s16[3,128,128]{2,1,0:T(8,128)(2,1)S(1)}, s16[3,128,128]{2,1,0:T(8,128)(2,1)S(1)}, u32[]{:S(2)}, u32[]{:S(2)}) collective-permute-start(s16[3,128,128]{2,1,0:T(8,128)(2,1)S(1)} %get-tuple-element.26.flat_ref.flat0_ref), channel_id=1, source_target_pairs={{32,0},{48,16},{64,32},{80,48},{96,64},{112,80},{0,96},{16,112},{3... | collective-permute-start | bytes 294920 | tf_op jit(solution)/shard_map/ppermute | solution.py:447
  16.7 3.1 %theory.2 = (f8e4m3fn[3,512,2048]{2,1,0:T(32,128)(4,1)}, f32[3,8,128]{2,1,0:T(8,128)}) custom-call(s16[3,128,128]{2,1,0:T(8,128)(2,1)S(1)} %get-tuple-element.26.flat_ref.flat0_ref), custom_call_target="tpu_custom_call" | custom-call | flops 2000000000 | bytes 6400000 | tf_op jit(solution)/shard_map/theory/pallas_call | solution.py:211
  19.8 0.0 collective-permute-done.2.flat3_ref
  19.8 0.0 collective-permute-done.1.flat2_ref
  19.8 0.2 collective-permute-done.flat_ref.flat1_ref
  20.0 2.1 %all-to-all-done = bf16[16,8,2048]{2,1,0:T(8,128)(2,1)S(1)} async-done(((bf16[16,8,2048]{2,1,0:T(8,128)(2,1)}), bf16[16,8,2048]{2,1,0:T(8,128)(2,1)S(1)}, u32[]{:S(2)}, u32[]{:S(2)}) %all-to-all-start) | async-done | bytes 524320 | tf_op jit(solution)/shard_map/all_to_all | solution.py:452
  22.1 0.0 copy-start
  22.1 2.0 %collective-permute-start.3 = (bf16[128,2048]{1,0:T(8,128)(2,1)S(1)}, bf16[128,2048]{1,0:T(8,128)(2,1)S(1)}, u32[]{:S(2)}, u32[]{:S(2)}) collective-permute-start(bf16[128,2048]{1,0:T(8,128)(2,1)S(1)} %bitcast.7), channel_id=1, source_target_pairs={{0,16},{16,0},{32,48},{48,32},{64,80},{80,64},{96,112},{112,96},{1... | collective-permute-start | bytes 1572872 | tf_op jit(solution)/shard_map/ppermute | solution.py:455
  24.1 2.2 %theory.3 = (f8e4m3fn[3,512,2048]{2,1,0:T(32,128)(4,1)S(1)}, f32[3,8,128]{2,1,0:T(8,128)S(1)}) custom-call(s16[3,128,128]{2,1,0:T(8,128)(2,1)S(1)} %collective-permute-done.flat_ref.flat1_ref), custom_call_target="tpu_custom_call" | custom-call | flops 2000000000 | bytes 6400000 | tf_op jit(solution)/shard_map/theory/pallas_call | solution.py:211
  26.3 0.0 collective-permute-done.3.other_ref
  26.4 0.0 copy-done
  26.4 9.8 %score.1 = f32[256,128]{1,0:T(8,128)S(1)} custom-call(s32[48]{0:T(128)S(1)} %copy-done, f8e4m3fn[3,512,2048]{2,1,0:T(32,128)(4,1)} %get-tuple-element.21.stored_hbm, f32[3,8,128]{2,1,0:T(8,128)} %get-tuple-element.22.stored_largest_hbm, f8e4m3fn[3,512,2048]{2,1,0:T(32,128)(4,1)S(1)} %get-tuple-element.24.theory_ref, ...), custom_call_target="tpu_custom_call" | custom-call | tf_op jit(solution)/shard_map/score/pallas_call | solution.py:457
  36.2 12.4 %all_to_all.23 = f32[32,8,128]{2,1,0:T(8,128)} all-to-all(f32[32,8,128]{2,1,0:T(8,128)S(1)} %bitcast.9), channel_id=1, replica_groups={{0,1,2,3,4,5,6,7,8,9,10,11,12,13,14,15,16,17,18,19,20,21,22,23,24,25,26..., dimensions={0} | all-to-all | bytes 262144 | tf_op jit(solution)/shard_map/all_to_all | solution.py:489
  48.6 1.7 %finish.1 = (f32[2,32]{1,0:T(2,128)}, f32[2,32]{1,0:T(2,128)}) custom-call(f32[8,128]{1,0:T(8,128)} %get-tuple-element.17.where_hbm, f32[256,128]{1,0:T(8,128)} %bitcast.11), custom_call_target="tpu_custom_call" | custom-call | tf_op jit(solution)/shard_map/finish/pallas_call | solution.py:497
Async XLA Ops:
  3.2 19.0 %all-to-all-start = ((bf16[16,8,2048]{2,1,0:T(8,128)(2,1)}), bf16[16,8,2048]{2,1,0:T(8,128)(2,1)S(1)}, u32[]{:S(2)}, u32[]{:S(2)}) async-start(bf16[16,8,2048]{2,1,0:T(8,128)(2,1)} %bitcast.10), calls=%async_computation | async-start | bytes 1048576 | tf_op jit(solution)/shard_map/all_to_all | solution.py:452
  11.6 8.2 %collective-permute-start.2 = (s16[3,128,128]{2,1,0:T(8,128)(2,1)S(1)}, s16[3,128,128]{2,1,0:T(8,128)(2,1)S(1)}, u32[]{:S(2)}, u32[]{:S(2)}) collective-permute-start(s16[3,128,128]{2,1,0:T(8,128)(2,1)S(1)} %get-tuple-element.26.flat_ref.flat0_ref), channel_id=1, source_target_pairs={{96,0},{112,16},{0,32},{16,48},{32,64},{48,80},{64,96},{80,112},{9... | collective-permute-start | bytes 294920 | tf_op jit(solution)/shard_map/ppermute | solution.py:447
  13.0 6.8 %collective-permute-start.1 = (s16[3,128,128]{2,1,0:T(8,128)(2,1)S(1)}, s16[3,128,128]{2,1,0:T(8,128)(2,1)S(1)}, u32[]{:S(2)}, u32[]{:S(2)}) collective-permute-start(s16[3,128,128]{2,1,0:T(8,128)(2,1)S(1)} %get-tuple-element.26.flat_ref.flat0_ref), channel_id=1, source_target_pairs={{64,0},{80,16},{96,32},{112,48},{0,64},{16,80},{32,96},{48,112},{6... | collective-permute-start | bytes 294920 | tf_op jit(solution)/shard_map/ppermute | solution.py:447
  15.6 4.4 %collective-permute-start = (s16[3,128,128]{2,1,0:T(8,128)(2,1)S(1)}, s16[3,128,128]{2,1,0:T(8,128)(2,1)S(1)}, u32[]{:S(2)}, u32[]{:S(2)}) collective-permute-start(s16[3,128,128]{2,1,0:T(8,128)(2,1)S(1)} %get-tuple-element.26.flat_ref.flat0_ref), channel_id=1, source_target_pairs={{32,0},{48,16},{64,32},{80,48},{96,64},{112,80},{0,96},{16,112},{3... | collective-permute-start | bytes 294920 | tf_op jit(solution)/shard_map/ppermute | solution.py:447
  22.1 4.2 %copy-start = (s32[48]{0:T(128)S(1)}, s32[48]{0:T(128)}, u32[]{:S(2)}) copy-start(s32[48]{0:T(128)} %counts_ref.1) | copy-start | bytes 580
  22.1 4.2 %collective-permute-start.3 = (bf16[128,2048]{1,0:T(8,128)(2,1)S(1)}, bf16[128,2048]{1,0:T(8,128)(2,1)S(1)}, u32[]{:S(2)}, u32[]{:S(2)}) collective-permute-start(bf16[128,2048]{1,0:T(8,128)(2,1)S(1)} %bitcast.7), channel_id=1, source_target_pairs={{0,16},{16,0},{32,48},{48,32},{64,80},{80,64},{96,112},{112,96},{1... | collective-permute-start | bytes 1572872 | tf_op jit(solution)/shard_map/ppermute | solution.py:455

commit v7 on v6

--- a/solution.py
+++ b/solution.py
@@ -97,7 +97,6 @@
         )
         leaving[-1].start()
     copies[3].wait()
-    mass = lax.axis_index("mass")
     windows = counts_ref.shape[0]
     named_by = routes_ref[...]
     live = jnp.zeros(named_by.shape, jnp.int32)
@@ -112,7 +111,7 @@
         found = jnp.sum(jnp.where(mine, place, 0), axis=0, keepdims=True)
         lanes = slice(pick * rows, (pick + 1) * rows)
         inside = found % SLOTS
-        where_ref[0:1, lanes] = ((inside // 2) * 32 + mass * 2 + inside % 2).astype(jnp.float32)
+        where_ref[0:1, lanes] = ((inside // 2) * 32 + inside % 2).astype(jnp.float32)
         where_ref[1:2, lanes] = (found // SLOTS).astype(jnp.float32)
         where_ref[2:3, lanes] = live[pick : pick + 1].astype(jnp.float32)
         where_ref[3:4, lanes] = turned_scale
@@ -357,6 +356,7 @@
         lax.fori_loop(0, steps, exact_window, 0)
 
     part = iota((8, 128), 1) // 32
+    place = iota((1, 128), 1) % 32 // 4
     tiles = []
     for half in range(2):
         tile = jnp.zeros((8, 128), jnp.float32)
@@ -366,10 +366,15 @@
         tiles.append(tile)
     first = jnp.where(core == 0, tiles[0], tiles[1])
     second = jnp.where(core == 0, tiles[1], tiles[0])
-    peers = out_ref.shape[0] // 16
-    for peer in range(peers):
-        out_ref[peer * 8 : peer * 8 + 8, :] = first
-        out_ref[(peers + peer) * 8 : (peers + peer) * 8 + 8, :] = second
+    peers = out_ref.shape[0] // 2
+    for half, tile in enumerate((first, second)):
+        for peer in range(peers):
+            row = jnp.zeros((1, 128), jnp.float32)
+            for stat in range(3):
+                moved = pltpu.roll(tile, (4 * stat - 2 * peer) % 128, 1)[stat : stat + 1]
+                row = jnp.where(place == stat, moved, row)
+            at = half * peers + peer
+            out_ref[at : at + 1, :] = row
 
 
 def finish_kernel(where_hbm, stats_hbm, best_ref, z_ref, where_ref, stats_ref, sems):
@@ -382,22 +387,23 @@
     for copy in copies:
         copy.wait()
     rows = best_ref.shape[1]
-    peers = stats_ref.shape[0] // 16
-    lane = jnp.broadcast_to(where_ref[0:1, :].astype(jnp.int32), (8, 128))
+    peers = stats_ref.shape[0] // 2
+    lane = where_ref[0:1, :].astype(jnp.int32)
     shard = where_ref[1:2, :].astype(jnp.int32)
     live = where_ref[2:3, :]
     unscale = 1.0 / (where_ref[3:4, :] * 32.0)
-    halves = []
-    for half in range(2):
-        chosen = jnp.zeros((8, 128), jnp.float32)
-        for peer in range(peers):
-            at = (half * peers + peer) * 8
-            found = jnp.take_along_axis(stats_ref[at : at + 8, :], lane, axis=1)
-            chosen = jnp.where(shard == peer, found, chosen)
-        halves.append(chosen)
-    best = jnp.maximum(halves[0][0:1], halves[1][0:1]) * unscale
-    total = (halves[0][1:2] + halves[1][1:2]) * unscale
-    square = (halves[0][2:3] + halves[1][2:3]) * unscale * unscale
+    mine = iota((peers, 128), 0) == shard
+    picked = []
+    for stat in range(3):
+        index = jnp.broadcast_to(lane + 4 * stat, (peers, 128))
+        for half in range(2):
+            found = jnp.take_along_axis(
+                stats_ref[half * peers : (half + 1) * peers, :], index, axis=1
+            )
+            picked.append(jnp.sum(jnp.where(mine, found, 0.0), axis=0, keepdims=True))
+    best = jnp.maximum(picked[0], picked[1]) * unscale
+    total = (picked[2] + picked[3]) * unscale
+    square = (picked[4] + picked[5]) * unscale * unscale
     mean = total / live
     spread = square / live - mean * mean
     z = (best - mean) / jnp.sqrt(spread + EPS)
@@ -456,7 +462,7 @@
     second, second_largest = build_theory(flats[1], width, False)
     stats = pl.pallas_call(
         score_kernel,
-        out_shape=jax.ShapeDtypeStruct((2 * mass_count * 8, 128), jnp.float32),
+        out_shape=jax.ShapeDtypeStruct((2 * mass_count, 128), jnp.float32),
         in_specs=[smem, hbm, hbm] + [vmem] * 8,
         out_specs=vmem,
         scratch_shapes=[

time: 50.5 us -> 49.6 us (0.982)
  blocking collectives: 12.4 us -> 11.6 us
    all_to_all x1, blocking collectives: 12.4 us -> 11.6 us  [per_device(): lax.all_to_all(stats, ('spec', 'mass'), split_axis=0, concat_axis=0, tile...]
where the time goes in v7:
time: 49.6 us; the launch traced here: 49.3 us
  Pallas kernels  19.2 us (39%)
  starting transfers between devices  15.5 us (31%)
  blocking collectives  11.6 us (23%)
  waiting for transfers between devices  2.34 us (5%)
  between operations  0.7 us (1%)
    all_to_all x1, blocking collectives, per_device(): lax.all_to_all(stats, ('spec', 'mass'), split_axis=0, concat_axis=0, tile...  11.6 us
    pallas_call x1, Pallas kernels, per_device(): pl.pallas_call(score_kernel, out_shape=jax.ShapeDtypeStruct((2 * mass_cou...  9.91 us
    all_to_all x1, starting transfers between devices, per_device(): lax.all_to_all(outgoing, 'mass', split_axis=0, concat_axis=0, tiled=True)  8.44 us
    pallas_call x2, Pallas kernels, build_theory(): pl.pallas_call(stored_theory_kernel if stored else theory_kernel, out_sha...  5.32 us
    ppermute x3, starting transfers between devices, per_device(): lax.ppermute(flat, 'spec', [((i + 2 * turn) % spec_count, i) for i in ran...  5.06 us
    pallas_call x1, Pallas kernels, per_device(): pl.pallas_call(prepare_kernel, out_shape=(pltpu.HBM((mass_count * SLOTS,...  2.51 us
    all_to_all x1, waiting for transfers between devices, per_device(): lax.all_to_all(outgoing, 'mass', split_axis=0, concat_axis=0, tiled=True)  2.14 us
    ppermute x1, starting transfers between devices, per_device(): other = lax.ppermute(own, 'spec', [(i, i ^ 1) for i in range(spec_count)])  1.98 us
  transfers between devices with their start and end apart: 5, of which 2 were waited for; matrix products, arithmetic and copies ran while one was open for 0% of the time, Pallas kernels for 11%

profile of v7, /device:TPU:1, one launch (start us, length us, event | category | flops | bytes accessed | tf_op | source)
XLA Modules:
  0.0 49.3 jit_solution(16614354956023553279)
XLA Ops:
  0.6 2.5 %prepare.1 = (bf16[128,2048]{1,0:T(8,128)(2,1)}, s16[3,128,128]{2,1,0:T(8,128)(2,1)S(1)}, f32[8,128]{1,0:T(8,128)}) custom-call(bf16[32,2048]{1,0:T(8,128)(2,1)} %spectra_hbm.1, s32[2,32]{1,0:T(2,128)} %bitcast.14, s32[3,32,512]{2,1,0:T(8,128)} %pep_hbm.1, s32[48]{0:T(128)} %counts_ref.1), custom_call_target="tpu_custom_call" | custom-call | tf_op jit(solution)/shard_map/prepare/pallas_call | solution.py:425
  3.1 8.4 %all-to-all-start = ((bf16[16,8,2048]{2,1,0:T(8,128)(2,1)}), bf16[16,8,2048]{2,1,0:T(8,128)(2,1)S(1)}, u32[]{:S(2)}, u32[]{:S(2)}) async-start(bf16[16,8,2048]{2,1,0:T(8,128)(2,1)} %bitcast.12), calls=%async_computation | async-start | bytes 1048576 | tf_op jit(solution)/shard_map/all_to_all | solution.py:458
  11.6 1.4 %collective-permute-start.2 = (s16[3,128,128]{2,1,0:T(8,128)(2,1)S(1)}, s16[3,128,128]{2,1,0:T(8,128)(2,1)S(1)}, u32[]{:S(2)}, u32[]{:S(2)}) collective-permute-start(s16[3,128,128]{2,1,0:T(8,128)(2,1)S(1)} %get-tuple-element.26.flat_ref.flat0_ref), channel_id=1, source_target_pairs={{96,0},{112,16},{0,32},{16,48},{32,64},{48,80},{64,96},{80,112},{9... | collective-permute-start | bytes 294920 | tf_op jit(solution)/shard_map/ppermute | solution.py:453
  13.0 2.6 %collective-permute-start.1 = (s16[3,128,128]{2,1,0:T(8,128)(2,1)S(1)}, s16[3,128,128]{2,1,0:T(8,128)(2,1)S(1)}, u32[]{:S(2)}, u32[]{:S(2)}) collective-permute-start(s16[3,128,128]{2,1,0:T(8,128)(2,1)S(1)} %get-tuple-element.26.flat_ref.flat0_ref), channel_id=1, source_target_pairs={{64,0},{80,16},{96,32},{112,48},{0,64},{16,80},{32,96},{48,112},{6... | collective-permute-start | bytes 294920 | tf_op jit(solution)/shard_map/ppermute | solution.py:453
  15.6 1.1 %collective-permute-start = (s16[3,128,128]{2,1,0:T(8,128)(2,1)S(1)}, s16[3,128,128]{2,1,0:T(8,128)(2,1)S(1)}, u32[]{:S(2)}, u32[]{:S(2)}) collective-permute-start(s16[3,128,128]{2,1,0:T(8,128)(2,1)S(1)} %get-tuple-element.26.flat_ref.flat0_ref), channel_id=1, source_target_pairs={{32,0},{48,16},{64,32},{80,48},{96,64},{112,80},{0,96},{16,112},{3... | collective-permute-start | bytes 294920 | tf_op jit(solution)/shard_map/ppermute | solution.py:453
  16.6 3.1 %theory.2 = (f8e4m3fn[3,512,2048]{2,1,0:T(32,128)(4,1)}, f32[3,8,128]{2,1,0:T(8,128)}) custom-call(s16[3,128,128]{2,1,0:T(8,128)(2,1)S(1)} %get-tuple-element.26.flat_ref.flat0_ref), custom_call_target="tpu_custom_call" | custom-call | flops 2000000000 | bytes 6400000 | tf_op jit(solution)/shard_map/theory/pallas_call | solution.py:210
  19.7 0.0 collective-permute-done.2.flat3_ref
  19.8 0.0 collective-permute-done.1.flat2_ref
  19.8 0.2 collective-permute-done.flat_ref.flat1_ref
  20.0 2.1 %all-to-all-done = bf16[16,8,2048]{2,1,0:T(8,128)(2,1)S(1)} async-done(((bf16[16,8,2048]{2,1,0:T(8,128)(2,1)}), bf16[16,8,2048]{2,1,0:T(8,128)(2,1)S(1)}, u32[]{:S(2)}, u32[]{:S(2)}) %all-to-all-start) | async-done | bytes 524320 | tf_op jit(solution)/shard_map/all_to_all | solution.py:458
  22.1 0.0 copy-start
  22.1 2.0 %collective-permute-start.3 = (bf16[128,2048]{1,0:T(8,128)(2,1)S(1)}, bf16[128,2048]{1,0:T(8,128)(2,1)S(1)}, u32[]{:S(2)}, u32[]{:S(2)}) collective-permute-start(bf16[128,2048]{1,0:T(8,128)(2,1)S(1)} %bitcast.9), channel_id=1, source_target_pairs={{0,16},{16,0},{32,48},{48,32},{64,80},{80,64},{96,112},{112,96},{1... | collective-permute-start | bytes 1572872 | tf_op jit(solution)/shard_map/ppermute | solution.py:461
  24.1 2.2 %theory.3 = (f8e4m3fn[3,512,2048]{2,1,0:T(32,128)(4,1)S(1)}, f32[3,8,128]{2,1,0:T(8,128)S(1)}) custom-call(s16[3,128,128]{2,1,0:T(8,128)(2,1)S(1)} %collective-permute-done.flat_ref.flat1_ref), custom_call_target="tpu_custom_call" | custom-call | flops 2000000000 | bytes 6400000 | tf_op jit(solution)/shard_map/theory/pallas_call | solution.py:210
  26.3 0.0 collective-permute-done.3.other_ref
  26.3 0.0 copy-done
  26.3 9.9 %score.1 = f32[32,128]{1,0:T(8,128)S(1)} custom-call(s32[48]{0:T(128)S(1)} %copy-done, f8e4m3fn[3,512,2048]{2,1,0:T(32,128)(4,1)} %get-tuple-element.21.stored_hbm, f32[3,8,128]{2,1,0:T(8,128)} %get-tuple-element.22.stored_largest_hbm, f8e4m3fn[3,512,2048]{2,1,0:T(32,128)(4,1)S(1)} %get-tuple-element.24.theory_ref, ...), custom_call_target="tpu_custom_call" | custom-call | tf_op jit(solution)/shard_map/score/pallas_call | solution.py:463
  36.3 11.6 %all_to_all.23 = f32[32,1,128]{2,1,0:T(1,128)} all-to-all(f32[32,1,128]{2,1,0:T(1,128)S(1)} %bitcast.11), channel_id=1, replica_groups={{0,1,2,3,4,5,6,7,8,9,10,11,12,13,14,15,16,17,18,19,20,21,22,23,24,25,26..., dimensions={0} | all-to-all | bytes 32768 | tf_op jit(solution)/shard_map/all_to_all | solution.py:495
  47.8 1.5 %finish.1 = (f32[2,32]{1,0:T(2,128)}, f32[2,32]{1,0:T(2,128)}) custom-call(f32[8,128]{1,0:T(8,128)} %get-tuple-element.17.where_hbm, f32[32,128]{1,0:T(8,128)} %bitcast.13), custom_call_target="tpu_custom_call" | custom-call | tf_op jit(solution)/shard_map/finish/pallas_call | solution.py:503
Async XLA Ops:
  3.1 19.0 %all-to-all-start = ((bf16[16,8,2048]{2,1,0:T(8,128)(2,1)}), bf16[16,8,2048]{2,1,0:T(8,128)(2,1)S(1)}, u32[]{:S(2)}, u32[]{:S(2)}) async-start(bf16[16,8,2048]{2,1,0:T(8,128)(2,1)} %bitcast.12), calls=%async_computation | async-start | bytes 1048576 | tf_op jit(solution)/shard_map/all_to_all | solution.py:458
  11.6 8.2 %collective-permute-start.2 = (s16[3,128,128]{2,1,0:T(8,128)(2,1)S(1)}, s16[3,128,128]{2,1,0:T(8,128)(2,1)S(1)}, u32[]{:S(2)}, u32[]{:S(2)}) collective-permute-start(s16[3,128,128]{2,1,0:T(8,128)(2,1)S(1)} %get-tuple-element.26.flat_ref.flat0_ref), channel_id=1, source_target_pairs={{96,0},{112,16},{0,32},{16,48},{32,64},{48,80},{64,96},{80,112},{9... | collective-permute-start | bytes 294920 | tf_op jit(solution)/shard_map/ppermute | solution.py:453
  13.0 6.8 %collective-permute-start.1 = (s16[3,128,128]{2,1,0:T(8,128)(2,1)S(1)}, s16[3,128,128]{2,1,0:T(8,128)(2,1)S(1)}, u32[]{:S(2)}, u32[]{:S(2)}) collective-permute-start(s16[3,128,128]{2,1,0:T(8,128)(2,1)S(1)} %get-tuple-element.26.flat_ref.flat0_ref), channel_id=1, source_target_pairs={{64,0},{80,16},{96,32},{112,48},{0,64},{16,80},{32,96},{48,112},{6... | collective-permute-start | bytes 294920 | tf_op jit(solution)/shard_map/ppermute | solution.py:453
  15.6 4.4 %collective-permute-start = (s16[3,128,128]{2,1,0:T(8,128)(2,1)S(1)}, s16[3,128,128]{2,1,0:T(8,128)(2,1)S(1)}, u32[]{:S(2)}, u32[]{:S(2)}) collective-permute-start(s16[3,128,128]{2,1,0:T(8,128)(2,1)S(1)} %get-tuple-element.26.flat_ref.flat0_ref), channel_id=1, source_target_pairs={{32,0},{48,16},{64,32},{80,48},{96,64},{112,80},{0,96},{16,112},{3... | collective-permute-start | bytes 294920 | tf_op jit(solution)/shard_map/ppermute | solution.py:453
  22.1 4.2 %copy-start = (s32[48]{0:T(128)S(1)}, s32[48]{0:T(128)}, u32[]{:S(2)}) copy-start(s32[48]{0:T(128)} %counts_ref.1) | copy-start | bytes 580
  22.1 4.2 %collective-permute-start.3 = (bf16[128,2048]{1,0:T(8,128)(2,1)S(1)}, bf16[128,2048]{1,0:T(8,128)(2,1)S(1)}, u32[]{:S(2)}, u32[]{:S(2)}) collective-permute-start(bf16[128,2048]{1,0:T(8,128)(2,1)S(1)} %bitcast.9), channel_id=1, source_target_pairs={{0,16},{16,0},{32,48},{48,32},{64,80},{80,64},{96,112},{112,96},{1... | collective-permute-start | bytes 1572872 | tf_op jit(solution)/shard_map/ppermute | solution.py:461

commit v8 on v7

--- a/solution.py
+++ b/solution.py
@@ -169,7 +169,8 @@
         largest_ref[step] = theory_of(flat_ref[step].astype(jnp.int32), theory_ref.at[step])
         return carry
 
-    lax.fori_loop(0, flat_ref.shape[0], window, 0)
+    for step in range(flat_ref.shape[0]):
+        window(step, 0)
 
 
 def stored_theory_kernel(flat_ref, theory_hbm, largest_hbm, held, largest, sems):
@@ -189,7 +190,8 @@
         )
         return carry
 
-    lax.fori_loop(0, steps, window, 0)
+    for step in range(steps):
+        window(step, 0)
     last = pltpu.make_async_copy(largest, largest_hbm, sems.at[steps, 0])
     last.start()
     for step in range(steps):

time: 49.6 us -> 49.4 us (level)
  transfers between devices with their start and end apart: 5 -> 5, of which waited for: 2 -> 2; matrix products, arithmetic and copies ran while one was open for 0% -> 0% of each run, Pallas kernels for 11% -> 10%
where the time goes in v8:
time: 49.4 us; the launch traced here: 49.1 us
  Pallas kernels  18.8 us (38%)
  starting transfers between devices  15.5 us (31%)
  blocking collectives  11.6 us (23%)
  waiting for transfers between devices  2.55 us (5%)
  between operations  0.69 us (1%)
    all_to_all x1, blocking collectives, per_device(): lax.all_to_all(stats, ('spec', 'mass'), split_axis=0, concat_axis=0, tile...  11.6 us
    pallas_call x1, Pallas kernels, per_device(): pl.pallas_call(score_kernel, out_shape=jax.ShapeDtypeStruct((2 * mass_cou...  9.91 us
    all_to_all x1, starting transfers between devices, per_device(): lax.all_to_all(outgoing, 'mass', split_axis=0, concat_axis=0, tiled=True)  8.44 us
    ppermute x3, starting transfers between devices, per_device(): lax.ppermute(flat, 'spec', [((i + 2 * turn) % spec_count, i) for i in ran...  5.06 us
    pallas_call x2, Pallas kernels, build_theory(): pl.pallas_call(stored_theory_kernel if stored else theory_kernel, out_sha...  4.91 us
    pallas_call x1, Pallas kernels, per_device(): pl.pallas_call(prepare_kernel, out_shape=(pltpu.HBM((mass_count * SLOTS,...  2.51 us
    all_to_all x1, waiting for transfers between devices, per_device(): lax.all_to_all(outgoing, 'mass', split_axis=0, concat_axis=0, tiled=True)  2.14 us
    ppermute x1, starting transfers between devices, per_device(): other = lax.ppermute(own, 'spec', [(i, i ^ 1) for i in range(spec_count)])  1.98 us
  transfers between devices with their start and end apart: 5, of which 2 were waited for; matrix products, arithmetic and copies ran while one was open for 0% of the time, Pallas kernels for 10%

profile of v8, /device:TPU:1, one launch (start us, length us, event | category | flops | bytes accessed | tf_op | source)
XLA Modules:
  0.0 49.1 jit_solution(8257707583634128070)
XLA Ops:
  0.6 2.5 %prepare.1 = (bf16[128,2048]{1,0:T(8,128)(2,1)}, s16[3,128,128]{2,1,0:T(8,128)(2,1)S(1)}, f32[8,128]{1,0:T(8,128)}) custom-call(bf16[32,2048]{1,0:T(8,128)(2,1)} %spectra_hbm.1, s32[2,32]{1,0:T(2,128)} %bitcast.14, s32[3,32,512]{2,1,0:T(8,128)} %pep_hbm.1, s32[48]{0:T(128)} %counts_ref.1), custom_call_target="tpu_custom_call" | custom-call | tf_op jit(solution)/shard_map/prepare/pallas_call | solution.py:427
  3.1 8.4 %all-to-all-start = ((bf16[16,8,2048]{2,1,0:T(8,128)(2,1)}), bf16[16,8,2048]{2,1,0:T(8,128)(2,1)S(1)}, u32[]{:S(2)}, u32[]{:S(2)}) async-start(bf16[16,8,2048]{2,1,0:T(8,128)(2,1)} %bitcast.12), calls=%async_computation | async-start | bytes 1048576 | tf_op jit(solution)/shard_map/all_to_all | solution.py:460
  11.6 1.4 %collective-permute-start.2 = (s16[3,128,128]{2,1,0:T(8,128)(2,1)S(1)}, s16[3,128,128]{2,1,0:T(8,128)(2,1)S(1)}, u32[]{:S(2)}, u32[]{:S(2)}) collective-permute-start(s16[3,128,128]{2,1,0:T(8,128)(2,1)S(1)} %get-tuple-element.26.flat_ref.flat0_ref), channel_id=1, source_target_pairs={{96,0},{112,16},{0,32},{16,48},{32,64},{48,80},{64,96},{80,112},{9... | collective-permute-start | bytes 294920 | tf_op jit(solution)/shard_map/ppermute | solution.py:455
  13.0 2.6 %collective-permute-start.1 = (s16[3,128,128]{2,1,0:T(8,128)(2,1)S(1)}, s16[3,128,128]{2,1,0:T(8,128)(2,1)S(1)}, u32[]{:S(2)}, u32[]{:S(2)}) collective-permute-start(s16[3,128,128]{2,1,0:T(8,128)(2,1)S(1)} %get-tuple-element.26.flat_ref.flat0_ref), channel_id=1, source_target_pairs={{64,0},{80,16},{96,32},{112,48},{0,64},{16,80},{32,96},{48,112},{6... | collective-permute-start | bytes 294920 | tf_op jit(solution)/shard_map/ppermute | solution.py:455
  15.6 1.1 %collective-permute-start = (s16[3,128,128]{2,1,0:T(8,128)(2,1)S(1)}, s16[3,128,128]{2,1,0:T(8,128)(2,1)S(1)}, u32[]{:S(2)}, u32[]{:S(2)}) collective-permute-start(s16[3,128,128]{2,1,0:T(8,128)(2,1)S(1)} %get-tuple-element.26.flat_ref.flat0_ref), channel_id=1, source_target_pairs={{32,0},{48,16},{64,32},{80,48},{96,64},{112,80},{0,96},{16,112},{3... | collective-permute-start | bytes 294920 | tf_op jit(solution)/shard_map/ppermute | solution.py:455
  16.6 2.9 %theory.2 = (f8e4m3fn[3,512,2048]{2,1,0:T(32,128)(4,1)}, f32[3,8,128]{2,1,0:T(8,128)}) custom-call(s16[3,128,128]{2,1,0:T(8,128)(2,1)S(1)} %get-tuple-element.26.flat_ref.flat0_ref), custom_call_target="tpu_custom_call" | custom-call | flops 2000000000 | bytes 6400000 | tf_op jit(solution)/shard_map/theory/pallas_call | solution.py:212
  19.5 0.0 collective-permute-done.2.flat3_ref
  19.6 0.0 collective-permute-done.1.flat2_ref
  19.6 0.4 collective-permute-done.flat_ref.flat1_ref
  20.0 2.1 %all-to-all-done = bf16[16,8,2048]{2,1,0:T(8,128)(2,1)S(1)} async-done(((bf16[16,8,2048]{2,1,0:T(8,128)(2,1)}), bf16[16,8,2048]{2,1,0:T(8,128)(2,1)S(1)}, u32[]{:S(2)}, u32[]{:S(2)}) %all-to-all-start) | async-done | bytes 524320 | tf_op jit(solution)/shard_map/all_to_all | solution.py:460
  22.1 0.0 copy-start
  22.1 2.0 %collective-permute-start.3 = (bf16[128,2048]{1,0:T(8,128)(2,1)S(1)}, bf16[128,2048]{1,0:T(8,128)(2,1)S(1)}, u32[]{:S(2)}, u32[]{:S(2)}) collective-permute-start(bf16[128,2048]{1,0:T(8,128)(2,1)S(1)} %bitcast.9), channel_id=1, source_target_pairs={{0,16},{16,0},{32,48},{48,32},{64,80},{80,64},{96,112},{112,96},{1... | collective-permute-start | bytes 1572872 | tf_op jit(solution)/shard_map/ppermute | solution.py:463
  24.1 2.0 %theory.3 = (f8e4m3fn[3,512,2048]{2,1,0:T(32,128)(4,1)S(1)}, f32[3,8,128]{2,1,0:T(8,128)S(1)}) custom-call(s16[3,128,128]{2,1,0:T(8,128)(2,1)S(1)} %collective-permute-done.flat_ref.flat1_ref), custom_call_target="tpu_custom_call" | custom-call | flops 2000000000 | bytes 6400000 | tf_op jit(solution)/shard_map/theory/pallas_call | solution.py:212
  26.1 0.0 collective-permute-done.3.other_ref
  26.1 0.0 copy-done
  26.1 9.9 %score.1 = f32[32,128]{1,0:T(8,128)S(1)} custom-call(s32[48]{0:T(128)S(1)} %copy-done, f8e4m3fn[3,512,2048]{2,1,0:T(32,128)(4,1)} %get-tuple-element.21.stored_hbm, f32[3,8,128]{2,1,0:T(8,128)} %get-tuple-element.22.stored_largest_hbm, f8e4m3fn[3,512,2048]{2,1,0:T(32,128)(4,1)S(1)} %get-tuple-element.24.theory_ref, ...), custom_call_target="tpu_custom_call" | custom-call | tf_op jit(solution)/shard_map/score/pallas_call | solution.py:465
  36.0 11.6 %all_to_all.23 = f32[32,1,128]{2,1,0:T(1,128)} all-to-all(f32[32,1,128]{2,1,0:T(1,128)S(1)} %bitcast.11), channel_id=1, replica_groups={{0,1,2,3,4,5,6,7,8,9,10,11,12,13,14,15,16,17,18,19,20,21,22,23,24,25,26..., dimensions={0} | all-to-all | bytes 32768 | tf_op jit(solution)/shard_map/all_to_all | solution.py:497
  47.6 1.5 %finish.1 = (f32[2,32]{1,0:T(2,128)}, f32[2,32]{1,0:T(2,128)}) custom-call(f32[8,128]{1,0:T(8,128)} %get-tuple-element.17.where_hbm, f32[32,128]{1,0:T(8,128)} %bitcast.13), custom_call_target="tpu_custom_call" | custom-call | tf_op jit(solution)/shard_map/finish/pallas_call | solution.py:505
Async XLA Ops:
  3.1 19.0 %all-to-all-start = ((bf16[16,8,2048]{2,1,0:T(8,128)(2,1)}), bf16[16,8,2048]{2,1,0:T(8,128)(2,1)S(1)}, u32[]{:S(2)}, u32[]{:S(2)}) async-start(bf16[16,8,2048]{2,1,0:T(8,128)(2,1)} %bitcast.12), calls=%async_computation | async-start | bytes 1048576 | tf_op jit(solution)/shard_map/all_to_all | solution.py:460
  11.6 8.0 %collective-permute-start.2 = (s16[3,128,128]{2,1,0:T(8,128)(2,1)S(1)}, s16[3,128,128]{2,1,0:T(8,128)(2,1)S(1)}, u32[]{:S(2)}, u32[]{:S(2)}) collective-permute-start(s16[3,128,128]{2,1,0:T(8,128)(2,1)S(1)} %get-tuple-element.26.flat_ref.flat0_ref), channel_id=1, source_target_pairs={{96,0},{112,16},{0,32},{16,48},{32,64},{48,80},{64,96},{80,112},{9... | collective-permute-start | bytes 294920 | tf_op jit(solution)/shard_map/ppermute | solution.py:455
  13.0 6.6 %collective-permute-start.1 = (s16[3,128,128]{2,1,0:T(8,128)(2,1)S(1)}, s16[3,128,128]{2,1,0:T(8,128)(2,1)S(1)}, u32[]{:S(2)}, u32[]{:S(2)}) collective-permute-start(s16[3,128,128]{2,1,0:T(8,128)(2,1)S(1)} %get-tuple-element.26.flat_ref.flat0_ref), channel_id=1, source_target_pairs={{64,0},{80,16},{96,32},{112,48},{0,64},{16,80},{32,96},{48,112},{6... | collective-permute-start | bytes 294920 | tf_op jit(solution)/shard_map/ppermute | solution.py:455
  15.6 4.4 %collective-permute-start = (s16[3,128,128]{2,1,0:T(8,128)(2,1)S(1)}, s16[3,128,128]{2,1,0:T(8,128)(2,1)S(1)}, u32[]{:S(2)}, u32[]{:S(2)}) collective-permute-start(s16[3,128,128]{2,1,0:T(8,128)(2,1)S(1)} %get-tuple-element.26.flat_ref.flat0_ref), channel_id=1, source_target_pairs={{32,0},{48,16},{64,32},{80,48},{96,64},{112,80},{0,96},{16,112},{3... | collective-permute-start | bytes 294920 | tf_op jit(solution)/shard_map/ppermute | solution.py:455
  22.1 4.0 %copy-start = (s32[48]{0:T(128)S(1)}, s32[48]{0:T(128)}, u32[]{:S(2)}) copy-start(s32[48]{0:T(128)} %counts_ref.1) | copy-start | bytes 580
  22.1 4.0 %collective-permute-start.3 = (bf16[128,2048]{1,0:T(8,128)(2,1)S(1)}, bf16[128,2048]{1,0:T(8,128)(2,1)S(1)}, u32[]{:S(2)}, u32[]{:S(2)}) collective-permute-start(bf16[128,2048]{1,0:T(8,128)(2,1)S(1)} %bitcast.9), channel_id=1, source_target_pairs={{0,16},{16,0},{32,48},{48,32},{64,80},{80,64},{96,112},{112,96},{1... | collective-permute-start | bytes 1572872 | tf_op jit(solution)/shard_map/ppermute | solution.py:463
